TPU v7x, 32 devices: a whole 2x2x4 slice. The times are simulated.
32 devices in a mesh: dp: 4 (over y, x), tensor: 8 (over z, core).
Axes of the slice: x: 2, y: 2, z: 4, core: 2. Of those that a mesh axis runs over, the one named last changes fastest.
Arguments:
- tokens: bfloat16 [2048, 8192], P('dp', 'tensor'), may hold values from -6 to 6
- cotangent: bfloat16 [2048, 8192], P('dp', 'tensor'), may hold values from -6 to 6
- w_first: bfloat16 [32, 256, 1024], P('tensor'), may hold values from -0.375 to 0.375
- w_second: bfloat16 [128, 256, 256], P('tensor'), may hold values from -0.375 to 0.375
- third_weight_blocks: bfloat16 [128, 256, 256], P('tensor'), may hold values from -0.375 to 0.375
- w_fourth: bfloat16 [32, 1024, 256], P('tensor'), may hold values from -0.1875 to 0.1875
Outputs:
- layer_out: bfloat16 [2048, 8192], P('dp', 'tensor')
- tokens_grad: bfloat16 [2048, 8192], P('dp', 'tensor')
- grad_first: float32 [32, 256, 1024], P('tensor')
- grad_second: float32 [128, 256, 256], P('tensor')
- grad_third: float32 [128, 256, 256], P('tensor')
- grad_fourth: float32 [32, 1024, 256], P('tensor')
All inputs are finite; a program needn't handle non-finite values.
Results may differ from a plain program's by a relative error of at most 0.0095.
Values may be sent and summed in bfloat16 or wider, within the bound.
No kernel may reach another device: no remote copies, remote signals or barrier semaphores. Data moves between devices by JAX's collectives and lax.ppermute only.
A program may use at most 128 MiB of HBM per device.

v0:
```python
import math

import jax
import jax.numpy as jnp
from jax import lax
from jax.sharding import PartitionSpec as P


def gelu_parts(value_in):
    cdf_part = 0.5 * (1.0 + lax.erf(value_in * 0.7071067811865476))
    slope_part = cdf_part + value_in * jnp.exp(-0.5 * value_in * value_in) * 0.3989422804014327
    return (value_in * cdf_part, slope_part)


def body(tokens, cotangent, w_first, w_second, third_weight_blocks, w_fourth):
    row_count = tokens.shape[0]
    width_dev = w_first.shape[0]
    block_width = w_first.shape[1]
    hidden_dev = w_second.shape[0]
    groups = lax.axis_size("tensor")
    in_blocks = width_dev * groups
    hid_blocks = hidden_dev * groups
    sub_width = block_width // in_blocks
    grad_scale = 1.0 / math.sqrt(row_count * lax.axis_size("dp"))
    inputs_view = tokens.reshape(row_count, width_dev, block_width)
    cot_view = cotangent.reshape(row_count, width_dev, block_width)
    first_factor_parts = w_first.reshape(width_dev, block_width, groups, hidden_dev, sub_width)
    first_view = w_first.reshape(width_dev, block_width, hid_blocks, sub_width)
    second_view = w_second.reshape(hidden_dev, in_blocks, sub_width, block_width)
    second_split = w_second.reshape(hidden_dev, groups, width_dev, sub_width, block_width)
    third_split = third_weight_blocks.reshape(hidden_dev, block_width, groups, width_dev, sub_width)
    fourth_view = w_fourth.reshape(width_dev, hid_blocks, sub_width, block_width)
    fourth_split = w_fourth.reshape(width_dev, groups, hidden_dev, sub_width, block_width)
    first_out = jnp.einsum(
        "tai,aigbc->gabct", inputs_view, first_factor_parts, preferred_element_type=jnp.float32
    )
    first_out = first_out.astype(jnp.bfloat16)
    received = lax.all_to_all(first_out, "tensor", split_axis=0, concat_axis=0, tiled=True)
    count = received.shape[4]
    flat_rows = received.reshape(in_blocks * hidden_dev, sub_width, count)
    spread = flat_rows
    count = flat_rows.shape[2]
    spread_view = flat_rows.reshape(in_blocks, hidden_dev, sub_width, count)
    pre_act = jnp.einsum(
        "abct,bacj->bjt", spread_view, second_view, preferred_element_type=jnp.float32
    )
    gelu_val, gelu_slope = gelu_parts(pre_act)
    activated = gelu_val.astype(jnp.bfloat16)
    third_factor_output = jnp.einsum(
        "bjt,bjgac->gbact", activated, third_split, preferred_element_type=jnp.float32
    )
    third_factor_output = third_factor_output.astype(jnp.bfloat16)
    received = lax.all_to_all(
        third_factor_output, "tensor", split_axis=0, concat_axis=0, tiled=True
    )
    count = received.shape[4]
    flat_rows = received.reshape(hid_blocks * width_dev, sub_width, count)
    merged = received.reshape(hid_blocks, width_dev, sub_width, count)
    out_part = jnp.einsum("bact,abck->akt", merged, fourth_view, preferred_element_type=jnp.float32)
    out_rows = out_part.astype(jnp.bfloat16)
    layer_out = jnp.transpose(out_rows, (2, 0, 1)).reshape(row_count, width_dev * block_width)
    third_grad = jnp.einsum(
        "tak,agbck->gbact", cot_view, fourth_split, preferred_element_type=jnp.float32
    )
    third_grad = third_grad.astype(jnp.bfloat16)
    collected_view = flat_rows.reshape(hid_blocks, width_dev, sub_width, row_count)
    grad_fourth = jnp.einsum(
        "bact,tak->abck", collected_view, cot_view, preferred_element_type=jnp.float32
    )
    grad_fourth = (grad_fourth * grad_scale).reshape(width_dev, hid_blocks * sub_width, block_width)
    returned = lax.all_to_all(third_grad, "tensor", split_axis=0, concat_axis=0, tiled=True)
    activation_gradient = jnp.einsum(
        "gbact,bjgac->bjt", returned, third_split, preferred_element_type=jnp.float32
    )
    pre_grad = (activation_gradient * gelu_slope).astype(jnp.bfloat16)
    grad_third = jnp.einsum(
        "bjt,gbact->bjgac", activated, returned, preferred_element_type=jnp.float32
    )
    grad_third = (grad_third * grad_scale).reshape(hidden_dev, block_width, block_width)
    first_grad = jnp.einsum(
        "bjt,bgacj->gbact", pre_grad, second_split, preferred_element_type=jnp.float32
    )
    first_grad = first_grad.astype(jnp.bfloat16)
    spread_view = spread.reshape(in_blocks, hidden_dev, sub_width, row_count)
    grad_second = jnp.einsum(
        "abct,bjt->bacj", spread_view, pre_grad, preferred_element_type=jnp.float32
    )
    grad_second = (grad_second * grad_scale).reshape(hidden_dev, block_width, block_width)
    back_first = lax.all_to_all(first_grad, "tensor", split_axis=0, concat_axis=0, tiled=True)
    back_view = back_first.reshape(hid_blocks, width_dev, sub_width, row_count)
    tokens_grad = jnp.einsum(
        "bact,aibc->tai", back_view, first_view, preferred_element_type=jnp.float32
    )
    tokens_grad = tokens_grad.astype(jnp.bfloat16).reshape(row_count, width_dev * block_width)
    grad_first = jnp.einsum(
        "tai,bact->aibc", inputs_view, back_view, preferred_element_type=jnp.float32
    )
    grad_first = (grad_first * grad_scale).reshape(width_dev, block_width, hid_blocks * sub_width)
    grad_first, grad_second, grad_third, grad_fourth = (
        lax.psum(grad_first.astype(jnp.bfloat16), "dp").astype(jnp.float32),
        lax.psum(grad_second.astype(jnp.bfloat16), "dp").astype(jnp.float32),
        lax.psum(grad_third.astype(jnp.bfloat16), "dp").astype(jnp.float32),
        lax.psum(grad_fourth.astype(jnp.bfloat16), "dp").astype(jnp.float32),
    )
    return (layer_out, tokens_grad, grad_first, grad_second, grad_third, grad_fourth)


def solution(mesh):
    return jax.shard_map(
        body,
        mesh=mesh,
        in_specs=(
            P("dp", "tensor"),
            P("dp", "tensor"),
            P("tensor", None, None),
            P("tensor", None, None),
            P("tensor", None, None),
            P("tensor", None, None),
        ),
        out_specs=(
            P("dp", "tensor"),
            P("dp", "tensor"),
            P("tensor", None, None),
            P("tensor", None, None),
            P("tensor", None, None),
            P("tensor", None, None),
        ),
        check_vma=False,
    )
```

profile of v0, /device:TPU:16, one launch (start us, length us, event | category | flops | bytes accessed | tf_op | source)
XLA Modules:
  0.0 626.6 jit_solution(12406556423778622042)
XLA Ops:
  9.2 4.0 copy.64
  13.2 2.9 convert_bitcast_fusion.3
  18.5 5.2 all-to-all-start
  23.7 2.6 reshape.67
  26.4 3.1 convert_bitcast_fusion.1
  32.0 82.5 %all-to-all-done = bf16[8,4,16,8,512]{4,3,2,1,0:T(8,128)(2,1)} async-done(((bf16[8,4,16,8,512]{4,3,2,1,0:T(8,128)(2,1)}), bf16[8,4,16,8,512]{4,3,2,1,0:T(8,128)(2,1)}, u32[]{:S(2)}, u32[]{:S(2)}) %all-to-all-start) | async-done | bytes 4194336 | tf_op jit(solution)/shard_map/all_to_all | solution.py:38
  114.5 7.9 %all-to-all-start.2 = ((bf16[8,16,4,8,512]{4,3,1,2,0:T(8,128)(2,1)}), bf16[8,16,4,8,512]{4,3,1,2,0:T(8,128)(2,1)}, u32[]{:S(2)}, u32[]{:S(2)}) async-start(bf16[8,16,4,8,512]{4,3,1,2,0:T(8,128)(2,1)} %copy.73), calls=%async_computation.2 | async-start | bytes 8388608 | tf_op jit(solution)/shard_map/all_to_all | solution.py:71
  122.4 3.9 copy.68
  126.3 7.4 %fusion.9 = (bf16[16,256,512]{1,2,0:T(8,128)(2,1)}, f32[16,512,256,1]{2,1,0,3:T(8,128)}) fusion(bf16[32,16,8,512]{3,2,1,0:T(8,128)(2,1)} %bitcast.3, bf16[16,256,256]{2,1,0:T(8,128)(2,1)S(1)} %copy-done), kind=kOutput, calls=%fused_computation.12 | convolution fusion | flops 1084227584 | bytes 18874368 | tf_op jit(solution)/shard_map/abct,bacj->bjt/dot_general | solution.py:44
  133.6 79.4 %all-to-all-done.2 = bf16[8,16,4,8,512]{4,3,1,2,0:T(8,128)(2,1)} async-done(((bf16[8,16,4,8,512]{4,3,1,2,0:T(8,128)(2,1)}), bf16[8,16,4,8,512]{4,3,1,2,0:T(8,128)(2,1)}, u32[]{:S(2)}, u32[]{:S(2)}) %all-to-all-start.2) | async-done | bytes 4194336 | tf_op jit(solution)/shard_map/all_to_all | solution.py:71
  213.1 7.9 %fusion.5 = bf16[16,256,512]{1,2,0:T(8,128)(2,1)S(1)} fusion(f32[16,512,256,1]{2,1,0,3:T(8,128)} %get-tuple-element.29, bf16[8,16,4,8,512]{4,3,1,2,0:T(8,128)(2,1)} %all-to-all-done.2, bf16[16,256,8,4,8]{1,4,3,2,0:T(8,128)(2,1)} %bitcast.118), kind=kOutput, calls=%fused_computation.6 | convolution fusion | flops 1094713344 | bytes 18874368 | tf_op jit(solution)/shard_map/gbact,bjgac->bjt/dot_general | solution.py:72
  225.5 8.0 %all-to-all-start.3 = ((bf16[8,16,4,8,512]{4,3,2,1,0:T(8,128)(2,1)}), bf16[8,16,4,8,512]{4,3,2,1,0:T(8,128)(2,1)}, u32[]{:S(2)}, u32[]{:S(2)}) async-start(bf16[8,16,4,8,512]{4,3,2,1,0:T(8,128)(2,1)} %copy.77), calls=%async_computation.3 | async-start | bytes 8388608 | tf_op jit(solution)/shard_map/all_to_all | solution.py:89
  233.5 3.5 fusion.57
  239.9 84.2 %all-to-all-done.3 = bf16[8,16,4,8,512]{4,3,2,1,0:T(8,128)(2,1)} async-done(((bf16[8,16,4,8,512]{4,3,2,1,0:T(8,128)(2,1)}), bf16[8,16,4,8,512]{4,3,2,1,0:T(8,128)(2,1)}, u32[]{:S(2)}, u32[]{:S(2)}) %all-to-all-start.3) | async-done | bytes 4194336 | tf_op jit(solution)/shard_map/all_to_all | solution.py:89
  324.2 7.8 %all-to-all-start.1 = ((bf16[8,16,4,8,512]{4,3,2,1,0:T(8,128)(2,1)}), bf16[8,16,4,8,512]{4,3,2,1,0:T(8,128)(2,1)}, u32[]{:S(2)}, u32[]{:S(2)}) async-start(bf16[8,16,4,8,512]{4,3,2,1,0:T(8,128)(2,1)} %copy.70), calls=%async_computation.1 | async-start | bytes 8388608 | tf_op jit(solution)/shard_map/all_to_all | solution.py:53
  332.0 4.7 multiply_convert_fusion.1
  339.2 6.0 fusion.33
  345.2 7.0 %fusion.32 = bf16[4,256,128,8]{1,2,3,0:T(8,128)(2,1)S(1)} fusion(bf16[128,4,8,512]{3,2,1,0:T(8,128)(2,1)} %bitcast.26, bf16[512,4,256,1]{2,1,0,3:T(4,128)(2,1)S(1)} %bitcast.114), kind=kOutput, calls=%fused_computation.35 | convolution fusion | flops 1075838976 | bytes 7340032 | tf_op jit(solution)/shard_map/tai,bact->aibc/dot_general | solution.py:95
  354.7 68.0 %all-to-all-done.1 = bf16[8,16,4,8,512]{4,3,2,1,0:T(8,128)(2,1)} async-done(((bf16[8,16,4,8,512]{4,3,2,1,0:T(8,128)(2,1)}), bf16[8,16,4,8,512]{4,3,2,1,0:T(8,128)(2,1)}, u32[]{:S(2)}, u32[]{:S(2)}) %all-to-all-start.1) | async-done | bytes 4194336 | tf_op jit(solution)/shard_map/all_to_all | solution.py:53
  422.7 7.2 %multiply_convert_fusion = bf16[4,128,8,256]{3,1,2,0:T(8,128)(2,1)S(1)} fusion(bf16[128,4,8,512]{3,2,1,0:T(8,128)(2,1)} %bitcast.12, bf16[512,4,256,1]{2,1,0,3:T(4,128)(2,1)S(1)} %bitcast.116), kind=kOutput, calls=%fused_computation.27 | convolution fusion | flops 1075838976 | bytes 7340032 | tf_op jit(solution)/shard_map/bact,tak->abck/dot_general | solution.py:67
  434.0 3.5 bitcast_convert_fusion
  438.8 5.1 bitcast_convert_fusion.1
  445.3 162.8 %all-reduce.3.cloned.1.call-done = (bf16[4,256,1024]{1,2,0:T(8,128)(2,1)}, bf16[16,256,256]{2,1,0:T(8,128)(2,1)}, bf16[16,256,256]{2,1,0:T(8,128)(2,1)}, bf16[4,1024,256]{2,1,0:T(8,128)(2,1)}) async-done(((bf16[4,256,1024]{1,2,0:T(8,128)(2,1)}, bf16[16,256,256]{2,1,0:T(8,128)(2,1)}, bf16[16,256,256]{2,1,0:T(8,128)(2,1)}, bf16[4,1024,256]{2,1,0:T(8,128)(2,1)}), (bf16[4,256,1024]{1,2,0:T(8,128)(2,1)}, ...) | async-done | bytes 8388624 | tf_op jit(solution)/shard_map/psum | solution.py:100
  608.1 4.3 copy.93
  (35 shorter events, 33.7 us)
Async XLA Ops:
  7.2 119.1 %copy-start = (bf16[16,256,256]{2,1,0:T(8,128)(2,1)S(1)}, bf16[16,256,256]{2,1,0:T(8,128)(2,1)}, u32[]{:S(2)}) copy-start(bf16[16,256,256]{2,1,0:T(8,128)(2,1)} %param.9) | copy-start | bytes 6291460
  18.5 95.9 %all-to-all-start = ((bf16[8,4,16,8,512]{4,3,2,1,0:T(8,128)(2,1)}), bf16[8,4,16,8,512]{4,3,2,1,0:T(8,128)(2,1)}, u32[]{:S(2)}, u32[]{:S(2)}) async-start(bf16[8,4,16,8,512]{4,3,2,1,0:T(8,128)(2,1)} %copy.66), calls=%async_computation | async-start | bytes 8388608 | tf_op jit(solution)/shard_map/all_to_all | solution.py:38
  114.5 98.6 %all-to-all-start.2 = ((bf16[8,16,4,8,512]{4,3,1,2,0:T(8,128)(2,1)}), bf16[8,16,4,8,512]{4,3,1,2,0:T(8,128)(2,1)}, u32[]{:S(2)}, u32[]{:S(2)}) async-start(bf16[8,16,4,8,512]{4,3,1,2,0:T(8,128)(2,1)} %copy.73), calls=%async_computation.2 | async-start | bytes 8388608 | tf_op jit(solution)/shard_map/all_to_all | solution.py:71
  221.0 2.0 copy-start.5
  225.5 8.0 %copy-start.2 = (bf16[16,256,256]{2,1,0:T(8,128)(2,1)S(1)}, bf16[16,256,256]{2,1,0:T(8,128)(2,1)}, u32[]{:S(2)}) copy-start(bf16[16,256,256]{2,1,0:T(8,128)(2,1)} %param.10) | copy-start | bytes 6291460
  225.5 98.7 %all-to-all-start.3 = ((bf16[8,16,4,8,512]{4,3,2,1,0:T(8,128)(2,1)}), bf16[8,16,4,8,512]{4,3,2,1,0:T(8,128)(2,1)}, u32[]{:S(2)}, u32[]{:S(2)}) async-start(bf16[8,16,4,8,512]{4,3,2,1,0:T(8,128)(2,1)} %copy.77), calls=%async_computation.3 | async-start | bytes 8388608 | tf_op jit(solution)/shard_map/all_to_all | solution.py:89
  324.2 98.6 %all-to-all-start.1 = ((bf16[8,16,4,8,512]{4,3,2,1,0:T(8,128)(2,1)}), bf16[8,16,4,8,512]{4,3,2,1,0:T(8,128)(2,1)}, u32[]{:S(2)}, u32[]{:S(2)}) async-start(bf16[8,16,4,8,512]{4,3,2,1,0:T(8,128)(2,1)} %copy.70), calls=%async_computation.1 | async-start | bytes 8388608 | tf_op jit(solution)/shard_map/all_to_all | solution.py:53
  332.0 276.1 %all-reduce.3.cloned.1.call-start = ((), (), s32[]{:S(2)}) async-start(), calls=%async_computation.4 | async-start | bytes 16777216 | tf_op jit(solution)/shard_map/psum | solution.py:100
  352.2 70.5 %copy-start.4 = (bf16[512,4,256]{2,1,0:T(4,128)(2,1)S(1)}, bf16[512,4,256]{2,1,0:T(4,128)(2,1)}, u32[]{:S(2)}) copy-start(bf16[512,4,256]{2,1,0:T(4,128)(2,1)} %reshape.67) | copy-start | bytes 3145732
  432.5 1.6 copy-start.3
  608.1 4.3 copy-start.8
  612.3 2.5 copy-start.7
  614.8 2.6 copy-start.6
  614.8 5.0 copy-start.1
Sparse Core Ops, SparseCore 0:
  432.6 175.4 all-reduce.2
where the time goes:
time: 629 us; the launch traced here: 627 us
  waiting for transfers between devices  477 us (76%)
  matrix products  59.6 us (9%)
  local copies, waits for them, and re-layouts  39 us (6%)
  starting transfers between devices  28.9 us (5%)
  between operations  14.1 us (2%)
  other arithmetic  8.08 us (1%)
    psum x1, waiting for transfers between devices, body(): lax.psum(grad_first.astype(jnp.bfloat16), 'dp').astype(jnp.float32)  163 us
    all_to_all x1, waiting for transfers between devices, body(): lax.all_to_all(first_grad, 'tensor', split_axis=0, concat_axis=0, tiled=T...  84.2 us
    all_to_all x1, waiting for transfers between devices, body(): lax.all_to_all(first_out, 'tensor', split_axis=0, concat_axis=0, tiled=True)  82.5 us
    all_to_all x1, waiting for transfers between devices, body(): lax.all_to_all(third_grad, 'tensor', split_axis=0, concat_axis=0, tiled=T...  79.4 us
    all_to_all x1, waiting for transfers between devices, body(): lax.all_to_all(third_factor_output, 'tensor', split_axis=0, concat_axis=0...  68 us
    unnamed x23, local copies, waits for them, and re-layouts  17 us
  transfers between devices with their start and end apart: 5, of which 5 were waited for; matrix products, arithmetic and copies ran while one was open for 10% of the time, Pallas kernels for 0%

commit v1 on v0

v1 whole, which is shorter than its diff:
```python
import functools
import math

import jax
import jax.numpy as jnp
from jax import lax
from jax.experimental import pallas as pl
from jax.experimental.pallas import tpu as pltpu
from jax.sharding import PartitionSpec as P

F32 = jnp.float32
BF16 = jnp.bfloat16


def gelu_parts(value_in):
    cdf_part = 0.5 * (1.0 + lax.erf(value_in * 0.7071067811865476))
    slope_part = cdf_part + value_in * jnp.exp(-0.5 * value_in * value_in) * 0.3989422804014327
    return (value_in * cdf_part, slope_part)


def dot(a, b, ca, cb):
    return lax.dot_general(a, b, (((ca,), (cb,)), ((), ())), preferred_element_type=F32)


def split_rows(val, hid, sub):
    return val.reshape(hid, sub, val.shape[-1])


def expand_kernel(rel_ref, x_ref, w_ref, y_ref, *, wd, bw, hd, sub):
    outs = []
    for a in range(wd):
        val = dot(w_ref[0, a], x_ref[0, a * bw : (a + 1) * bw, :], 1, 0)
        outs.append(val.reshape(hd, sub, val.shape[-1]))
    for a in range(0, wd, 2):
        if a + 1 < wd:
            both = jnp.concatenate(outs[a : a + 2], axis=1)
            y_ref[:, a * sub : (a + 2) * sub, :] = both.astype(BF16)
        else:
            y_ref[:, a * sub : (a + 1) * sub, :] = outs[a].astype(BF16)


def expand(rel, x_rel, w_own, wd, bw, hd, sub):
    n, _, rows = x_rel.shape
    m = w_own.shape[2]
    return pl.pallas_call(
        functools.partial(expand_kernel, wd=wd, bw=bw, hd=hd, sub=sub),
        grid_spec=pltpu.PrefetchScalarGridSpec(
            num_scalar_prefetch=1,
            grid=(n,),
            in_specs=[
                pl.BlockSpec((1, wd * bw, rows), lambda d, rel: (rel[d], 0, 0)),
                pl.BlockSpec((1, wd, m, bw), lambda d, rel: (d, 0, 0, 0)),
            ],
            out_specs=pl.BlockSpec((hd, wd * sub, rows), lambda d, rel: (0, d, 0)),
        ),
        out_shape=jax.ShapeDtypeStruct((hd, n * wd * sub, rows), BF16),
        compiler_params=pltpu.CompilerParams(dimension_semantics=("arbitrary",)),
        cost_estimate=pl.CostEstimate(
            flops=2 * n * wd * m * bw * rows,
            bytes_accessed=2 * (n * wd * bw * rows + n * wd * m * bw + n * wd * m * rows),
            transcendentals=0,
        ),
        name="expand",
    )(rel, x_rel, w_own)


def middle_kernel(y_ref, dz_ref, w2_ref, w3_ref, z_ref, dy_ref, g2_ref, g3_ref, *, scale):
    yb = y_ref[0]
    dzb = dz_ref[0]
    w2 = w2_ref[0]
    w3 = w3_ref[0]
    pre = dot(w2, yb, 0, 0)
    val, slope = gelu_parts(pre)
    act = val.astype(BF16)
    z_ref[0] = dot(w3, act, 0, 0).astype(BF16)
    dact = dot(w3, dzb, 1, 0)
    dpre = (dact * slope).astype(BF16)
    dy_ref[0] = dot(w2, dpre, 1, 0).astype(BF16)
    g2_ref[0] = (dot(yb, dpre, 1, 1) * scale).astype(BF16)
    g3_ref[0] = (dot(act, dzb, 1, 1) * scale).astype(BF16)


def middle(y, dz, w2, w3, scale):
    hd, k, rows = y.shape
    j = w2.shape[2]
    row_spec = pl.BlockSpec((1, k, rows), lambda b: (b, 0, 0))
    w2_spec = pl.BlockSpec((1, k, j), lambda b: (b, 0, 0))
    w3_spec = pl.BlockSpec((1, j, k), lambda b: (b, 0, 0))
    return pl.pallas_call(
        functools.partial(middle_kernel, scale=scale),
        grid=(hd,),
        in_specs=[row_spec, row_spec, w2_spec, w3_spec],
        out_specs=[row_spec, row_spec, w2_spec, w3_spec],
        out_shape=[
            jax.ShapeDtypeStruct(y.shape, BF16),
            jax.ShapeDtypeStruct(y.shape, BF16),
            jax.ShapeDtypeStruct(w2.shape, BF16),
            jax.ShapeDtypeStruct(w3.shape, BF16),
        ],
        compiler_params=pltpu.CompilerParams(dimension_semantics=("arbitrary",)),
        cost_estimate=pl.CostEstimate(
            flops=2 * 6 * hd * k * j * rows,
            bytes_accessed=2 * (4 * hd * k * rows + 4 * hd * k * j),
            transcendentals=2 * hd * j * rows,
        ),
        name="middle",
    )(y, dz, w2, w3)


def contract_kernel(
    rel_ref, dst_ref, z_ref, dy_ref, x_ref, g_ref, w1_ref, w4_ref, out_ref, tg_ref, gr_ref,
    *, wd, bw, hd, sub, dp, scale
):
    rows = z_ref.shape[-1]
    m = hd * sub
    step = m // dp

    def parts(ref):
        vals = []
        for a in range(0, wd, 2):
            width = min(2, wd - a)
            chunk = ref[:, a * sub : (a + width) * sub, :].astype(F32)
            for k in range(width):
                piece = chunk[:, k * sub : (k + 1) * sub, :]
                vals.append(piece.reshape(m, rows).astype(BF16))
        return vals

    zs = parts(z_ref)
    dys = parts(dy_ref)
    for a in range(wd):
        span = slice(a * bw, (a + 1) * bw)
        out_ref[0, span, :] = dot(w4_ref[0, a], zs[a], 0, 0).astype(BF16)
        tg_ref[0, span, :] = dot(w1_ref[0, a], dys[a], 0, 0).astype(BF16)
        g1 = (dot(dys[a], x_ref[0, span, :], 1, 1) * scale).astype(BF16)
        g4 = (dot(zs[a], g_ref[0, span, :], 1, 1) * scale).astype(BF16)
        for q in range(dp):
            gr_ref[q, 0, 0, a] = g1[q * step : (q + 1) * step]
            gr_ref[q, 0, 1, a] = g4[q * step : (q + 1) * step]


def contract(rel, dst, z, dy, x_rel, g_rel, w1t, w4, wd, bw, hd, sub, dp, scale):
    n, _, rows = x_rel.shape
    m = hd * sub
    zspec = pl.BlockSpec((hd, wd * sub, rows), lambda s, rel, dst: (0, dst[s], 0))
    xspec = pl.BlockSpec((1, wd * bw, rows), lambda s, rel, dst: (rel[s], 0, 0))
    wspec = pl.BlockSpec((1, wd, m, bw), lambda s, rel, dst: (dst[s], 0, 0, 0))
    return pl.pallas_call(
        functools.partial(
            contract_kernel, wd=wd, bw=bw, hd=hd, sub=sub, dp=dp, scale=scale
        ),
        grid_spec=pltpu.PrefetchScalarGridSpec(
            num_scalar_prefetch=2,
            grid=(n,),
            in_specs=[zspec, zspec, xspec, xspec, wspec, wspec],
            out_specs=[
                xspec,
                xspec,
                pl.BlockSpec(
                    (dp, 1, 2, wd, m // dp, bw), lambda s, rel, dst: (0, dst[s], 0, 0, 0, 0)
                ),
            ],
        ),
        out_shape=[
            jax.ShapeDtypeStruct(x_rel.shape, BF16),
            jax.ShapeDtypeStruct(x_rel.shape, BF16),
            jax.ShapeDtypeStruct((dp, n, 2, wd, m // dp, bw), BF16),
        ],
        compiler_params=pltpu.CompilerParams(dimension_semantics=("arbitrary",)),
        cost_estimate=pl.CostEstimate(
            flops=2 * 4 * n * wd * m * bw * rows,
            bytes_accessed=2 * (4 * n * wd * bw * rows + 2 * n * wd * m * rows + 4 * n * wd * m * bw),
            transcendentals=0,
        ),
        name="contract",
    )(rel, dst, z, dy, x_rel, g_rel, w1t, w4)


def up_pairs(lo, hi):
    return [(2 * p + c, 2 * p + 2 + c) for p in range(lo, hi) for c in range(2)]


def down_pairs(lo, hi):
    return [(2 * p + 2 + c, 2 * p + c) for p in range(lo, hi) for c in range(2)]


def line_gather(own, nl):
    ups, downs = [own], [own]
    for r in range(1, nl):
        ups.append(lax.ppermute(ups[-1], "tensor", up_pairs(r - 1, nl - 1)))
        downs.append(lax.ppermute(downs[-1], "tensor", down_pairs(0, nl - r)))
    return [own] + [downs[k] + ups[nl - k] for k in range(1, nl)]


def swap(val, n):
    return lax.ppermute(val, "tensor", [(i, i ^ 1) for i in range(n)])


def line_scatter(parts, nl):
    up, down = parts[nl - 1], parts[1]
    for r in range(1, nl):
        up = lax.ppermute(up, "tensor", up_pairs(0, r))
        down = lax.ppermute(down, "tensor", down_pairs(nl - 1 - r, nl - 1))
        if r < nl - 1:
            up = up + parts[nl - 1 - r]
            down = down + parts[r + 1]
    return (parts[0].astype(F32) + up.astype(F32) + down.astype(F32)).astype(BF16)


def gather_all(own, n):
    nl = n // 2
    mine = line_gather(own, nl)
    return jnp.stack([v for p in mine for v in (p, swap(p, n))])


def scatter_all(partial, n):
    nl = n // 2
    parts = []
    for k in range(nl):
        parts.append(partial[2 * k] + swap(partial[2 * k + 1], n))
    return line_scatter(parts, nl)


def body(tokens, cotangent, w_first, w_second, w_third, w_fourth):
    rows = tokens.shape[0]
    wd, bw, _ = w_first.shape
    hd = w_second.shape[0]
    n = lax.axis_size("tensor")
    dp = lax.axis_size("dp")
    nl = n // 2
    sub = bw // (wd * n)
    m = hd * sub
    step = m // dp
    scale = 1.0 / math.sqrt(rows * dp)
    me = lax.axis_index("tensor")
    quarter = lax.axis_index("dp")
    pos, core = me // 2, me % 2

    order = jnp.arange(n, dtype=jnp.int32)
    rel_of = 2 * ((order // 2 - pos + nl) % nl) + (order % 2 + core) % 2
    dst_of = 2 * ((order // 2 + pos) % nl) + (order % 2 + core) % 2

    w14 = jnp.stack([jnp.swapaxes(w_first, 1, 2), w_fourth])
    w14 = w14.reshape(2, wd, n, dp, step, bw)
    w14 = lax.dynamic_index_in_dim(w14, quarter, axis=3, keepdims=False)
    w14 = jnp.transpose(w14, (2, 0, 1, 3, 4))
    w14 = lax.all_to_all(w14, "tensor", split_axis=0, concat_axis=0, tiled=True)
    w14 = lax.all_gather(w14, "dp")
    w14 = jnp.transpose(w14, (2, 1, 3, 0, 4, 5)).reshape(2, n, wd, m, bw)
    w1t, w4 = w14[0], w14[1]

    x_rel = gather_all(tokens.T, n)
    g_rel = gather_all(cotangent.T, n)
    y = expand(rel_of, x_rel, w1t, wd, bw, hd, sub)
    dz = expand(rel_of, g_rel, w4, wd, bw, hd, sub)
    z, dy, g2, g3 = middle(y, dz, w_second, w_third, scale)
    out_part, tg_part, g14 = contract(
        order, dst_of, z, dy, x_rel, g_rel, w1t, w4, wd, bw, hd, sub, dp, scale
    )

    layer_out = scatter_all(out_part, n).T
    tokens_grad = scatter_all(tg_part, n).T

    g2, g3 = lax.psum((g2, g3), "dp")
    g14 = lax.psum_scatter(g14, "dp")
    g14 = lax.all_to_all(g14, "tensor", split_axis=0, concat_axis=0, tiled=True)
    g14 = lax.all_gather(g14, "dp")
    g1 = jnp.transpose(g14[:, :, 0], (2, 4, 1, 0, 3)).reshape(wd, bw, n * m).astype(F32)
    g4 = jnp.transpose(g14[:, :, 1], (2, 1, 0, 3, 4)).reshape(wd, n * m, bw).astype(F32)
    return (layer_out, tokens_grad, g1, g2.astype(F32), g3.astype(F32), g4)


def solution(mesh):
    return jax.shard_map(
        body,
        mesh=mesh,
        in_specs=(
            P("dp", "tensor"),
            P("dp", "tensor"),
            P("tensor", None, None),
            P("tensor", None, None),
            P("tensor", None, None),
            P("tensor", None, None),
        ),
        out_specs=(
            P("dp", "tensor"),
            P("dp", "tensor"),
            P("tensor", None, None),
            P("tensor", None, None),
            P("tensor", None, None),
            P("tensor", None, None),
        ),
        check_vma=False,
    )
```

time: 629 us -> 589 us (0.936)
  waiting for transfers between devices: 477 us -> 340 us
  matrix products: 59.6 us -> 0 us
  Pallas kernels: 0 us -> 59.3 us
  starting transfers between devices: 28.9 us -> 75.6 us
  other arithmetic: 8.08 us -> 48.1 us
  local copies, waits for them, and re-layouts: 39 us -> 49 us
    all_to_all x4 -> x2, waiting for transfers between devices: 314 us -> 12.6 us  [the longest x1 12.6 us: body(): g14 = lax.all_to_all(g14, 'tensor', split_axis=0, concat_axis=0, tiled=True)]
    ppermute x0 -> x40, waiting for transfers between devices: none -> 255 us  [the longest x6 111 us: line_gather(): ups.append(lax.ppermute(ups[-1], 'tensor', up_pairs(r - 1, nl - 1)))]
    psum x1, waiting for transfers between devices: 163 us -> 0.02 us  [body(): g2, g3 = lax.psum((g2, g3), 'dp')]
    unnamed x1 -> x5, waiting for transfers between devices: 0.02 us -> 72.9 us
    ppermute x0 -> x40, starting transfers between devices: none -> 65.6 us  [the longest x6 25.7 us: line_scatter(): down = lax.ppermute(down, 'tensor', down_pairs(nl - 1 - r, nl - 1))]
    pallas_call x0 -> x4, Pallas kernels: none -> 59.3 us  [the longest x1 21.3 us: contract(): pl.pallas_call(functools.partial(contract_kernel, wd=wd, bw=bw, hd=hd, su...]
    dot_general x11 -> x0, matrix products: 56.1 us -> none  [the longest x1 7.85 us: body(): jnp.einsum('gbact,bjgac->bjt', returned, third_split, preferred_element_t...]
    all_to_all x4 -> x2, starting transfers between devices: 28.9 us -> 9.89 us  [the longest x1 5.1 us: body(): g14 = lax.all_to_all(g14, 'tensor', split_axis=0, concat_axis=0, tiled=True)]
  transfers between devices with their start and end apart: 5 -> 46, of which waited for: 5 -> 18; matrix products, arithmetic and copies ran while one was open for 10% -> 13% of each run, Pallas kernels for 0% -> 0%
where the time goes in v1:
time: 589 us; the launch traced here: 587 us
  waiting for transfers between devices  340 us (58%)
  starting transfers between devices  75.6 us (13%)
  Pallas kernels  59.3 us (10%)
  local copies, waits for them, and re-layouts  49 us (8%)
  other arithmetic  48.1 us (8%)
  between operations  14.2 us (2%)
    ppermute x6, waiting for transfers between devices, line_gather(): ups.append(lax.ppermute(ups[-1], 'tensor', up_pairs(r - 1, nl - 1)))  111 us
    unnamed x5, waiting for transfers between devices  72.9 us
    ppermute x6, waiting for transfers between devices, line_scatter(): down = lax.ppermute(down, 'tensor', down_pairs(nl - 1 - r, nl - 1))  69.9 us
    ppermute x6, waiting for transfers between devices, line_scatter(): up = lax.ppermute(up, 'tensor', up_pairs(0, r))  55.8 us
    unnamed x24, local copies, waits for them, and re-layouts  26.7 us
    ppermute x6, starting transfers between devices, line_scatter(): down = lax.ppermute(down, 'tensor', down_pairs(nl - 1 - r, nl - 1))  25.7 us
    pallas_call x1, Pallas kernels, contract(): pl.pallas_call(functools.partial(contract_kernel, wd=wd, bw=bw, hd=hd, su...  21.3 us
    pallas_call x1, Pallas kernels, middle(): pl.pallas_call(functools.partial(middle_kernel, scale=scale), grid=(hd,),...  19 us
  transfers between devices with their start and end apart: 46, of which 18 were waited for; matrix products, arithmetic and copies ran while one was open for 13% of the time, Pallas kernels for 0%

profile of v1, /device:TPU:16, one launch (start us, length us, event | category | flops | bytes accessed | tf_op | source)
XLA Modules:
  0.0 586.6 jit_solution(11489365975478344722)
XLA Ops:
  17.3 4.8 all-to-all-start
  26.9 14.0 %collective-permute-done.12 = bf16[1024,512]{1,0:T(8,128)(2,1)} collective-permute-done((bf16[1024,512]{1,0:T(8,128)(2,1)S(1)}, bf16[1024,512]{1,0:T(8,128)(2,1)}, u32[]{:S(2)}, u32[]{:S(2)}) %collective-permute-start.12) | collective-permute-done | bytes 1048608 | tf_op jit(solution)/shard_map/ppermute | solution.py:189
  47.9 33.9 %collective-permute-done.2 = bf16[1024,512]{1,0:T(8,128)(2,1)} collective-permute-done((bf16[1024,512]{1,0:T(8,128)(2,1)S(1)}, bf16[1024,512]{1,0:T(8,128)(2,1)}, u32[]{:S(2)}, u32[]{:S(2)}) %collective-permute-start.2) | collective-permute-done | bytes 1048608 | tf_op jit(solution)/shard_map/ppermute | solution.py:189
  83.7 20.5 %collective-permute-done.13 = bf16[1024,512]{1,0:T(8,128)(2,1)} collective-permute-done((bf16[1024,512]{1,0:T(8,128)(2,1)}, bf16[1024,512]{1,0:T(8,128)(2,1)}, u32[]{:S(2)}, u32[]{:S(2)}) %collective-permute-start.13) | collective-permute-done | bytes 1048608 | tf_op jit(solution)/shard_map/ppermute | solution.py:189
  110.5 15.0 %collective-permute-done.3 = bf16[1024,512]{1,0:T(8,128)(2,1)} collective-permute-done((bf16[1024,512]{1,0:T(8,128)(2,1)}, bf16[1024,512]{1,0:T(8,128)(2,1)}, u32[]{:S(2)}, u32[]{:S(2)}) %collective-permute-start.3) | collective-permute-done | bytes 1048608 | tf_op jit(solution)/shard_map/ppermute | solution.py:189
  131.6 10.9 %collective-permute-done.14 = bf16[1024,512]{1,0:T(8,128)(2,1)} collective-permute-done((bf16[1024,512]{1,0:T(8,128)(2,1)}, bf16[1024,512]{1,0:T(8,128)(2,1)}, u32[]{:S(2)}, u32[]{:S(2)}) %collective-permute-start.14) | collective-permute-done | bytes 1048608 | tf_op jit(solution)/shard_map/ppermute | solution.py:189
  147.7 16.2 %collective-permute-done.4 = bf16[1024,512]{1,0:T(8,128)(2,1)S(1)} collective-permute-done((bf16[1024,512]{1,0:T(8,128)(2,1)}, bf16[1024,512]{1,0:T(8,128)(2,1)S(1)}, u32[]{:S(2)}, u32[]{:S(2)}) %collective-permute-start.4) | collective-permute-done | bytes 1048608 | tf_op jit(solution)/shard_map/ppermute | solution.py:189
  172.4 17.4 %collective-permute-done.6 = bf16[1024,512]{1,0:T(8,128)(2,1)S(1)} collective-permute-done((bf16[1024,512]{1,0:T(8,128)(2,1)S(1)}, bf16[1024,512]{1,0:T(8,128)(2,1)S(1)}, u32[]{:S(2)}, u32[]{:S(2)}) %collective-permute-start.6) | collective-permute-done | bytes 1048608 | tf_op jit(solution)/shard_map/ppermute | solution.py:190
  210.9 9.5 %expand.3.dz_ref = bf16[16,256,512]{2,1,0:T(8,128)(2,1)} custom-call(s32[8]{0:T(128)} %get-tuple-element.93.rel_ref, bf16[8,1024,512]{2,1,0:T(8,128)(2,1)} %bitcast_dynamic-update-slice_fusion.2.x_ref.g_ref, bf16[8,4,128,256]{3,2,1,0:T(8,128)(2,1)} %bitcast.118), custom_call_target="tpu_custom_call" | custom-call | flops 1073741824 | bytes 14680064 | tf_op jit(solution)/shard_map/expand/pallas_call | solution.py:45
  220.4 9.5 %expand.2.y_ref = bf16[16,256,512]{2,1,0:T(8,128)(2,1)} custom-call(s32[8]{0:T(128)} %get-tuple-element.93.rel_ref, bf16[8,1024,512]{2,1,0:T(8,128)(2,1)} %bitcast_dynamic-update-slice_fusion.9.x_ref, bf16[8,4,128,256]{3,2,1,0:T(8,128)(2,1)} %bitcast.120), custom_call_target="tpu_custom_call" | custom-call | flops 1073741824 | bytes 14680064 | tf_op jit(solution)/shard_map/expand/pallas_call | solution.py:45
  229.9 19.0 %middle.1 = (bf16[16,256,512]{2,1,0:T(8,128)(2,1)}, bf16[16,256,512]{2,1,0:T(8,128)(2,1)}, bf16[16,256,256]{2,1,0:T(8,128)(2,1)}, bf16[16,256,256]{2,1,0:T(8,128)(2,1)}) custom-call(bf16[16,256,512]{2,1,0:T(8,128)(2,1)} %expand.2.y_ref, bf16[16,256,512]{2,1,0:T(8,128)(2,1)} %expand.3.dz_ref, bf16[16,256,256]{2,1,0:T(8,128)(2,1)} %w2_ref.1, ...), custom_call_target="tpu_custom_call" | custom-call | flops 6442450944 | bytes 25165824 | tf_op jit(solution)/shard_map/middle/pallas_call | solution.py:89
  249.4 21.3 %contract.1 = (bf16[8,1024,512]{2,1,0:T(8,128)(2,1)}, bf16[8,1024,512]{2,1,0:T(8,128)(2,1)}, bf16[4,8,2,4,32,256]{5,4,3,2,1,0:T(8,128)(2,1)}) custom-call(s32[8]{0:T(128)} %iota.9.rel_ref, s32[8]{0:T(128)} %get-tuple-element.92.dst_ref, bf16[16,256,512]{2,1,0:T(8,128)(2,1)} %get-tuple-element.13.z_ref, bf16[16,256,512]{2,1,0:T(8,128)(2,1)} %get-tuple-element.14.dy_ref, ...), custom_call_target="tpu_custom_call" | custom-call | flops 4294967296 | bytes 50331648 | tf_op jit(solution)/shard_map/contract/pallas_call | solution.py:147
  275.5 72.1 %reduce-scatter.4.cloned.1.call-done = bf16[1,8,2,4,32,256]{5,4,3,2,1,0:T(8,128)(2,1)} async-done(((bf16[4,8,2,4,32,256]{5,4,3,2,1,0:T(8,128)(2,1)}), bf16[1,8,2,4,32,256]{5,4,3,2,1,0:T(8,128)(2,1)}) %reduce-scatter.4.cloned.1.call-update) | async-done | bytes 1048592
  347.7 5.1 all-to-all-start.1
  363.5 12.6 %all-to-all-done.1 = bf16[8,2,4,32,256]{4,3,2,1,0:T(8,128)(2,1)S(1)} async-done(((bf16[8,2,4,32,256]{4,3,2,1,0:T(8,128)(2,1)}), bf16[8,2,4,32,256]{4,3,2,1,0:T(8,128)(2,1)S(1)}, u32[]{:S(2)}, u32[]{:S(2)}) %all-to-all-start.1) | async-done | bytes 1048608 | tf_op jit(solution)/shard_map/all_to_all | solution.py:265
  384.6 37.1 %collective-permute-done.24 = bf16[1024,512]{1,0:T(8,128)(2,1)S(1)} collective-permute-done((bf16[1024,512]{1,0:T(8,128)(2,1)S(1)}, bf16[1024,512]{1,0:T(8,128)(2,1)S(1)}, u32[]{:S(2)}, u32[]{:S(2)}) %collective-permute-start.24) | collective-permute-done | bytes 1048608 | tf_op jit(solution)/shard_map/ppermute | solution.py:201
  425.3 18.7 %collective-permute-done.34 = bf16[1024,512]{1,0:T(8,128)(2,1)S(1)} collective-permute-done((bf16[1024,512]{1,0:T(8,128)(2,1)S(1)}, bf16[1024,512]{1,0:T(8,128)(2,1)S(1)}, u32[]{:S(2)}, u32[]{:S(2)}) %collective-permute-start.34) | collective-permute-done | bytes 1048608 | tf_op jit(solution)/shard_map/ppermute | solution.py:201
  452.6 15.2 %collective-permute-start.28 = (bf16[1024,512]{1,0:T(8,128)(2,1)S(1)}, bf16[1024,512]{1,0:T(8,128)(2,1)S(1)}, u32[]{:S(2)}, u32[]{:S(2)}) collective-permute-start(bf16[1024,512]{1,0:T(8,128)(2,1)S(1)} %fusion.4), channel_id=1, source_target_pairs={{4,2},{5,3},{6,4},{7,5},{12,10},{13,11},{14,12},{15,13},{20,18},{2... | collective-permute-start | bytes 3145736 | tf_op jit(solution)/shard_map/ppermute | solution.py:202
  467.9 5.8 collective-permute-done.37
  481.4 14.7 %collective-permute-done.28 = bf16[1024,512]{1,0:T(8,128)(2,1)S(1)} collective-permute-done((bf16[1024,512]{1,0:T(8,128)(2,1)S(1)}, bf16[1024,512]{1,0:T(8,128)(2,1)S(1)}, u32[]{:S(2)}, u32[]{:S(2)}) %collective-permute-start.28) | collective-permute-done | bytes 1048608 | tf_op jit(solution)/shard_map/ppermute | solution.py:202
  499.4 19.2 %collective-permute-done.38 = bf16[1024,512]{1,0:T(8,128)(2,1)S(1)} collective-permute-done((bf16[1024,512]{1,0:T(8,128)(2,1)S(1)}, bf16[1024,512]{1,0:T(8,128)(2,1)S(1)}, u32[]{:S(2)}, u32[]{:S(2)}) %collective-permute-start.38) | collective-permute-done | bytes 1048608 | tf_op jit(solution)/shard_map/ppermute | solution.py:202
  532.4 8.7 %collective-permute-done.29 = bf16[1024,512]{1,0:T(8,128)(2,1)} collective-permute-done((bf16[1024,512]{1,0:T(8,128)(2,1)}, bf16[1024,512]{1,0:T(8,128)(2,1)}, u32[]{:S(2)}, u32[]{:S(2)}) %collective-permute-start.29) | collective-permute-done | bytes 1048608 | tf_op jit(solution)/shard_map/ppermute | solution.py:202
  545.2 17.5 %collective-permute-done.39 = bf16[1024,512]{1,0:T(8,128)(2,1)} collective-permute-done((bf16[1024,512]{1,0:T(8,128)(2,1)}, bf16[1024,512]{1,0:T(8,128)(2,1)}, u32[]{:S(2)}, u32[]{:S(2)}) %collective-permute-start.39) | collective-permute-done | bytes 1048608 | tf_op jit(solution)/shard_map/ppermute | solution.py:202
  574.7 5.3 copy.80
  (134 shorter events, 148.2 us)
Async XLA Ops:
  17.3 89.2 %all-to-all-start = ((bf16[8,2,4,32,256]{4,3,2,1,0:T(8,128)(2,1)}), bf16[8,2,4,32,256]{4,3,2,1,0:T(8,128)(2,1)S(1)}, u32[]{:S(2)}, u32[]{:S(2)}) async-start(bf16[8,2,4,32,256]{4,3,2,1,0:T(8,128)(2,1)} %copy.72), calls=%async_computation | async-start | bytes 2097152 | tf_op jit(solution)/shard_map/all_to_all | solution.py:246
  22.1 183.1 %all-gather.5.cloned.1.call-start = ((), (), s32[]{:S(2)}) async-start(), calls=%async_computation.3 | async-start | bytes 5242880 | tf_op jit(solution)/shard_map/all_gather | solution.py:247
  23.6 58.2 %collective-permute-start.2 = (bf16[1024,512]{1,0:T(8,128)(2,1)S(1)}, bf16[1024,512]{1,0:T(8,128)(2,1)}, u32[]{:S(2)}, u32[]{:S(2)}) collective-permute-start(bf16[1024,512]{1,0:T(8,128)(2,1)S(1)} %bitcast.130), channel_id=1, source_target_pairs={{0,2},{1,3},{2,4},{3,5},{4,6},{5,7},{8,10},{9,11},{10,12},{11,13},... | collective-permute-start | bytes 3145736 | tf_op jit(solution)/shard_map/ppermute | solution.py:189
  41.0 63.2 %collective-permute-start.13 = (bf16[1024,512]{1,0:T(8,128)(2,1)}, bf16[1024,512]{1,0:T(8,128)(2,1)}, u32[]{:S(2)}, u32[]{:S(2)}) collective-permute-start(bf16[1024,512]{1,0:T(8,128)(2,1)} %collective-permute-done.12), channel_id=1, source_target_pairs={{2,4},{3,5},{4,6},{5,7},{10,12},{11,13},{12,14},{13,15},{18,20},{1... | collective-permute-start | bytes 3145736 | tf_op jit(solution)/shard_map/ppermute | solution.py:189
  44.0 64.6 %collective-permute-start.11 = (bf16[1024,512]{1,0:T(8,128)(2,1)S(1)}, bf16[1024,512]{1,0:T(8,128)(2,1)}, u32[]{:S(2)}, u32[]{:S(2)}) collective-permute-start(bf16[1024,512]{1,0:T(8,128)(2,1)S(1)} %bitcast.128), channel_id=1, source_target_pairs={{2,0},{3,1},{4,2},{5,3},{6,4},{7,5},{10,8},{11,9},{12,10},{13,11},... | collective-permute-start | bytes 3145736 | tf_op jit(solution)/shard_map/ppermute | solution.py:190
  81.7 43.8 %collective-permute-start.3 = (bf16[1024,512]{1,0:T(8,128)(2,1)}, bf16[1024,512]{1,0:T(8,128)(2,1)}, u32[]{:S(2)}, u32[]{:S(2)}) collective-permute-start(bf16[1024,512]{1,0:T(8,128)(2,1)} %collective-permute-done.2), channel_id=1, source_target_pairs={{2,4},{3,5},{4,6},{5,7},{10,12},{11,13},{12,14},{13,15},{18,20},{1... | collective-permute-start | bytes 3145736 | tf_op jit(solution)/shard_map/ppermute | solution.py:189
  83.7 44.3 %collective-permute-start.10 = (bf16[1024,512]{1,0:T(8,128)(2,1)S(1)}, bf16[1024,512]{1,0:T(8,128)(2,1)}, u32[]{:S(2)}, u32[]{:S(2)}) collective-permute-start(bf16[1024,512]{1,0:T(8,128)(2,1)S(1)} %bitcast.129), channel_id=1, source_target_pairs={{0,1},{1,0},{2,3},{3,2},{4,5},{5,4},{6,7},{7,6},{8,9},{9,8},{10,11... | collective-permute-start | bytes 3145736 | tf_op jit(solution)/shard_map/ppermute | solution.py:195
  106.5 38.9 %collective-permute-start = (bf16[1024,512]{1,0:T(8,128)(2,1)S(1)}, bf16[1024,512]{1,0:T(8,128)(2,1)}, u32[]{:S(2)}, u32[]{:S(2)}) collective-permute-start(bf16[1024,512]{1,0:T(8,128)(2,1)S(1)} %bitcast.131), channel_id=1, source_target_pairs={{0,1},{1,0},{2,3},{3,2},{4,5},{5,4},{6,7},{7,6},{8,9},{9,8},{10,11... | collective-permute-start | bytes 3145736 | tf_op jit(solution)/shard_map/ppermute | solution.py:195
  107.5 240.2 %reduce-scatter.4.cloned.1.call-start = ((), (), s32[]{:S(2)}) async-start(), calls=%async_computation.5 | async-start | bytes 5242880
  108.6 39.1 %collective-permute-start.1 = (bf16[1024,512]{1,0:T(8,128)(2,1)S(1)}, bf16[1024,512]{1,0:T(8,128)(2,1)S(1)}, u32[]{:S(2)}, u32[]{:S(2)}) collective-permute-start(bf16[1024,512]{1,0:T(8,128)(2,1)S(1)} %bitcast.132), channel_id=1, source_target_pairs={{2,0},{3,1},{4,2},{5,3},{6,4},{7,5},{10,8},{11,9},{12,10},{13,11},... | collective-permute-start | bytes 3145736 | tf_op jit(solution)/shard_map/ppermute | solution.py:190
  128.0 38.5 %collective-permute-start.16 = (bf16[1024,512]{1,0:T(8,128)(2,1)}, bf16[1024,512]{1,0:T(8,128)(2,1)S(1)}, u32[]{:S(2)}, u32[]{:S(2)}) collective-permute-start(bf16[1024,512]{1,0:T(8,128)(2,1)} %collective-permute-done.11), channel_id=1, source_target_pairs={{2,0},{3,1},{4,2},{5,3},{10,8},{11,9},{12,10},{13,11},{18,16},{19,... | collective-permute-start | bytes 3145736 | tf_op jit(solution)/shard_map/ppermute | solution.py:190
  270.7 255.0 %all-reduce.4.cloned.1.call-start = ((), (), s32[]{:S(2)}) async-start(), calls=%async_computation.6 | async-start | bytes 8388608 | tf_op jit(solution)/shard_map/psum | solution.py:263
  275.4 81.8 %collective-permute-start.21 = (bf16[1024,512]{1,0:T(8,128)(2,1)S(1)}, bf16[1024,512]{1,0:T(8,128)(2,1)S(1)}, u32[]{:S(2)}, u32[]{:S(2)}) collective-permute-start(bf16[1024,512]{1,0:T(8,128)(2,1)S(1)} %get-tuple-element.87), channel_id=1, source_target_pairs={{0,1},{1,0},{2,3},{3,2},{4,5},{5,4},{6,7},{7,6},{8,9},{9,8},{10,11... | collective-permute-start | bytes 3145736 | tf_op jit(solution)/shard_map/ppermute | solution.py:195
  352.8 213.7 %all-gather.7.cloned.1.call-start = ((), (), s32[]{:S(2)}) async-start(), calls=%async_computation.4 | async-start | bytes 5242880 | tf_op jit(solution)/shard_map/all_gather | solution.py:266
  379.3 42.3 %collective-permute-start.24 = (bf16[1024,512]{1,0:T(8,128)(2,1)S(1)}, bf16[1024,512]{1,0:T(8,128)(2,1)S(1)}, u32[]{:S(2)}, u32[]{:S(2)}) collective-permute-start(bf16[1024,512]{1,0:T(8,128)(2,1)S(1)} %fusion.5), channel_id=1, source_target_pairs={{0,2},{1,3},{2,4},{3,5},{8,10},{9,11},{10,12},{11,13},{16,18},{17,... | collective-permute-start | bytes 3145736 | tf_op jit(solution)/shard_map/ppermute | solution.py:201
  380.6 44.7 %collective-permute-start.35 = (bf16[1024,512]{1,0:T(8,128)(2,1)S(1)}, bf16[1024,512]{1,0:T(8,128)(2,1)S(1)}, u32[]{:S(2)}, u32[]{:S(2)}) collective-permute-start(bf16[1024,512]{1,0:T(8,128)(2,1)S(1)} %copy-done.4), channel_id=1, source_target_pairs={{0,1},{1,0},{2,3},{3,2},{4,5},{5,4},{6,7},{7,6},{8,9},{9,8},{10,11... | collective-permute-start | bytes 3145736 | tf_op jit(solution)/shard_map/ppermute | solution.py:195
  383.1 61.0 %collective-permute-start.34 = (bf16[1024,512]{1,0:T(8,128)(2,1)S(1)}, bf16[1024,512]{1,0:T(8,128)(2,1)S(1)}, u32[]{:S(2)}, u32[]{:S(2)}) collective-permute-start(bf16[1024,512]{1,0:T(8,128)(2,1)S(1)} %fusion.7), channel_id=1, source_target_pairs={{0,2},{1,3},{2,4},{3,5},{8,10},{9,11},{10,12},{11,13},{16,18},{17,... | collective-permute-start | bytes 3145736 | tf_op jit(solution)/shard_map/ppermute | solution.py:201
  452.6 43.5 %collective-permute-start.28 = (bf16[1024,512]{1,0:T(8,128)(2,1)S(1)}, bf16[1024,512]{1,0:T(8,128)(2,1)S(1)}, u32[]{:S(2)}, u32[]{:S(2)}) collective-permute-start(bf16[1024,512]{1,0:T(8,128)(2,1)S(1)} %fusion.4), channel_id=1, source_target_pairs={{4,2},{5,3},{6,4},{7,5},{12,10},{13,11},{14,12},{15,13},{20,18},{2... | collective-permute-start | bytes 3145736 | tf_op jit(solution)/shard_map/ppermute | solution.py:202
  475.4 43.2 %collective-permute-start.38 = (bf16[1024,512]{1,0:T(8,128)(2,1)S(1)}, bf16[1024,512]{1,0:T(8,128)(2,1)S(1)}, u32[]{:S(2)}, u32[]{:S(2)}) collective-permute-start(bf16[1024,512]{1,0:T(8,128)(2,1)S(1)} %fusion.6), channel_id=1, source_target_pairs={{4,2},{5,3},{6,4},{7,5},{12,10},{13,11},{14,12},{15,13},{20,18},{2... | collective-permute-start | bytes 3145736 | tf_op jit(solution)/shard_map/ppermute | solution.py:202
  477.3 44.5 %collective-permute-start.20 = (bf16[1024,512]{1,0:T(8,128)(2,1)S(1)}, bf16[1024,512]{1,0:T(8,128)(2,1)}, u32[]{:S(2)}, u32[]{:S(2)}) collective-permute-start(bf16[1024,512]{1,0:T(8,128)(2,1)S(1)} %copy-done.3), channel_id=1, source_target_pairs={{0,1},{1,0},{2,3},{3,2},{4,5},{5,4},{6,7},{7,6},{8,9},{9,8},{10,11... | collective-permute-start | bytes 3145736 | tf_op jit(solution)/shard_map/ppermute | solution.py:195
  477.4 55.0 %collective-permute-start.26 = (bf16[1024,512]{1,0:T(8,128)(2,1)}, bf16[1024,512]{1,0:T(8,128)(2,1)}, u32[]{:S(2)}, u32[]{:S(2)}) collective-permute-start(bf16[1024,512]{1,0:T(8,128)(2,1)} %get-tuple-element.66), channel_id=1, source_target_pairs={{0,2},{1,3},{2,4},{3,5},{4,6},{5,7},{8,10},{9,11},{10,12},{11,13},... | collective-permute-start | bytes 3145736 | tf_op jit(solution)/shard_map/ppermute | solution.py:201
  497.4 43.8 %collective-permute-start.29 = (bf16[1024,512]{1,0:T(8,128)(2,1)}, bf16[1024,512]{1,0:T(8,128)(2,1)}, u32[]{:S(2)}, u32[]{:S(2)}) collective-permute-start(bf16[1024,512]{1,0:T(8,128)(2,1)} %add.166), channel_id=1, source_target_pairs={{2,0},{3,1},{4,2},{5,3},{6,4},{7,5},{10,8},{11,9},{12,10},{13,11},... | collective-permute-start | bytes 3145736 | tf_op jit(solution)/shard_map/ppermute | solution.py:202
  499.3 45.9 %collective-permute-start.30 = (bf16[1024,512]{1,0:T(8,128)(2,1)}, bf16[1024,512]{1,0:T(8,128)(2,1)S(1)}, u32[]{:S(2)}, u32[]{:S(2)}) collective-permute-start(bf16[1024,512]{1,0:T(8,128)(2,1)} %get-tuple-element.80), channel_id=1, source_target_pairs={{0,1},{1,0},{2,3},{3,2},{4,5},{5,4},{6,7},{7,6},{8,9},{9,8},{10,11... | collective-permute-start | bytes 3145736 | tf_op jit(solution)/shard_map/ppermute | solution.py:195
  521.8 40.9 %collective-permute-start.39 = (bf16[1024,512]{1,0:T(8,128)(2,1)}, bf16[1024,512]{1,0:T(8,128)(2,1)}, u32[]{:S(2)}, u32[]{:S(2)}) collective-permute-start(bf16[1024,512]{1,0:T(8,128)(2,1)} %add.176), channel_id=1, source_target_pairs={{2,0},{3,1},{4,2},{5,3},{6,4},{7,5},{10,8},{11,9},{12,10},{13,11},... | collective-permute-start | bytes 3145736 | tf_op jit(solution)/shard_map/ppermute | solution.py:202
  (27 other events, 471.8 us)
Sparse Core Ops, SparseCore 0:
  107.6 52.9 all-gather.4
  270.9 76.7 reduce-scatter.3
  351.6 104.1 all-reduce.3
  457.5 52.6 all-gather.6

commit v2 on v0

v2 whole, which is shorter than its diff:
```python
import functools
import math

import jax
import jax.numpy as jnp
from jax import lax
from jax.experimental import pallas as pl
from jax.experimental.pallas import tpu as pltpu
from jax.sharding import PartitionSpec as P

F32 = jnp.float32
BF16 = jnp.bfloat16
PARAMS = pltpu.CompilerParams(dimension_semantics=("arbitrary",))


def gelu_parts(value_in):
    cdf_part = 0.5 * (1.0 + lax.erf(value_in * 0.7071067811865476))
    slope_part = cdf_part + value_in * jnp.exp(-0.5 * value_in * value_in) * 0.3989422804014327
    return (value_in * cdf_part, slope_part)


def dot(a, b, ca, cb):
    return lax.dot_general(a, b, (((ca,), (cb,)), ((), ())), preferred_element_type=F32)


def cost(flops, elements, trans=0):
    return pl.CostEstimate(flops=flops, bytes_accessed=2 * elements, transcendentals=trans)


def expand_kernel(meta, x_ref, w_ref, own_ref, send_ref, *, pa, bw, hd, sub):
    low = meta[1] == 0
    m = hd * sub
    for e in range(2):
        own, send = [], []
        for a in range(pa):
            val = dot(w_ref[e, 0, a], x_ref[e, a * bw : (a + 1) * bw, :], 1, 0)
            first = val[:m].reshape(hd, sub, val.shape[-1])
            second = val[m:].reshape(hd, sub, val.shape[-1])
            own.append(jnp.where(low, first, second))
            send.append(jnp.where(low, second, first))
        own_ref[e] = jnp.concatenate(own, axis=1).astype(BF16)
        send_ref[e] = jnp.concatenate(send, axis=1).astype(BF16)


def expand(meta, xg, w14, hd, sub):
    _, nl, wd, m2, bw = w14.shape
    rows = xg.shape[-1]
    pa = min(wd, 2)
    out = jax.ShapeDtypeStruct((2, hd, wd * sub, rows), BF16)
    out_spec = pl.BlockSpec((2, hd, pa * sub, rows), lambda s, meta: (0, 0, s, 0))
    return pl.pallas_call(
        functools.partial(expand_kernel, pa=pa, bw=bw, hd=hd, sub=sub),
        grid_spec=pltpu.PrefetchScalarGridSpec(
            num_scalar_prefetch=1,
            grid=(wd // pa,),
            in_specs=[
                pl.BlockSpec((2, pa * bw, rows), lambda s, meta: (0, s, 0)),
                pl.BlockSpec((2, 1, pa, m2, bw), lambda s, meta: (0, meta[0], s, 0, 0)),
            ],
            out_specs=[out_spec, out_spec],
        ),
        out_shape=[out, out],
        compiler_params=PARAMS,
        cost_estimate=cost(4 * wd * m2 * bw * rows, 2 * wd * (bw * rows + m2 * bw + m2 * rows)),
        name="expand",
    )(meta, xg, w14)


def middle_kernel(meta, *refs, nl, part, dp, scale):
    slots = nl + 1
    owns, recvs = refs[:slots], refs[slots : 2 * slots]
    w2_ref, w3_ref, own_ref, send_ref, g2_ref, g3_ref, ysc = refs[2 * slots :]
    pos, core = meta[0], meta[1]

    def place(k, where):
        base = pl.multiple_of((where * 2 + core) * part, part)
        other = pl.multiple_of((where * 2 + 1 - core) * part, part)
        for e in range(2):
            ysc[e, pl.ds(base, part), :] = owns[k][e, 0].astype(F32)
            ysc[e, pl.ds(other, part), :] = recvs[k][e, 0].astype(F32)

    for k in range(nl):
        place(k, lax.rem(pos + k, nl))

    @pl.when(meta[2] >= 0)
    def _():
        place(nl, meta[2])

    yb = ysc[0].astype(BF16)
    dzb = ysc[1].astype(BF16)
    w2 = w2_ref[0]
    w3 = w3_ref[0]
    pre = dot(w2, yb, 0, 0)
    val, slope = gelu_parts(pre)
    act = val.astype(BF16)
    dact = dot(w3, dzb, 1, 0)
    dpre = (dact * slope).astype(BF16)
    g2 = (dot(yb, dpre, 1, 1) * scale).astype(BF16)
    g3 = (dot(act, dzb, 1, 1) * scale).astype(BF16)
    step = g2.shape[0] // dp
    for q in range(dp):
        g2_ref[meta[4 + q], 0] = g2[q * step : (q + 1) * step]
        g3_ref[meta[4 + dp + q], 0] = g3[q * step : (q + 1) * step]
    ysc[0] = dot(w3, act, 0, 0)
    ysc[1] = dot(w2, dpre, 1, 0)
    for k in range(nl):
        for e in range(2):
            base = pl.multiple_of((k * 2 + core) * part, part)
            other = pl.multiple_of((k * 2 + 1 - core) * part, part)
            own_ref[e, 0, k * part : (k + 1) * part] = ysc[e, pl.ds(base, part), :].astype(BF16)
            send_ref[e, 0, k * part : (k + 1) * part] = ysc[e, pl.ds(other, part), :].astype(BF16)


def middle(meta, owns, recvs, w2, w3, dp, scale):
    hd, k, j = w2.shape
    nl = len(owns) - 1
    _, _, part, rows = owns[0].shape
    slot = pl.BlockSpec((2, 1, part, rows), lambda b, meta: (0, b, 0, 0))
    full = pl.BlockSpec((2, 1, nl * part, rows), lambda b, meta: (0, b, 0, 0))
    wspec = pl.BlockSpec((1, k, j), lambda b, meta: (b, 0, 0))
    gspec = pl.BlockSpec((dp, 1, k // dp, j), lambda b, meta: (0, b, 0, 0))
    zout = jax.ShapeDtypeStruct((2, hd, nl * part, rows), BF16)
    gout = jax.ShapeDtypeStruct((dp, hd, k // dp, j), BF16)
    return pl.pallas_call(
        functools.partial(middle_kernel, nl=nl, part=part, dp=dp, scale=scale),
        grid_spec=pltpu.PrefetchScalarGridSpec(
            num_scalar_prefetch=1,
            grid=(hd,),
            in_specs=[slot] * (2 * nl + 2) + [wspec, wspec],
            out_specs=[full, full, gspec, gspec],
            scratch_shapes=[pltpu.VMEM((2, k, rows), F32)],
        ),
        out_shape=[zout, zout, gout, gout],
        compiler_params=PARAMS,
        cost_estimate=cost(
            12 * hd * k * j * rows, 4 * hd * k * rows + 4 * hd * k * j, 2 * hd * j * rows
        ),
        name="middle",
    )(meta, *owns, *recvs, w2, w3)


def contract_kernel(meta, *refs, late, chain, pa, bw, hd, sub, dp, scale):
    refs = list(refs)
    zo_ref, zr_ref, w_ref, x_ref = refs[:4]
    refs = refs[4:]
    late_ref = refs.pop(0) if late else None
    if chain:
        refs = refs[2:]
    part_ref, g1_ref, g4_ref, zsc = refs
    core = meta[1]
    rows = zo_ref.shape[-1]
    m = hd * sub
    step = 2 * m // dp
    mine = pl.multiple_of(core * m, m)
    other = pl.multiple_of((1 - core) * m, m)
    for e in range(2):
        for ref, base in ((zo_ref, mine), (zr_ref, other)):
            chunk = ref[e].astype(F32)
            for a in range(pa):
                piece = chunk[:, a * sub : (a + 1) * sub, :].reshape(m, rows)
                zsc[e, a, pl.ds(base, m), :] = piece.astype(BF16)
    for a in range(pa):
        span = slice(a * bw, (a + 1) * bw)
        z, dy = zsc[0, a], zsc[1, a]
        part_ref[0, span, :] = dot(w_ref[1, 0, a], z, 0, 0).astype(BF16)
        part_ref[1, span, :] = dot(w_ref[0, 0, a], dy, 0, 0).astype(BF16)
        x, g = x_ref[0, span, :], x_ref[1, span, :]
        if late:
            take = meta[3] > 0
            x = jnp.where(take, late_ref[0, span, :], x)
            g = jnp.where(take, late_ref[1, span, :], g)
        g1 = (dot(dy, x, 1, 1) * scale).astype(BF16)
        g4 = (dot(z, g, 1, 1) * scale).astype(BF16)
        for q in range(dp):
            g1_ref[meta[4 + q], 0, a] = g1[q * step : (q + 1) * step]
            g4_ref[meta[4 + dp + q], 0, a] = g4[q * step : (q + 1) * step]


def contract(meta, z_own, z_recv, w14, xg, late, grads, sub, dp, scale):
    _, nl, wd, m2, bw = w14.shape
    hd, rows = z_own.shape[1], z_own.shape[-1]
    pa = min(wd, 2)
    steps = wd // pa
    zspec = pl.BlockSpec((2, hd, pa * sub, rows), lambda s, meta: (0, 0, meta[0] * steps + s, 0))
    xspec = pl.BlockSpec((2, pa * bw, rows), lambda s, meta: (0, s, 0))
    wspec = pl.BlockSpec((2, 1, pa, m2, bw), lambda s, meta: (0, meta[0], s, 0, 0))
    gspec = pl.BlockSpec((dp, 1, pa, m2 // dp, bw), lambda s, meta: (0, meta[0], s, 0, 0))
    gout = jax.ShapeDtypeStruct((dp, nl, wd, m2 // dp, bw), BF16)
    args = [meta, z_own, z_recv, w14, xg]
    specs = [zspec, zspec, wspec, xspec]
    if late is not None:
        args.append(late)
        specs.append(xspec)
    aliases = {}
    if grads is not None:
        aliases = {len(args): 1, len(args) + 1: 2}
        args += list(grads)
        specs += [pl.BlockSpec(memory_space=pl.ANY)] * 2
    return pl.pallas_call(
        functools.partial(
            contract_kernel,
            late=late is not None,
            chain=grads is not None,
            pa=pa,
            bw=bw,
            hd=hd,
            sub=sub,
            dp=dp,
            scale=scale,
        ),
        grid_spec=pltpu.PrefetchScalarGridSpec(
            num_scalar_prefetch=1,
            grid=(steps,),
            in_specs=specs,
            out_specs=[xspec, gspec, gspec],
            scratch_shapes=[pltpu.VMEM((2, pa, m2, rows), BF16)],
        ),
        out_shape=[jax.ShapeDtypeStruct(xg.shape, BF16), gout, gout],
        input_output_aliases=aliases,
        compiler_params=PARAMS,
        cost_estimate=cost(
            8 * wd * m2 * bw * rows, 2 * wd * (2 * bw * rows + m2 * rows + 2 * m2 * bw)
        ),
        name="contract",
    )(*args)


def finish_kernel(tab, p_ref, q_ref, o_ref, *, dp, flip):
    half = dp // 2
    for q in range(dp):
        slot = tab[q]
        inner = lax.rem(slot, half)
        val = jnp.where(slot < half, p_ref[inner, 0, 0].astype(F32), q_ref[inner, 0, 0].astype(F32))
        step = val.shape[0]
        if flip:
            o_ref[0, :, q * step : (q + 1) * step] = val.T
        else:
            o_ref[0, q * step : (q + 1) * step, :] = val


def finish_flip_kernel(tab, p_ref, q_ref, o_ref, *, dp):
    half = dp // 2
    vals = []
    for q in range(dp):
        slot = tab[q]
        inner = lax.rem(slot, half)
        vals.append(
            jnp.where(slot < half, p_ref[inner, 0, 0].astype(F32), q_ref[inner, 0, 0].astype(F32))
        )
    o_ref[0] = jnp.concatenate(vals, axis=0).T


def finish(tab, halves, flip):
    p, q = halves
    half, outer, wd, step, bw = p.shape
    dp = 2 * half
    size = dp * step
    spec = pl.BlockSpec((half, 1, 1, step, bw), lambda o, a, tab: (0, o, a, 0, 0))
    if flip:
        shape, ospec = (wd, bw, outer * size), pl.BlockSpec((1, bw, size), lambda o, a, tab: (a, 0, o))
        body = functools.partial(finish_flip_kernel, dp=dp)
        if size % 128:
            merged = jnp.concatenate([p, q], axis=0)[tab]
            return jnp.transpose(merged, (2, 4, 1, 0, 3)).reshape(shape).astype(F32)
    else:
        shape, ospec = (wd, outer * size, bw), pl.BlockSpec((1, size, bw), lambda o, a, tab: (a, o, 0))
        body = functools.partial(finish_kernel, dp=dp, flip=False)
    return pl.pallas_call(
        body,
        grid_spec=pltpu.PrefetchScalarGridSpec(
            num_scalar_prefetch=1, grid=(outer, wd), in_specs=[spec, spec], out_specs=ospec
        ),
        out_shape=jax.ShapeDtypeStruct(shape, F32),
        compiler_params=pltpu.CompilerParams(dimension_semantics=("arbitrary", "arbitrary")),
        cost_estimate=cost(0, 3 * wd * outer * size * bw),
        name="finish",
    )(tab, p, q)


def up_pairs(lo, hi):
    return [(2 * p + c, 2 * p + 2 + c) for p in range(lo, hi) for c in range(2)]


def down_pairs(lo, hi):
    return [(2 * p + 2 + c, 2 * p + c) for p in range(lo, hi) for c in range(2)]


def swap(val, n):
    return lax.ppermute(val, "tensor", [(i, i ^ 1) for i in range(n)])


def add(a, b):
    return (a.astype(F32) + b.astype(F32)).astype(BF16)


def line_scatter(parts, nl):
    up, down = parts[nl - 1], parts[1]
    for r in range(1, nl):
        up = lax.ppermute(up, "tensor", up_pairs(0, r))
        down = lax.ppermute(down, "tensor", down_pairs(nl - 1 - r, nl - 1))
        if r < nl - 1:
            up = add(up, parts[nl - 1 - r])
            down = add(down, parts[r + 1])
    return (parts[0].astype(F32) + up.astype(F32) + down.astype(F32)).astype(BF16)


X_PAIRS = [(i, i ^ 1) for i in range(4)]
Y_PAIRS = [(i, i ^ 2) for i in range(4)]


def reduce_dp(val, dp, pairs):
    if dp != 4:
        return lax.psum_scatter(val, "dp")
    kept = add(val[:2], lax.ppermute(val[2:], "dp", pairs[0]))
    return add(kept[0], lax.ppermute(kept[1], "dp", pairs[1]))


def gather_dp(val, dp, pairs):
    if dp != 4:
        every = lax.all_gather(val, "dp")
        return every[: dp // 2], every[dp // 2 :]
    low = jnp.stack([val, lax.ppermute(val, "dp", pairs[1])])
    return low, lax.ppermute(low, "dp", pairs[0])


def body(tokens, cotangent, w_first, w_second, w_third, w_fourth):
    rows = tokens.shape[0]
    wd, bw, _ = w_first.shape
    hd = w_second.shape[0]
    n = lax.axis_size("tensor")
    dp = lax.axis_size("dp")
    nl = n // 2
    sub = bw // (wd * n)
    m2 = 2 * hd * sub
    step = m2 // dp
    scale = 1.0 / math.sqrt(rows * dp)
    me = lax.axis_index("tensor")
    mine = lax.axis_index("dp")
    pos, core = me // 2, me % 2
    lines = [[2 * p + c for p in range(nl)] for c in range(2)]
    x_first, y_first = (X_PAIRS, Y_PAIRS), (Y_PAIRS, X_PAIRS)

    dps = jnp.arange(dp, dtype=jnp.int32)
    if dp == 4:
        flips = dps ^ mine
        tab_x = ((flips & 1) << 1) | (flips >> 1)
        tab_y = flips
    else:
        tab_x = tab_y = dps
    low_end, high_end = pos == 0, pos == nl - 1
    late_pos = jnp.where(low_end, nl - 1, jnp.where(high_end, 0, -1))

    def meta_of(head, late):
        head = jnp.stack([jnp.asarray(v, jnp.int32) for v in (head, core, late_pos, late)])
        return jnp.concatenate([head, tab_x, tab_y])

    w14 = jnp.stack([jnp.swapaxes(w_first, 1, 2), w_fourth])
    w14 = w14.reshape(2, wd, nl, dp, step, bw)
    w14 = lax.dynamic_index_in_dim(w14, mine, axis=3, keepdims=False)
    w14 = jnp.transpose(w14, (2, 0, 1, 3, 4))
    w14 = lax.all_to_all(
        w14, "tensor", split_axis=0, concat_axis=0, axis_index_groups=lines, tiled=True
    )
    sides = []
    for e, (pairs, tab) in enumerate(((x_first, tab_x), (y_first, tab_y))):
        every = jnp.concatenate(gather_dp(w14[:, e], dp, pairs))
        every = [lax.dynamic_index_in_dim(every, tab[q], keepdims=False) for q in range(dp)]
        sides.append(jnp.stack(every, axis=2).reshape(nl, wd, m2, bw))
    w14 = jnp.stack(sides)

    own = jnp.stack([tokens.T, cotangent.T])
    ups, downs = [own], [own]
    for r in range(1, nl):
        ups.append(lax.ppermute(ups[-1], "tensor", up_pairs(r - 1, nl - 1)))
        downs.append(lax.ppermute(downs[-1], "tensor", down_pairs(0, nl - r)))
    slots = [own]
    for k in range(1, nl):
        if k == 1:
            slots.append(downs[1])
        elif k == nl - 1:
            slots.append(ups[1])
        else:
            slots.append(downs[k] + ups[nl - k])
    late = ups[nl - 1] + downs[nl - 1]
    metas = [meta_of((pos + k) % nl, 0) for k in range(nl)]
    metas[1] = meta_of((pos + 1) % nl, high_end)
    metas[nl - 1] = meta_of((pos + nl - 1) % nl, low_end)
    late_meta = meta_of(jnp.maximum(late_pos, 0), 0)

    owns, recvs = [], []
    for meta, xg in zip(metas + [late_meta], slots + [late]):
        mine_part, send = expand(meta, xg, w14, hd, sub)
        owns.append(mine_part)
        recvs.append(swap(send, n))
    z_own, z_send, g2, g3 = middle(
        meta_of(pos, 0), owns, recvs, w_second, w_third, dp, scale
    )
    z_recv = swap(z_send, n)

    parts, grads = [None] * nl, None
    order = [k for pair in zip(range(nl - 1, nl // 2, -1), range(1, nl // 2)) for k in pair]
    for k in order + [nl // 2, 0]:
        extra = late if k in (1, nl - 1) else None
        parts[k], g1, g4 = contract(
            metas[k], z_own, z_recv, w14, slots[k], extra, grads, sub, dp, scale
        )
        grads = (g1, g4)
    both = line_scatter(parts, nl)

    g2 = gather_dp(reduce_dp(g2, dp, x_first), dp, x_first)
    g3 = gather_dp(reduce_dp(g3, dp, y_first), dp, y_first)
    g1 = reduce_dp(grads[0], dp, x_first)
    g4 = reduce_dp(grads[1], dp, y_first)
    g14 = jnp.stack([g1, g4], axis=1)
    g14 = lax.all_to_all(
        g14, "tensor", split_axis=0, concat_axis=0, axis_index_groups=lines, tiled=True
    )
    g1 = gather_dp(g14[:, 0], dp, x_first)
    g4 = gather_dp(g14[:, 1], dp, y_first)

    def single(halves):
        return [h[:, None] for h in halves]

    return (
        both[0].T,
        both[1].T,
        finish(tab_x, g1, True),
        finish(tab_x, single(g2), False),
        finish(tab_y, single(g3), False),
        finish(tab_y, g4, False),
    )


def solution(mesh):
    return jax.shard_map(
        body,
        mesh=mesh,
        in_specs=(
            P("dp", "tensor"),
            P("dp", "tensor"),
            P("tensor", None, None),
            P("tensor", None, None),
            P("tensor", None, None),
            P("tensor", None, None),
        ),
        out_specs=(
            P("dp", "tensor"),
            P("dp", "tensor"),
            P("tensor", None, None),
            P("tensor", None, None),
            P("tensor", None, None),
            P("tensor", None, None),
        ),
        check_vma=False,
    )
```

time: 629 us -> 457 us (0.73)
  waiting for transfers between devices: 477 us -> 181 us
  Pallas kernels: 0 us -> 107 us
  matrix products: 59.6 us -> 0 us
  starting transfers between devices: 28.9 us -> 76.7 us
  other arithmetic: 8.08 us -> 40.3 us
  local copies, waits for them, and re-layouts: 39 us -> 27.7 us
    all_to_all x4 -> x2, waiting for transfers between devices: 314 us -> 20.5 us  [the longest x1 12.2 us: body(): lax.all_to_all(w14, 'tensor', split_axis=0, concat_axis=0, axis_index_gro...]
    psum x1 -> x0, waiting for transfers between devices: 163 us -> none  [body(): lax.psum(grad_first.astype(jnp.bfloat16), 'dp').astype(jnp.float32)]
    ppermute x0 -> x38, waiting for transfers between devices: none -> 161 us  [the longest x3 60.2 us: body(): ups.append(lax.ppermute(ups[-1], 'tensor', up_pairs(r - 1, nl - 1)))]
    pallas_call x0 -> x14, Pallas kernels: none -> 107 us  [the longest x4 42 us: finish(): pl.pallas_call(body, grid_spec=pltpu.PrefetchScalarGridSpec(num_scalar_pr...]
    ppermute x0 -> x38, starting transfers between devices: none -> 64.9 us  [the longest x3 12.7 us: body(): downs.append(lax.ppermute(downs[-1], 'tensor', down_pairs(0, nl - r)))]
    dot_general x11 -> x0, matrix products: 56.1 us -> none  [the longest x1 7.85 us: body(): jnp.einsum('gbact,bjgac->bjt', returned, third_split, preferred_element_t...]
    convert_element_type x7 -> x0, local copies, waits for them, and re-layouts: 17.3 us -> none  [the longest x1 2.53 us: body(): grad_fourth.astype(jnp.bfloat16)]
    all_to_all x4 -> x2, starting transfers between devices: 28.9 us -> 11.8 us  [the longest x1 6.48 us: body(): lax.all_to_all(w14, 'tensor', split_axis=0, concat_axis=0, axis_index_gro...]
  transfers between devices with their start and end apart: 5 -> 40, of which waited for: 5 -> 17; matrix products, arithmetic and copies ran while one was open for 10% -> 12% of each run, Pallas kernels for 0% -> 19%
where the time goes in v2:
time: 457 us; the launch traced here: 449 us
  waiting for transfers between devices  181 us (40%)
  Pallas kernels  107 us (23%)
  starting transfers between devices  76.7 us (17%)
  other arithmetic  40.3 us (9%)
  local copies, waits for them, and re-layouts  27.7 us (6%)
  between operations  15.9 us (3%)
    ppermute x3, waiting for transfers between devices, body(): ups.append(lax.ppermute(ups[-1], 'tensor', up_pairs(r - 1, nl - 1)))  60.2 us
    pallas_call x4, Pallas kernels, finish(): pl.pallas_call(body, grid_spec=pltpu.PrefetchScalarGridSpec(num_scalar_pr...  42 us
    ppermute x6, waiting for transfers between devices, gather_dp(): low = jnp.stack([val, lax.ppermute(val, 'dp', pairs[1])])  24.5 us
    pallas_call x1, Pallas kernels, middle(): pl.pallas_call(functools.partial(middle_kernel, nl=nl, part=part, dp=dp,...  22.6 us
    pallas_call x4, Pallas kernels, contract(): pl.pallas_call(functools.partial(contract_kernel, late=late is not None,...  22.2 us
    pallas_call x5, Pallas kernels, expand(): pl.pallas_call(functools.partial(expand_kernel, pa=pa, bw=bw, hd=hd, sub=...  19.7 us
    ppermute x3, waiting for transfers between devices, line_scatter(): down = lax.ppermute(down, 'tensor', down_pairs(nl - 1 - r, nl - 1))  19.6 us
    ppermute x4, waiting for transfers between devices, reduce_dp(): kept = add(val[:2], lax.ppermute(val[2:], 'dp', pairs[0]))  18.8 us
  transfers between devices with their start and end apart: 40, of which 17 were waited for; matrix products, arithmetic and copies ran while one was open for 12% of the time, Pallas kernels for 19%

profile of v2, /device:TPU:16, one launch (start us, length us, event | category | flops | bytes accessed | tf_op | source)
XLA Modules:
  0.0 448.6 jit_solution(8981043931164297943)
XLA Ops:
  17.2 6.5 %all-to-all-start = ((bf16[4,2,4,64,256]{4,3,2,1,0:T(8,128)(2,1)}), bf16[4,2,4,64,256]{4,3,2,1,0:T(8,128)(2,1)S(1)}, u32[]{:S(2)}, u32[]{:S(2)}) async-start(bf16[4,2,4,64,256]{4,3,2,1,0:T(8,128)(2,1)} %copy.52), calls=%async_computation | async-start | bytes 2097152 | tf_op jit(solution)/shard_map/all_to_all | solution.py:361
  23.6 31.9 %collective-permute-done.6.x_ref.refs_3_ = bf16[2,1024,512]{2,1,0:T(8,128)(2,1)} collective-permute-done((bf16[2,1024,512]{2,1,0:T(8,128)(2,1)S(1)}, bf16[2,1024,512]{2,1,0:T(8,128)(2,1)}, u32[]{:S(2)}, u32[]{:S(2)}) %collective-permute-start.6) | collective-permute-done | bytes 2097184 | tf_op jit(solution)/shard_map/ppermute | solution.py:374
  59.0 8.2 %collective-permute-start.5 = (bf16[2,1024,512]{2,1,0:T(8,128)(2,1)}, bf16[2,1024,512]{2,1,0:T(8,128)(2,1)}, u32[]{:S(2)}, u32[]{:S(2)}) collective-permute-start(bf16[2,1024,512]{2,1,0:T(8,128)(2,1)} %collective-permute-done.4.x_ref.refs_3_), channel_id=1, source_target_pairs={{2,0},{3,1},{4,2},{5,3},{10,8},{11,9},{12,10},{13,11},{18,16},{19,... | collective-permute-start | bytes 6291464 | tf_op jit(solution)/shard_map/ppermute | solution.py:375
  67.3 12.2 %all-to-all-done = bf16[4,2,4,64,256]{4,3,2,1,0:T(8,128)(2,1)S(1)} async-done(((bf16[4,2,4,64,256]{4,3,2,1,0:T(8,128)(2,1)}), bf16[4,2,4,64,256]{4,3,2,1,0:T(8,128)(2,1)S(1)}, u32[]{:S(2)}, u32[]{:S(2)}) %all-to-all-start) | async-done | bytes 1048608 | tf_op jit(solution)/shard_map/all_to_all | solution.py:361
  82.8 8.0 %collective-permute-done = bf16[4,4,64,256]{3,2,1,0:T(8,128)(2,1)S(1)} collective-permute-done((bf16[4,4,64,256]{3,2,1,0:T(8,128)(2,1)S(1)}, bf16[4,4,64,256]{3,2,1,0:T(8,128)(2,1)S(1)}, u32[]{:S(2)}, u32[]{:S(2)}) %collective-permute-start) | collective-permute-done | bytes 524320 | tf_op jit(solution)/shard_map/ppermute | solution.py:322
  93.5 28.4 %collective-permute-done.7 = bf16[2,1024,512]{2,1,0:T(8,128)(2,1)} collective-permute-done((bf16[2,1024,512]{2,1,0:T(8,128)(2,1)}, bf16[2,1024,512]{2,1,0:T(8,128)(2,1)}, u32[]{:S(2)}, u32[]{:S(2)}) %collective-permute-start.7) | collective-permute-done | bytes 2097184 | tf_op jit(solution)/shard_map/ppermute | solution.py:374
  188.4 22.6 %middle.1 = (bf16[2,16,128,512]{3,2,1,0:T(8,128)(2,1)}, bf16[2,16,128,512]{3,2,1,0:T(8,128)(2,1)}, bf16[4,16,64,256]{3,2,1,0:T(8,128)(2,1)}, bf16[4,16,64,256]{3,2,1,0:T(8,128)(2,1)}) custom-call(s32[12]{0:T(128)} %concatenate.28.meta, bf16[2,16,32,512]{3,2,1,0:T(8,128)(2,1)} %get-tuple-element.32.refs_0_, ...), custom_call_target="tpu_custom_call" | custom-call | flops 6442450944 | bytes 25165824 | tf_op jit(solution)/shard_map/middle/pallas_call | solution.py:124
  218.6 5.8 %contract.4 = (bf16[2,1024,512]{2,1,0:T(8,128)(2,1)}, bf16[4,4,4,64,256]{4,3,2,1,0:T(8,128)(2,1)}, bf16[4,4,4,64,256]{4,3,2,1,0:T(8,128)(2,1)}) custom-call(s32[12]{0:T(128)} %concatenate.33.meta, bf16[2,16,128,512]{3,2,1,0:T(8,128)(2,1)} %get-tuple-element.42.refs_0_, bf16[2,16,128,512]{3,2,1,0:T(8,128)(2,1)} %collective-permute-done.15.refs_1_, ...), custom_call_target="tpu_custom_call" | custom-call | flops 1073741824 | bytes 8388608 | tf_op jit(solution)/shard_map/contract/pallas_call | solution.py:199
  224.3 5.8 %contract.5 = (bf16[2,1024,512]{2,1,0:T(8,128)(2,1)}, bf16[4,4,4,64,256]{4,3,2,1,0:T(8,128)(2,1)}, bf16[4,4,4,64,256]{4,3,2,1,0:T(8,128)(2,1)}) custom-call(s32[12]{0:T(128)} %concatenate.31.meta, bf16[2,16,128,512]{3,2,1,0:T(8,128)(2,1)} %get-tuple-element.42.refs_0_, ...), custom_call_target="tpu_custom_call", output_to_operand_aliasing={{1}: (6, {}), {2}: (7, {})} | custom-call | flops 1073741824 | bytes 8388608 | tf_op jit(solution)/shard_map/contract/pallas_call | solution.py:199
  235.4 5.4 %contract.7 = (bf16[2,1024,512]{2,1,0:T(8,128)(2,1)}, bf16[4,4,4,64,256]{4,3,2,1,0:T(8,128)(2,1)}, bf16[4,4,4,64,256]{4,3,2,1,0:T(8,128)(2,1)}) custom-call(s32[12]{0:T(128)} %concatenate.27.meta, bf16[2,16,128,512]{3,2,1,0:T(8,128)(2,1)} %get-tuple-element.42.refs_0_, ...), custom_call_target="tpu_custom_call", output_to_operand_aliasing={{1}: (5, {}), {2}: (6, {})} | custom-call | flops 1073741824 | bytes 8388608 | tf_op jit(solution)/shard_map/contract/pallas_call | solution.py:199
  253.1 15.1 %collective-permute-done.22 = bf16[2,4,4,64,256]{4,3,2,1,0:T(8,128)(2,1)S(1)} collective-permute-done((bf16[2,4,4,64,256]{4,3,2,1,0:T(8,128)(2,1)S(1)}, bf16[2,4,4,64,256]{4,3,2,1,0:T(8,128)(2,1)S(1)}, u32[]{:S(2)}, u32[]{:S(2)}) %collective-permute-start.22) | collective-permute-done | bytes 1048608 | tf_op jit(solution)/shard_map/ppermute | solution.py:314
  275.8 17.2 %collective-permute-done.19 = bf16[2,1024,512]{2,1,0:T(8,128)(2,1)S(1)} collective-permute-done((bf16[2,1024,512]{2,1,0:T(8,128)(2,1)S(1)}, bf16[2,1024,512]{2,1,0:T(8,128)(2,1)S(1)}, u32[]{:S(2)}, u32[]{:S(2)}) %collective-permute-start.19) | collective-permute-done | bytes 2097184 | tf_op jit(solution)/shard_map/ppermute | solution.py:300
  298.3 5.4 %collective-permute-start.20 = (bf16[2,1024,512]{2,1,0:T(8,128)(2,1)}, bf16[2,1024,512]{2,1,0:T(8,128)(2,1)}, u32[]{:S(2)}, u32[]{:S(2)}) collective-permute-start(bf16[2,1024,512]{2,1,0:T(8,128)(2,1)} %get-tuple-element.85), channel_id=1, source_target_pairs={{4,2},{5,3},{6,4},{7,5},{12,10},{13,11},{14,12},{15,13},{20,18},{2... | collective-permute-start | bytes 6291464 | tf_op jit(solution)/shard_map/ppermute | solution.py:300
  306.2 6.2 %collective-permute-done.25 = bf16[4,4,64,256]{3,2,1,0:T(8,128)(2,1)S(1)} collective-permute-done((bf16[4,4,64,256]{3,2,1,0:T(8,128)(2,1)S(1)}, bf16[4,4,64,256]{3,2,1,0:T(8,128)(2,1)S(1)}, u32[]{:S(2)}, u32[]{:S(2)}) %collective-permute-start.25) | collective-permute-done | bytes 524320 | tf_op jit(solution)/shard_map/ppermute | solution.py:315
  313.7 5.3 %all-to-all-start.1 = ((bf16[4,2,4,64,256]{4,3,2,1,0:T(8,128)(2,1)}), bf16[4,2,4,64,256]{4,3,2,1,0:T(8,128)(2,1)S(1)}, u32[]{:S(2)}, u32[]{:S(2)}) async-start(bf16[4,2,4,64,256]{4,3,2,1,0:T(8,128)(2,1)} %copy.57), calls=%async_computation.1 | async-start | bytes 2097152 | tf_op jit(solution)/shard_map/all_to_all | solution.py:415
  324.5 8.4 %collective-permute-done.34 = bf16[16,64,256]{2,1,0:T(8,128)(2,1)S(1)} collective-permute-done((bf16[16,64,256]{2,1,0:T(8,128)(2,1)S(1)}, bf16[16,64,256]{2,1,0:T(8,128)(2,1)S(1)}, u32[]{:S(2)}, u32[]{:S(2)}) %collective-permute-start.34) | collective-permute-done | bytes 524320 | tf_op jit(solution)/shard_map/ppermute | solution.py:322
  335.9 12.2 %collective-permute-done.17 = bf16[2,1024,512]{2,1,0:T(8,128)(2,1)} collective-permute-done((bf16[2,1024,512]{2,1,0:T(8,128)(2,1)}, bf16[2,1024,512]{2,1,0:T(8,128)(2,1)}, u32[]{:S(2)}, u32[]{:S(2)}) %collective-permute-start.17) | collective-permute-done | bytes 2097184 | tf_op jit(solution)/shard_map/ppermute | solution.py:299
  364.3 8.3 %all-to-all-done.1 = bf16[4,2,4,64,256]{4,3,2,1,0:T(8,128)(2,1)S(1)} async-done(((bf16[4,2,4,64,256]{4,3,2,1,0:T(8,128)(2,1)}), bf16[4,2,4,64,256]{4,3,2,1,0:T(8,128)(2,1)S(1)}, u32[]{:S(2)}, u32[]{:S(2)}) %all-to-all-start.1) | async-done | bytes 1048608 | tf_op jit(solution)/shard_map/all_to_all | solution.py:415
  376.5 8.1 %collective-permute-done.36 = bf16[4,4,64,256]{3,2,1,0:T(8,128)(2,1)S(1)} collective-permute-done((bf16[4,4,64,256]{3,2,1,0:T(8,128)(2,1)S(1)}, bf16[4,4,64,256]{3,2,1,0:T(8,128)(2,1)S(1)}, u32[]{:S(2)}, u32[]{:S(2)}) %collective-permute-start.36) | collective-permute-done | bytes 524320 | tf_op jit(solution)/shard_map/ppermute | solution.py:322
  388.6 10.4 %finish.6 = f32[16,256,256]{2,1,0:T(8,128)} custom-call(s32[4]{0:T(128)} %copy-done.20, bf16[2,1,16,64,256]{4,3,2,1,0:T(8,128)(2,1)} %get-tuple-element.99.p_ref, bf16[2,1,16,64,256]{4,3,2,1,0:T(8,128)(2,1)} %bitcast.148), custom_call_target="tpu_custom_call" | custom-call | bytes 6291456 | tf_op jit(solution)/shard_map/finish/pallas_call | solution.py:268
  398.9 12.1 %collective-permute-done.31 = bf16[2,16,64,256]{3,2,1,0:T(8,128)(2,1)} collective-permute-done((bf16[2,16,64,256]{3,2,1,0:T(8,128)(2,1)}, bf16[2,16,64,256]{3,2,1,0:T(8,128)(2,1)}, u32[]{:S(2)}, u32[]{:S(2)}) %collective-permute-start.31) | collective-permute-done | bytes 1048608 | tf_op jit(solution)/shard_map/ppermute | solution.py:323
  411.0 10.4 %finish.5 = f32[16,256,256]{2,1,0:T(8,128)} custom-call(s32[4]{0:T(128)} %copy-done.19, bf16[2,1,16,64,256]{4,3,2,1,0:T(8,128)(2,1)} %get-tuple-element.101.p_ref, bf16[2,1,16,64,256]{4,3,2,1,0:T(8,128)(2,1)} %bitcast.62.q_ref), custom_call_target="tpu_custom_call" | custom-call | bytes 6291456 | tf_op jit(solution)/shard_map/finish/pallas_call | solution.py:268
  421.4 10.4 %finish.7 = f32[4,1024,256]{2,1,0:T(8,128)} custom-call(s32[4]{0:T(128)} %copy-done.20, bf16[2,4,4,64,256]{4,3,2,1,0:T(8,128)(2,1)} %copy-done.3, bf16[2,4,4,64,256]{4,3,2,1,0:T(8,128)(2,1)} %collective-permute-done.37.q_ref), custom_call_target="tpu_custom_call" | custom-call | bytes 6291456 | tf_op jit(solution)/shard_map/finish/pallas_call | solution.py:268
  431.8 11.0 %finish.4 = f32[4,256,1024]{2,1,0:T(8,128)} custom-call(s32[4]{0:T(128)} %copy-done.19, bf16[2,4,4,64,256]{4,3,2,1,0:T(8,128)(2,1)} %copy-done.4, bf16[2,4,4,64,256]{4,3,2,1,0:T(8,128)(2,1)} %collective-permute-done.27.q_ref), custom_call_target="tpu_custom_call" | custom-call | bytes 6291456 | tf_op jit(solution)/shard_map/finish/pallas_call | solution.py:268
  (175 shorter events, 157.6 us)
Async XLA Ops:
  5.0 50.5 %collective-permute-start.6 = (bf16[2,1024,512]{2,1,0:T(8,128)(2,1)S(1)}, bf16[2,1024,512]{2,1,0:T(8,128)(2,1)}, u32[]{:S(2)}, u32[]{:S(2)}) collective-permute-start(bf16[2,1024,512]{2,1,0:T(8,128)(2,1)S(1)} %pad_maximum_fusion.1.x_ref.refs_3_), channel_id=1, source_target_pairs={{0,2},{1,3},{2,4},{3,5},{4,6},{5,7},{8,10},{9,11},{10,12},{11,13},... | collective-permute-start | bytes 6291464 | tf_op jit(solution)/shard_map/ppermute | solution.py:374
  8.5 50.6 %collective-permute-start.4 = (bf16[2,1024,512]{2,1,0:T(8,128)(2,1)S(1)}, bf16[2,1024,512]{2,1,0:T(8,128)(2,1)}, u32[]{:S(2)}, u32[]{:S(2)}) collective-permute-start(bf16[2,1024,512]{2,1,0:T(8,128)(2,1)S(1)} %pad_maximum_fusion.1.x_ref.refs_3_), channel_id=1, source_target_pairs={{2,0},{3,1},{4,2},{5,3},{6,4},{7,5},{10,8},{11,9},{12,10},{13,11},... | collective-permute-start | bytes 6291464 | tf_op jit(solution)/shard_map/ppermute | solution.py:375
  17.2 62.4 %all-to-all-start = ((bf16[4,2,4,64,256]{4,3,2,1,0:T(8,128)(2,1)}), bf16[4,2,4,64,256]{4,3,2,1,0:T(8,128)(2,1)S(1)}, u32[]{:S(2)}, u32[]{:S(2)}) async-start(bf16[4,2,4,64,256]{4,3,2,1,0:T(8,128)(2,1)} %copy.52), calls=%async_computation | async-start | bytes 2097152 | tf_op jit(solution)/shard_map/all_to_all | solution.py:361
  55.5 66.3 %collective-permute-start.7 = (bf16[2,1024,512]{2,1,0:T(8,128)(2,1)}, bf16[2,1024,512]{2,1,0:T(8,128)(2,1)}, u32[]{:S(2)}, u32[]{:S(2)}) collective-permute-start(bf16[2,1024,512]{2,1,0:T(8,128)(2,1)} %collective-permute-done.6.x_ref.refs_3_), channel_id=1, source_target_pairs={{2,4},{3,5},{4,6},{5,7},{10,12},{11,13},{12,14},{13,15},{18,20},{1... | collective-permute-start | bytes 6291464 | tf_op jit(solution)/shard_map/ppermute | solution.py:374
  59.0 64.2 %collective-permute-start.5 = (bf16[2,1024,512]{2,1,0:T(8,128)(2,1)}, bf16[2,1024,512]{2,1,0:T(8,128)(2,1)}, u32[]{:S(2)}, u32[]{:S(2)}) collective-permute-start(bf16[2,1024,512]{2,1,0:T(8,128)(2,1)} %collective-permute-done.4.x_ref.refs_3_), channel_id=1, source_target_pairs={{2,0},{3,1},{4,2},{5,3},{10,8},{11,9},{12,10},{13,11},{18,16},{19,... | collective-permute-start | bytes 6291464 | tf_op jit(solution)/shard_map/ppermute | solution.py:375
  81.3 44.0 %collective-permute-start.2 = (bf16[4,4,64,256]{3,2,1,0:T(8,128)(2,1)S(1)}, bf16[4,4,64,256]{3,2,1,0:T(8,128)(2,1)S(1)}, u32[]{:S(2)}, u32[]{:S(2)}) collective-permute-start(bf16[4,4,64,256]{3,2,1,0:T(8,128)(2,1)S(1)} %get-tuple-element.105), channel_id=1, source_target_pairs={{0,8},{8,0},{16,24},{24,16},{1,9},{9,1},{17,25},{25,17},{2,10},{10... | collective-permute-start | bytes 1572872 | tf_op jit(solution)/shard_map/ppermute | solution.py:322
  92.0 55.9 %collective-permute-start.1 = (bf16[2,4,4,64,256]{4,3,2,1,0:T(8,128)(2,1)}, bf16[2,4,4,64,256]{4,3,2,1,0:T(8,128)(2,1)}, u32[]{:S(2)}, u32[]{:S(2)}) collective-permute-start(bf16[2,4,4,64,256]{4,3,2,1,0:T(8,128)(2,1)} %pad_maximum_fusion.6), channel_id=1, source_target_pairs={{0,8},{8,0},{16,24},{24,16},{1,9},{9,1},{17,25},{25,17},{2,10},{10... | collective-permute-start | bytes 3145736 | tf_op jit(solution)/shard_map/ppermute | solution.py:323
  121.8 54.7 %collective-permute-start.8 = (bf16[2,1024,512]{2,1,0:T(8,128)(2,1)}, bf16[2,1024,512]{2,1,0:T(8,128)(2,1)S(1)}, u32[]{:S(2)}, u32[]{:S(2)}) collective-permute-start(bf16[2,1024,512]{2,1,0:T(8,128)(2,1)} %collective-permute-done.7), channel_id=1, source_target_pairs={{4,6},{5,7},{12,14},{13,15},{20,22},{21,23},{28,30},{29,31}} | collective-permute-start | bytes 6291464 | tf_op jit(solution)/shard_map/ppermute | solution.py:374
  123.3 53.8 %collective-permute-start.9 = (bf16[2,1024,512]{2,1,0:T(8,128)(2,1)}, bf16[2,1024,512]{2,1,0:T(8,128)(2,1)}, u32[]{:S(2)}, u32[]{:S(2)}) collective-permute-start(bf16[2,1024,512]{2,1,0:T(8,128)(2,1)} %collective-permute-done.5), channel_id=1, source_target_pairs={{2,0},{3,1},{10,8},{11,9},{18,16},{19,17},{26,24},{27,25}} | collective-permute-start | bytes 6291464 | tf_op jit(solution)/shard_map/ppermute | solution.py:375
  213.5 34.7 %collective-permute-start.32 = (bf16[2,16,64,256]{3,2,1,0:T(8,128)(2,1)}, bf16[2,16,64,256]{3,2,1,0:T(8,128)(2,1)S(1)}, u32[]{:S(2)}, u32[]{:S(2)}) collective-permute-start(bf16[2,16,64,256]{3,2,1,0:T(8,128)(2,1)} %slice.116), channel_id=1, source_target_pairs={{0,16},{8,24},{16,0},{24,8},{1,17},{9,25},{17,1},{25,9},{2,18},{10... | collective-permute-start | bytes 3145736 | tf_op jit(solution)/shard_map/ppermute | solution.py:314
  243.7 49.3 %collective-permute-start.19 = (bf16[2,1024,512]{2,1,0:T(8,128)(2,1)S(1)}, bf16[2,1024,512]{2,1,0:T(8,128)(2,1)S(1)}, u32[]{:S(2)}, u32[]{:S(2)}) collective-permute-start(bf16[2,1024,512]{2,1,0:T(8,128)(2,1)S(1)} %copy-done.7), channel_id=1, source_target_pairs={{6,4},{7,5},{14,12},{15,13},{22,20},{23,21},{30,28},{31,29}} | collective-permute-start | bytes 6291464 | tf_op jit(solution)/shard_map/ppermute | solution.py:300
  245.0 48.5 %collective-permute-start.16 = (bf16[2,1024,512]{2,1,0:T(8,128)(2,1)S(1)}, bf16[2,1024,512]{2,1,0:T(8,128)(2,1)S(1)}, u32[]{:S(2)}, u32[]{:S(2)}) collective-permute-start(bf16[2,1024,512]{2,1,0:T(8,128)(2,1)S(1)} %copy-done.5), channel_id=1, source_target_pairs={{0,2},{1,3},{8,10},{9,11},{16,18},{17,19},{24,26},{25,27}} | collective-permute-start | bytes 6291464 | tf_op jit(solution)/shard_map/ppermute | solution.py:299
  247.5 50.3 %collective-permute-start.28 = (bf16[2,16,64,256]{3,2,1,0:T(8,128)(2,1)S(1)}, bf16[2,16,64,256]{3,2,1,0:T(8,128)(2,1)S(1)}, u32[]{:S(2)}, u32[]{:S(2)}) collective-permute-start(bf16[2,16,64,256]{3,2,1,0:T(8,128)(2,1)S(1)} %slice.112), channel_id=1, source_target_pairs={{0,8},{8,0},{16,24},{24,16},{1,9},{9,1},{17,25},{25,17},{2,10},{10... | collective-permute-start | bytes 3145736 | tf_op jit(solution)/shard_map/ppermute | solution.py:314
  268.2 50.7 %collective-permute-start.33 = (bf16[16,64,256]{2,1,0:T(8,128)(2,1)}, bf16[16,64,256]{2,1,0:T(8,128)(2,1)}, u32[]{:S(2)}, u32[]{:S(2)}) collective-permute-start(bf16[16,64,256]{2,1,0:T(8,128)(2,1)} %slice_bitcast_fusion.2), channel_id=1, source_target_pairs={{0,8},{8,0},{16,24},{24,16},{1,9},{9,1},{17,25},{25,17},{2,10},{10... | collective-permute-start | bytes 1572872 | tf_op jit(solution)/shard_map/ppermute | solution.py:315
  273.8 30.7 %collective-permute-start.23 = (bf16[4,4,64,256]{3,2,1,0:T(8,128)(2,1)S(1)}, bf16[4,4,64,256]{3,2,1,0:T(8,128)(2,1)S(1)}, u32[]{:S(2)}, u32[]{:S(2)}) collective-permute-start(bf16[4,4,64,256]{3,2,1,0:T(8,128)(2,1)S(1)} %slice_bitcast_fusion.8), channel_id=1, source_target_pairs={{0,16},{8,24},{16,0},{24,8},{1,17},{9,25},{17,1},{25,9},{2,18},{10... | collective-permute-start | bytes 1572872 | tf_op jit(solution)/shard_map/ppermute | solution.py:315
  296.6 51.6 %collective-permute-start.17 = (bf16[2,1024,512]{2,1,0:T(8,128)(2,1)}, bf16[2,1024,512]{2,1,0:T(8,128)(2,1)}, u32[]{:S(2)}, u32[]{:S(2)}) collective-permute-start(bf16[2,1024,512]{2,1,0:T(8,128)(2,1)} %get-tuple-element.84), channel_id=1, source_target_pairs={{0,2},{1,3},{2,4},{3,5},{8,10},{9,11},{10,12},{11,13},{16,18},{17,... | collective-permute-start | bytes 6291464 | tf_op jit(solution)/shard_map/ppermute | solution.py:299
  298.3 57.7 %collective-permute-start.20 = (bf16[2,1024,512]{2,1,0:T(8,128)(2,1)}, bf16[2,1024,512]{2,1,0:T(8,128)(2,1)}, u32[]{:S(2)}, u32[]{:S(2)}) collective-permute-start(bf16[2,1024,512]{2,1,0:T(8,128)(2,1)} %get-tuple-element.85), channel_id=1, source_target_pairs={{4,2},{5,3},{6,4},{7,5},{12,10},{13,11},{14,12},{15,13},{20,18},{2... | collective-permute-start | bytes 6291464 | tf_op jit(solution)/shard_map/ppermute | solution.py:300
  313.7 58.9 %all-to-all-start.1 = ((bf16[4,2,4,64,256]{4,3,2,1,0:T(8,128)(2,1)}), bf16[4,2,4,64,256]{4,3,2,1,0:T(8,128)(2,1)S(1)}, u32[]{:S(2)}, u32[]{:S(2)}) async-start(bf16[4,2,4,64,256]{4,3,2,1,0:T(8,128)(2,1)} %copy.57), calls=%async_computation.1 | async-start | bytes 2097152 | tf_op jit(solution)/shard_map/all_to_all | solution.py:415
  322.9 50.6 %collective-permute-start.30 = (bf16[16,64,256]{2,1,0:T(8,128)(2,1)S(1)}, bf16[16,64,256]{2,1,0:T(8,128)(2,1)S(1)}, u32[]{:S(2)}, u32[]{:S(2)}) collective-permute-start(bf16[16,64,256]{2,1,0:T(8,128)(2,1)S(1)} %fusion.5), channel_id=1, source_target_pairs={{0,16},{8,24},{16,0},{24,8},{1,17},{9,25},{17,1},{25,9},{2,18},{10... | collective-permute-start | bytes 1572872 | tf_op jit(solution)/shard_map/ppermute | solution.py:322
  334.4 52.6 %collective-permute-start.35 = (bf16[2,16,64,256]{3,2,1,0:T(8,128)(2,1)}, bf16[2,16,64,256]{3,2,1,0:T(8,128)(2,1)S(1)}, u32[]{:S(2)}, u32[]{:S(2)}) collective-permute-start(bf16[2,16,64,256]{3,2,1,0:T(8,128)(2,1)} %get-tuple-element.98), channel_id=1, source_target_pairs={{0,16},{8,24},{16,0},{24,8},{1,17},{9,25},{17,1},{25,9},{2,18},{10... | collective-permute-start | bytes 3145736 | tf_op jit(solution)/shard_map/ppermute | solution.py:323
  351.7 91.1 %collective-permute-start.18 = (bf16[2,1024,512]{2,1,0:T(8,128)(2,1)}, bf16[2,1024,512]{2,1,0:T(8,128)(2,1)}, u32[]{:S(2)}, u32[]{:S(2)}) collective-permute-start(bf16[2,1024,512]{2,1,0:T(8,128)(2,1)} %add_convert_fusion.2), channel_id=1, source_target_pairs={{0,2},{1,3},{2,4},{3,5},{4,6},{5,7},{8,10},{9,11},{10,12},{11,13},... | collective-permute-start | bytes 6291464 | tf_op jit(solution)/shard_map/ppermute | solution.py:299
  359.4 83.3 %collective-permute-start.21 = (bf16[2,1024,512]{2,1,0:T(8,128)(2,1)}, bf16[2,1024,512]{2,1,0:T(8,128)(2,1)}, u32[]{:S(2)}, u32[]{:S(2)}) collective-permute-start(bf16[2,1024,512]{2,1,0:T(8,128)(2,1)} %add_convert_fusion.1), channel_id=1, source_target_pairs={{2,0},{3,1},{4,2},{5,3},{6,4},{7,5},{10,8},{11,9},{12,10},{13,11},... | collective-permute-start | bytes 6291464 | tf_op jit(solution)/shard_map/ppermute | solution.py:300
  385.3 36.1 %collective-permute-start.37 = (bf16[2,4,4,64,256]{4,3,2,1,0:T(8,128)(2,1)S(1)}, bf16[2,4,4,64,256]{4,3,2,1,0:T(8,128)(2,1)}, u32[]{:S(2)}, u32[]{:S(2)}) collective-permute-start(bf16[2,4,4,64,256]{4,3,2,1,0:T(8,128)(2,1)S(1)} %pad_maximum_fusion.12.p_ref), channel_id=1, source_target_pairs={{0,16},{8,24},{16,0},{24,8},{1,17},{9,25},{17,1},{25,9},{2,18},{10... | collective-permute-start | bytes 3145736 | tf_op jit(solution)/shard_map/ppermute | solution.py:323
  387.0 44.7 %collective-permute-start.27 = (bf16[2,4,4,64,256]{4,3,2,1,0:T(8,128)(2,1)S(1)}, bf16[2,4,4,64,256]{4,3,2,1,0:T(8,128)(2,1)}, u32[]{:S(2)}, u32[]{:S(2)}) collective-permute-start(bf16[2,4,4,64,256]{4,3,2,1,0:T(8,128)(2,1)S(1)} %pad_maximum_fusion.9.p_ref), channel_id=1, source_target_pairs={{0,8},{8,0},{16,24},{24,16},{1,9},{9,1},{17,25},{25,17},{2,10},{10... | collective-permute-start | bytes 3145736 | tf_op jit(solution)/shard_map/ppermute | solution.py:323
  (39 other events, 595.2 us)

commit v3 on v2

v3 whole, which is shorter than its diff:
```python
import functools
import math

import jax
import jax.numpy as jnp
from jax import lax
from jax.experimental import pallas as pl
from jax.experimental.pallas import tpu as pltpu
from jax.sharding import PartitionSpec as P

F32 = jnp.float32
BF16 = jnp.bfloat16
PARAMS = pltpu.CompilerParams(dimension_semantics=("arbitrary",))


def gelu_parts(value_in):
    cdf_part = 0.5 * (1.0 + lax.erf(value_in * 0.7071067811865476))
    slope_part = cdf_part + value_in * jnp.exp(-0.5 * value_in * value_in) * 0.3989422804014327
    return (value_in * cdf_part, slope_part)


def dot(a, b, ca, cb):
    return lax.dot_general(a, b, (((ca,), (cb,)), ((), ())), preferred_element_type=F32)


def cost(flops, elements, trans=0):
    return pl.CostEstimate(flops=flops, bytes_accessed=2 * elements, transcendentals=trans)


def expand_kernel(meta, *refs, pa, bw, hd, sub):
    x_refs, (w_ref, own_ref, send_ref) = refs[:-3], refs[-3:]
    low = meta[1] == 0
    m = hd * sub
    for e in range(2):
        own, send = [], []
        for a in range(pa):
            x = total(x_refs, e, slice(a * bw, (a + 1) * bw))
            val = dot(w_ref[e, 0, a], x, 1, 0)
            first = val[:m].reshape(hd, sub, val.shape[-1])
            second = val[m:].reshape(hd, sub, val.shape[-1])
            own.append(jnp.where(low, first, second))
            send.append(jnp.where(low, second, first))
        own_ref[e] = jnp.concatenate(own, axis=1).astype(BF16)
        send_ref[e] = jnp.concatenate(send, axis=1).astype(BF16)


def total(refs, e, span):
    val = refs[0][e, span, :]
    for ref in refs[1:]:
        val = val + ref[e, span, :]
    return val


def expand(meta, xgs, w14, hd, sub):
    _, nl, wd, m2, bw = w14.shape
    rows = xgs[0].shape[-1]
    pa = min(wd, 2)
    out = jax.ShapeDtypeStruct((2, hd, wd * sub, rows), BF16)
    out_spec = pl.BlockSpec((2, hd, pa * sub, rows), lambda s, meta: (0, 0, s, 0))
    return pl.pallas_call(
        functools.partial(expand_kernel, pa=pa, bw=bw, hd=hd, sub=sub),
        grid_spec=pltpu.PrefetchScalarGridSpec(
            num_scalar_prefetch=1,
            grid=(wd // pa,),
            in_specs=[pl.BlockSpec((2, pa * bw, rows), lambda s, meta: (0, s, 0))] * len(xgs)
            + [pl.BlockSpec((2, 1, pa, m2, bw), lambda s, meta: (0, meta[0], s, 0, 0))],
            out_specs=[out_spec, out_spec],
        ),
        out_shape=[out, out],
        compiler_params=PARAMS,
        cost_estimate=cost(4 * wd * m2 * bw * rows, 2 * wd * (bw * rows + m2 * bw + m2 * rows)),
        name="expand",
    )(meta, *xgs, w14)


def put_shares(meta, first, gsc, val, keep_ref, send_ref, index, dp):
    gsc[...] = val
    step = val.shape[0] // dp
    half = dp // 2
    for p in range(dp):
        row = pl.multiple_of(meta[first + p] * step, step)
        ref = keep_ref if p < half else send_ref
        ref[(p % half, *index)] = gsc[pl.ds(row, step), :].astype(BF16)


def middle_kernel(meta, *refs, nl, part, hb, dp, scale):
    slots = nl + 1
    owns, recvs = refs[:slots], refs[slots : 2 * slots]
    (w2_ref, w3_ref, own_ref, send_ref, g2k_ref, g2s_ref, g3k_ref, g3s_ref, ysc, gsc) = refs[2 * slots :]
    pos, core = meta[0], meta[1]

    for b in range(hb):

        def place(k, where):
            base = pl.multiple_of((where * 2 + core) * part, part)
            other = pl.multiple_of((where * 2 + 1 - core) * part, part)
            for e in range(2):
                ysc[b, e, pl.ds(base, part), :] = owns[k][e, b].astype(F32)
                ysc[b, e, pl.ds(other, part), :] = recvs[k][e, b].astype(F32)

        for k in range(nl):
            place(k, lax.rem(pos + k, nl))

        @pl.when(meta[2] >= 0)
        def _():
            place(nl, meta[2])

    for b in range(hb):
        yb = ysc[b, 0].astype(BF16)
        dzb = ysc[b, 1].astype(BF16)
        w2 = w2_ref[b]
        w3 = w3_ref[b]
        pre = dot(w2, yb, 0, 0)
        dact = dot(w3, dzb, 1, 0)
        val, slope = gelu_parts(pre)
        act = val.astype(BF16)
        dpre = (dact * slope).astype(BF16)
        put_shares(meta, 4, gsc.at[b, 0], dot(yb, dpre, 1, 1) * scale, g2k_ref, g2s_ref, (b,), dp)
        put_shares(meta, 4 + dp, gsc.at[b, 1], dot(act, dzb, 1, 1) * scale, g3k_ref, g3s_ref, (b,), dp)
        ysc[b, 0] = dot(w3, act, 0, 0)
        ysc[b, 1] = dot(w2, dpre, 1, 0)
        for k in range(nl):
            for e in range(2):
                base = pl.multiple_of((k * 2 + core) * part, part)
                other = pl.multiple_of((k * 2 + 1 - core) * part, part)
                own_ref[e, b, k * part : (k + 1) * part] = ysc[b, e, pl.ds(base, part), :].astype(BF16)
                send_ref[e, b, k * part : (k + 1) * part] = ysc[b, e, pl.ds(other, part), :].astype(BF16)


def middle(meta, owns, recvs, w2, w3, dp, scale):
    hd, k, j = w2.shape
    nl = len(owns) - 1
    _, _, part, rows = owns[0].shape
    hb = 2
    half = dp // 2
    slot = pl.BlockSpec((2, hb, part, rows), lambda b, meta: (0, b, 0, 0))
    full = pl.BlockSpec((2, hb, nl * part, rows), lambda b, meta: (0, b, 0, 0))
    wspec = pl.BlockSpec((hb, k, j), lambda b, meta: (b, 0, 0))
    gspec = pl.BlockSpec((half, hb, k // dp, j), lambda b, meta: (0, b, 0, 0))
    zout = jax.ShapeDtypeStruct((2, hd, nl * part, rows), BF16)
    gout = jax.ShapeDtypeStruct((half, hd, k // dp, j), BF16)
    return pl.pallas_call(
        functools.partial(middle_kernel, nl=nl, part=part, hb=hb, dp=dp, scale=scale),
        grid_spec=pltpu.PrefetchScalarGridSpec(
            num_scalar_prefetch=1,
            grid=(hd // hb,),
            in_specs=[slot] * (2 * nl + 2) + [wspec, wspec],
            out_specs=[full, full, gspec, gspec, gspec, gspec],
            scratch_shapes=[pltpu.VMEM((hb, 2, k, rows), F32), pltpu.VMEM((hb, 2, k, j), F32)],
        ),
        out_shape=[zout, zout, gout, gout, gout, gout],
        compiler_params=PARAMS,
        cost_estimate=cost(
            12 * hd * k * j * rows, 4 * hd * k * rows + 4 * hd * k * j, 2 * hd * j * rows
        ),
        name="middle",
    )(meta, *owns, *recvs, w2, w3)


def contract_kernel(meta, *refs, nx, late, chain, pa, bw, hd, sub, dp, scale):
    refs = list(refs)
    zo_ref, zr_ref, w_ref = refs[:3]
    x_refs = refs[3 : 3 + nx]
    refs = refs[3 + nx + (4 if chain else 0) :]
    part_ref, g1k_ref, g1s_ref, g4k_ref, g4s_ref, zsc, gsc = refs
    core = meta[1]
    rows = zo_ref.shape[-1]
    m = hd * sub
    mine = pl.multiple_of(core * m, m)
    other = pl.multiple_of((1 - core) * m, m)
    for e in range(2):
        for ref, base in ((zo_ref, mine), (zr_ref, other)):
            chunk = ref[e].astype(F32)
            for a in range(pa):
                piece = chunk[:, a * sub : (a + 1) * sub, :].reshape(m, rows)
                zsc[e, a, pl.ds(base, m), :] = piece.astype(BF16)
    for a in range(pa):
        span = slice(a * bw, (a + 1) * bw)
        z, dy = zsc[0, a], zsc[1, a]
        if late:
            take = meta[3] > 0
            x, g = (jnp.where(take, x_refs[1][e, span, :], x_refs[0][e, span, :]) for e in range(2))
        else:
            x, g = (total(x_refs, e, span) for e in range(2))
        put_shares(meta, 4, gsc.at[a, 0], dot(dy, x, 1, 1) * scale, g1k_ref, g1s_ref, (0, a), dp)
        put_shares(meta, 4 + dp, gsc.at[a, 1], dot(z, g, 1, 1) * scale, g4k_ref, g4s_ref, (0, a), dp)
        part_ref[0, span, :] = dot(w_ref[1, 0, a], z, 0, 0).astype(BF16)
        part_ref[1, span, :] = dot(w_ref[0, 0, a], dy, 0, 0).astype(BF16)


def contract(meta, z_own, z_recv, w14, xgs, late, grads, sub, dp, scale):
    _, nl, wd, m2, bw = w14.shape
    hd, rows = z_own.shape[1], z_own.shape[-1]
    pa = min(wd, 2)
    steps = wd // pa
    half = dp // 2
    zspec = pl.BlockSpec((2, hd, pa * sub, rows), lambda s, meta: (0, 0, meta[0] * steps + s, 0))
    xspec = pl.BlockSpec((2, pa * bw, rows), lambda s, meta: (0, s, 0))
    wspec = pl.BlockSpec((2, 1, pa, m2, bw), lambda s, meta: (0, meta[0], s, 0, 0))
    gspec = pl.BlockSpec((half, 1, pa, m2 // dp, bw), lambda s, meta: (0, meta[0], s, 0, 0))
    gout = jax.ShapeDtypeStruct((half, nl, wd, m2 // dp, bw), BF16)
    args = [meta, z_own, z_recv, w14, *xgs]
    specs = [zspec, zspec, wspec] + [xspec] * len(xgs)
    aliases = {}
    if grads is not None:
        aliases = {len(args) + i: 1 + i for i in range(4)}
        args += list(grads)
        specs += [pl.BlockSpec(memory_space=pl.ANY)] * 4
    return pl.pallas_call(
        functools.partial(
            contract_kernel,
            nx=len(xgs),
            late=late,
            chain=grads is not None,
            pa=pa,
            bw=bw,
            hd=hd,
            sub=sub,
            dp=dp,
            scale=scale,
        ),
        grid_spec=pltpu.PrefetchScalarGridSpec(
            num_scalar_prefetch=1,
            grid=(steps,),
            in_specs=specs,
            out_specs=[xspec, gspec, gspec, gspec, gspec],
            scratch_shapes=[pltpu.VMEM((2, pa, m2, rows), BF16), pltpu.VMEM((pa, 2, m2, bw), F32)],
        ),
        out_shape=[jax.ShapeDtypeStruct(xgs[0].shape, BF16), gout, gout, gout, gout],
        input_output_aliases=aliases,
        compiler_params=PARAMS,
        cost_estimate=cost(
            8 * wd * m2 * bw * rows, 2 * wd * (2 * bw * rows + m2 * rows + 2 * m2 * bw)
        ),
        name="contract",
    )(*args)


def finish_kernel(tab, p_ref, q_ref, o_ref, *, dp, flip):
    half = dp // 2
    count = o_ref.shape[0]
    for a in range(count):
        vals = []
        for q in range(dp):
            slot = tab[q]
            inner = lax.rem(slot, half)
            vals.append(jnp.where(slot < half, p_ref[inner, 0, a], q_ref[inner, 0, a]).astype(F32))
        if flip:
            o_ref[a] = jnp.concatenate(vals, axis=0).T
        else:
            step = vals[0].shape[0]
            for q in range(dp):
                o_ref[a, q * step : (q + 1) * step, :] = vals[q]


def finish(tab, halves, flip):
    p, q = halves
    half, outer, wd, step, bw = p.shape
    dp = 2 * half
    size = dp * step
    count = min(wd, 4)
    spec = pl.BlockSpec((half, 1, count, step, bw), lambda o, a, tab: (0, o, a, 0, 0))
    if flip:
        if size % 128:
            merged = jnp.concatenate([p, q], axis=0)[tab]
            return jnp.transpose(merged, (2, 4, 1, 0, 3)).reshape(wd, bw, outer * size).astype(F32)
        shape = (wd, bw, outer * size)
        ospec = pl.BlockSpec((count, bw, size), lambda o, a, tab: (a, 0, o))
    else:
        shape = (wd, outer * size, bw)
        ospec = pl.BlockSpec((count, size, bw), lambda o, a, tab: (a, o, 0))
    return pl.pallas_call(
        functools.partial(finish_kernel, dp=dp, flip=flip),
        grid_spec=pltpu.PrefetchScalarGridSpec(
            num_scalar_prefetch=1,
            grid=(outer, wd // count),
            in_specs=[spec, spec],
            out_specs=ospec,
        ),
        out_shape=jax.ShapeDtypeStruct(shape, F32),
        compiler_params=pltpu.CompilerParams(dimension_semantics=("arbitrary", "arbitrary")),
        cost_estimate=cost(0, 3 * wd * outer * size * bw),
        name="finish",
    )(tab, p, q)


def up_pairs(lo, hi):
    return [(2 * p + c, 2 * p + 2 + c) for p in range(lo, hi) for c in range(2)]


def down_pairs(lo, hi):
    return [(2 * p + 2 + c, 2 * p + c) for p in range(lo, hi) for c in range(2)]


def swap(val, n):
    return lax.ppermute(val, "tensor", [(i, i ^ 1) for i in range(n)])


def add(a, b):
    return (a.astype(F32) + b.astype(F32)).astype(BF16)


def line_scatter(parts, nl):
    up, down = parts[nl - 1], parts[1]
    for r in range(1, nl):
        up = lax.ppermute(up, "tensor", up_pairs(0, r))
        down = lax.ppermute(down, "tensor", down_pairs(nl - 1 - r, nl - 1))
        if r < nl - 1:
            up = add(up, parts[nl - 1 - r])
            down = add(down, parts[r + 1])
    return (parts[0].astype(F32) + up.astype(F32) + down.astype(F32)).astype(BF16)


X_PAIRS = [(i, i ^ 1) for i in range(4)]
Y_PAIRS = [(i, i ^ 2) for i in range(4)]


def reduce_dp(keep, send, dp, pairs):
    if dp != 4:
        return lax.psum_scatter(jnp.concatenate([keep, send]), "dp")
    came = lax.ppermute(send, "dp", pairs[0])
    second = lax.ppermute(add(keep[1], came[1]), "dp", pairs[1])
    return (keep[0].astype(F32) + came[0].astype(F32) + second.astype(F32)).astype(BF16)


def gather_dp(val, dp, pairs):
    if dp != 4:
        every = lax.all_gather(val, "dp")
        return every[: dp // 2], every[dp // 2 :]
    low = jnp.stack([val, lax.ppermute(val, "dp", pairs[1])])
    return low, lax.ppermute(low, "dp", pairs[0])


def body(tokens, cotangent, w_first, w_second, w_third, w_fourth):
    rows = tokens.shape[0]
    wd, bw, _ = w_first.shape
    hd = w_second.shape[0]
    n = lax.axis_size("tensor")
    dp = lax.axis_size("dp")
    nl = n // 2
    sub = bw // (wd * n)
    m2 = 2 * hd * sub
    step = m2 // dp
    scale = 1.0 / math.sqrt(rows * dp)
    me = lax.axis_index("tensor")
    mine = lax.axis_index("dp")
    pos, core = me // 2, me % 2
    lines = [[2 * p + c for p in range(nl)] for c in range(2)]
    x_first, y_first = (X_PAIRS, Y_PAIRS), (Y_PAIRS, X_PAIRS)

    dps = jnp.arange(dp, dtype=jnp.int32)
    if dp == 4:
        tab_y = dps ^ mine
        tab_x = ((tab_y & 1) << 1) | (tab_y >> 1)
        inv_x = (((dps & 1) << 1) | (dps >> 1)) ^ mine
        inv_y = tab_y
    else:
        tab_x = tab_y = inv_x = inv_y = dps
    low_end, high_end = pos == 0, pos == nl - 1
    late_pos = jnp.where(low_end, nl - 1, jnp.where(high_end, 0, -1))

    def meta_of(head, late):
        head = jnp.stack([jnp.asarray(v, jnp.int32) for v in (head, core, late_pos, late)])
        return jnp.concatenate([head, inv_x, inv_y])

    w1 = lax.dynamic_index_in_dim(
        w_first.reshape(wd, bw, nl, dp, step), mine, axis=3, keepdims=False
    )
    w4 = lax.dynamic_index_in_dim(
        w_fourth.reshape(wd, nl, dp, step, bw), mine, axis=2, keepdims=False
    )
    w14 = jnp.stack([jnp.transpose(w1, (2, 0, 3, 1)), jnp.transpose(w4, (1, 0, 2, 3))], axis=1)
    w14 = lax.all_to_all(
        w14, "tensor", split_axis=0, concat_axis=0, axis_index_groups=lines, tiled=True
    )
    own, w14 = lax.optimization_barrier((jnp.stack([tokens.T, cotangent.T]), w14))
    ups, downs = [own], [own]
    for r in range(1, nl):
        ups.append(lax.ppermute(ups[-1], "tensor", up_pairs(r - 1, nl - 1)))
        downs.append(lax.ppermute(downs[-1], "tensor", down_pairs(0, nl - r)))
    sides = []
    for e, (pairs, tab) in enumerate(((x_first, tab_x), (y_first, tab_y))):
        every = jnp.concatenate(gather_dp(w14[:, e], dp, pairs))
        every = [lax.dynamic_index_in_dim(every, tab[q], keepdims=False) for q in range(dp)]
        sides.append(jnp.stack(every, axis=2).reshape(nl, wd, m2, bw))
    w14 = jnp.stack(sides)
    slots = [[own], [downs[1]]]
    slots += [[downs[k], ups[nl - k]] for k in range(2, nl - 1)]
    slots += [[ups[1]]]
    late = [ups[nl - 1], downs[nl - 1]]
    metas = [meta_of((pos + k) % nl, 0) for k in range(nl)]
    metas[1] = meta_of((pos + 1) % nl, high_end)
    metas[nl - 1] = meta_of((pos + nl - 1) % nl, low_end)
    late_meta = meta_of(jnp.maximum(late_pos, 0), 0)

    owns, recvs = [], []
    for meta, xg in zip(metas + [late_meta], slots + [late]):
        mine_part, send = expand(meta, xg, w14, hd, sub)
        owns.append(mine_part)
        recvs.append(swap(send, n))
    z_own, z_send, *g23 = middle(
        meta_of(pos, 0), owns, recvs, w_second, w_third, dp, scale
    )
    z_recv = swap(z_send, n)

    parts, grads = [None] * nl, None
    order = [k for pair in zip(range(nl - 1, nl // 2, -1), range(1, nl // 2)) for k in pair]
    for k in order + [nl // 2, 0]:
        xgs = slots[k]
        if k in (1, nl - 1):
            xgs = xgs + [late[0] if k == 1 else late[1]]
        parts[k], *grads = contract(
            metas[k], z_own, z_recv, w14, xgs, k in (1, nl - 1), grads, sub, dp, scale
        )
    both = line_scatter(parts, nl)

    g2 = gather_dp(reduce_dp(*g23[:2], dp, x_first), dp, x_first)
    g3 = gather_dp(reduce_dp(*g23[2:], dp, y_first), dp, y_first)
    g1 = reduce_dp(*grads[:2], dp, x_first)
    g4 = reduce_dp(*grads[2:], dp, y_first)
    g14 = jnp.stack([g1, g4], axis=1)
    g14 = lax.all_to_all(
        g14, "tensor", split_axis=0, concat_axis=0, axis_index_groups=lines, tiled=True
    )
    g1 = gather_dp(g14[:, 0], dp, x_first)
    g4 = gather_dp(g14[:, 1], dp, y_first)

    def single(halves):
        return [h[:, None] for h in halves]

    return (
        both[0].T,
        both[1].T,
        finish(tab_x, g1, True),
        finish(tab_x, single(g2), False),
        finish(tab_y, single(g3), False),
        finish(tab_y, g4, False),
    )


def solution(mesh):
    return jax.shard_map(
        body,
        mesh=mesh,
        in_specs=(
            P("dp", "tensor"),
            P("dp", "tensor"),
            P("tensor", None, None),
            P("tensor", None, None),
            P("tensor", None, None),
            P("tensor", None, None),
        ),
        out_specs=(
            P("dp", "tensor"),
            P("dp", "tensor"),
            P("tensor", None, None),
            P("tensor", None, None),
            P("tensor", None, None),
            P("tensor", None, None),
        ),
        check_vma=False,
    )
```

time: 457 us -> 444 us (0.972)
  Pallas kernels: 107 us -> 82.5 us
  waiting for transfers between devices: 181 us -> 193 us
  starting transfers between devices: 76.7 us -> 82.2 us
    pallas_call x9, Pallas kernels: 86.8 us -> 61.4 us  [the longest x4 23 us: contract(): pl.pallas_call(functools.partial(contract_kernel, nx=len(xgs), late=late,...]
    ppermute x8, waiting for transfers between devices: 25 us -> 38.2 us  [the longest x4 24.5 us: reduce_dp(): came = lax.ppermute(send, 'dp', pairs[0])]
    ppermute x3, waiting for transfers between devices: 19.6 us -> 6.85 us  [line_scatter(): down = lax.ppermute(down, 'tensor', down_pairs(nl - 1 - r, nl - 1))]
    ppermute x3, waiting for transfers between devices: 12.2 us -> 0.01 us  [line_scatter(): up = lax.ppermute(up, 'tensor', up_pairs(0, r))]
    ppermute x6, waiting for transfers between devices: 13.6 us -> 23.1 us  [gather_dp(): return (low, lax.ppermute(low, 'dp', pairs[0]))]
    add x2 -> x0, other arithmetic: 7.74 us -> none  [the longest x1 4.25 us: body(): slots.append(downs[k] + ups[nl - k])]
    all_to_all x1, waiting for transfers between devices: 12.2 us -> 18.1 us  [body(): lax.all_to_all(w14, 'tensor', split_axis=0, concat_axis=0, axis_index_gro...]
    ppermute x3, waiting for transfers between devices: 60.2 us -> 65.9 us  [body(): ups.append(lax.ppermute(ups[-1], 'tensor', up_pairs(r - 1, nl - 1)))]
  transfers between devices with their start and end apart: 40 -> 40, of which waited for: 17 -> 18; matrix products, arithmetic and copies ran while one was open for 12% -> 10% of each run, Pallas kernels for 19% -> 12%
where the time goes in v3:
time: 444 us; the launch traced here: 437 us
  waiting for transfers between devices  193 us (43%)
  Pallas kernels  82.5 us (19%)
  starting transfers between devices  82.2 us (19%)
  other arithmetic  38.1 us (9%)
  local copies, waits for them, and re-layouts  26.2 us (6%)
  between operations  15.3 us (3%)
    ppermute x3, waiting for transfers between devices, body(): ups.append(lax.ppermute(ups[-1], 'tensor', up_pairs(r - 1, nl - 1)))  65.9 us
    ppermute x4, waiting for transfers between devices, reduce_dp(): came = lax.ppermute(send, 'dp', pairs[0])  24.5 us
    ppermute x6, waiting for transfers between devices, gather_dp(): low = jnp.stack([val, lax.ppermute(val, 'dp', pairs[1])])  23.7 us
    ppermute x6, waiting for transfers between devices, gather_dp(): return (low, lax.ppermute(low, 'dp', pairs[0]))  23.1 us
    pallas_call x4, Pallas kernels, contract(): pl.pallas_call(functools.partial(contract_kernel, nx=len(xgs), late=late,...  23 us
    pallas_call x5, Pallas kernels, expand(): pl.pallas_call(functools.partial(expand_kernel, pa=pa, bw=bw, hd=hd, sub=...  21.1 us
    pallas_call x4, Pallas kernels, finish(): pl.pallas_call(functools.partial(finish_kernel, dp=dp, flip=flip), grid_s...  19.7 us
    pallas_call x1, Pallas kernels, middle(): pl.pallas_call(functools.partial(middle_kernel, nl=nl, part=part, hb=hb,...  18.6 us
  transfers between devices with their start and end apart: 40, of which 18 were waited for; matrix products, arithmetic and copies ran while one was open for 10% of the time, Pallas kernels for 12%

profile of v3, /device:TPU:16, one launch (start us, length us, event | category | flops | bytes accessed | tf_op | source)
XLA Modules:
  0.0 437.4 jit_solution(13849692007020808863)
XLA Ops:
  7.1 5.3 %all-to-all-start = ((bf16[4,2,4,64,256]{4,3,2,1,0:T(8,128)(2,1)}), bf16[4,2,4,64,256]{4,3,2,1,0:T(8,128)(2,1)S(1)}, u32[]{:S(2)}, u32[]{:S(2)}) async-start(bf16[4,2,4,64,256]{4,3,2,1,0:T(8,128)(2,1)} %copy.57), calls=%async_computation | async-start | bytes 2097152 | tf_op jit(solution)/shard_map/all_to_all | solution.py:373
  16.8 18.1 %all-to-all-done = bf16[4,2,4,64,256]{4,3,2,1,0:T(8,128)(2,1)S(1)} async-done(((bf16[4,2,4,64,256]{4,3,2,1,0:T(8,128)(2,1)}), bf16[4,2,4,64,256]{4,3,2,1,0:T(8,128)(2,1)S(1)}, u32[]{:S(2)}, u32[]{:S(2)}) %all-to-all-start) | async-done | bytes 1048608 | tf_op jit(solution)/shard_map/all_to_all | solution.py:373
  41.1 42.3 %collective-permute-done.6.refs_0_.refs_3_ = bf16[2,1024,512]{2,1,0:T(8,128)(2,1)S(1)} collective-permute-done((bf16[2,1024,512]{2,1,0:T(8,128)(2,1)S(1)}, bf16[2,1024,512]{2,1,0:T(8,128)(2,1)S(1)}, u32[]{:S(2)}, u32[]{:S(2)}) %collective-permute-start.6) | collective-permute-done | bytes 2097184 | tf_op jit(solution)/shard_map/ppermute | solution.py:379
  96.3 8.4 %collective-permute-done = bf16[4,4,64,256]{3,2,1,0:T(8,128)(2,1)S(1)} collective-permute-done((bf16[4,4,64,256]{3,2,1,0:T(8,128)(2,1)S(1)}, bf16[4,4,64,256]{3,2,1,0:T(8,128)(2,1)S(1)}, u32[]{:S(2)}, u32[]{:S(2)}) %collective-permute-start) | collective-permute-done | bytes 524320 | tf_op jit(solution)/shard_map/ppermute | solution.py:330
  107.4 23.6 %collective-permute-done.7.refs_1_.refs_4_ = bf16[2,1024,512]{2,1,0:T(8,128)(2,1)} collective-permute-done((bf16[2,1024,512]{2,1,0:T(8,128)(2,1)S(1)}, bf16[2,1024,512]{2,1,0:T(8,128)(2,1)}, u32[]{:S(2)}, u32[]{:S(2)}) %collective-permute-start.7) | collective-permute-done | bytes 2097184 | tf_op jit(solution)/shard_map/ppermute | solution.py:379
  193.3 18.6 %middle.1 = (bf16[2,16,128,512]{3,2,1,0:T(8,128)(2,1)}, bf16[2,16,128,512]{3,2,1,0:T(8,128)(2,1)}, bf16[2,16,64,256]{3,2,1,0:T(8,128)(2,1)}, bf16[2,16,64,256]{3...) custom-call(s32[12]{0:T(128)} %concatenate.27.meta, ...), custom_call_target="tpu_custom_call" | custom-call | flops 6442450944 | bytes 25165824 | tf_op jit(solution)/shard_map/middle/pallas_call | solution.py:142
  212.4 7.1 %collective-permute-done.15.refs_1_ = bf16[2,16,128,512]{3,2,1,0:T(8,128)(2,1)} collective-permute-done((bf16[2,16,128,512]{3,2,1,0:T(8,128)(2,1)}, bf16[2,16,128,512]{3,2,1,0:T(8,128)(2,1)}, u32[]{:S(2)}, u32[]{:S(2)}) %collective-permute-start.15) | collective-permute-done | bytes 4194336 | tf_op jit(solution)/shard_map/ppermute | solution.py:296
  219.5 5.8 %contract.4 = (bf16[2,1024,512]{2,1,0:T(8,128)(2,1)}, bf16[2,4,4,64,256]{4,3,2,1,0:T(8,128)(2,1)}, bf16[2,4,4,64,256]{4,3,2,1,0:T(8,128)(2,1)}, bf16[2,4,4,64,25...) custom-call(s32[12]{0:T(128)} %concatenate.32.meta, bf16[2,16,128,512]{3,2,1,0:T(8,128)(2,1)} %get-tuple-element.56.refs_0_, ...), custom_call_target="tpu_custom_call" | custom-call | flops 1073741824 | bytes 8388608 | tf_op jit(solution)/shard_map/contract/pallas_call | solution.py:209
  225.3 6.0 %contract.5 = (bf16[2,1024,512]{2,1,0:T(8,128)(2,1)}, bf16[2,4,4,64,256]{4,3,2,1,0:T(8,128)(2,1)}, bf16[2,4,4,64,256]{4,3,2,1,0:T(8,128)(2,1)}, bf16[2,4,4,64,25...) custom-call(s32[12]{0:T(128)} %concatenate.30.meta, ...), custom_call_target="tpu_custom_call", output_to_operand_aliasing={{1}: (6, {}), {2}: (7, {}), {3}: (8, {}), {4}: (9, {})} | custom-call | flops 1073741824 | bytes 8388608 | tf_op jit(solution)/shard_map/contract/pallas_call | solution.py:209
  235.1 5.8 %contract.6 = (bf16[2,1024,512]{2,1,0:T(8,128)(2,1)}, bf16[2,4,4,64,256]{4,3,2,1,0:T(8,128)(2,1)}, bf16[2,4,4,64,256]{4,3,2,1,0:T(8,128)(2,1)}, bf16[2,4,4,64,25...) custom-call(s32[12]{0:T(128)} %concatenate.31.meta, ...), custom_call_target="tpu_custom_call", output_to_operand_aliasing={{1}: (6, {}), {2}: (7, {}), {3}: (8, {}), {4}: (9, {})} | custom-call | flops 1073741824 | bytes 8388608 | tf_op jit(solution)/shard_map/contract/pallas_call | solution.py:209
  241.0 5.4 %contract.7 = (bf16[2,1024,512]{2,1,0:T(8,128)(2,1)}, bf16[2,4,4,64,256]{4,3,2,1,0:T(8,128)(2,1)}, bf16[2,4,4,64,256]{4,3,2,1,0:T(8,128)(2,1)}, bf16[2,4,4,64,25...) custom-call(s32[12]{0:T(128)} %concatenate.26.meta, ...), custom_call_target="tpu_custom_call", output_to_operand_aliasing={{1}: (5, {}), {2}: (6, {}), {3}: (7, {}), {4}: (8, {})} | custom-call | flops 1073741824 | bytes 8388608 | tf_op jit(solution)/shard_map/contract/pallas_call | solution.py:209
  249.4 11.5 %collective-permute-done.32 = bf16[2,16,64,256]{3,2,1,0:T(8,128)(2,1)} collective-permute-done((bf16[2,16,64,256]{3,2,1,0:T(8,128)(2,1)}, bf16[2,16,64,256]{3,2,1,0:T(8,128)(2,1)}, u32[]{:S(2)}, u32[]{:S(2)}) %collective-permute-start.32) | collective-permute-done | bytes 1048608 | tf_op jit(solution)/shard_map/ppermute | solution.py:321
  264.4 8.3 %collective-permute-done.22 = bf16[2,4,4,64,256]{4,3,2,1,0:T(8,128)(2,1)S(1)} collective-permute-done((bf16[2,4,4,64,256]{4,3,2,1,0:T(8,128)(2,1)}, bf16[2,4,4,64,256]{4,3,2,1,0:T(8,128)(2,1)S(1)}, u32[]{:S(2)}, u32[]{:S(2)}) %collective-permute-start.22) | collective-permute-done | bytes 1048608 | tf_op jit(solution)/shard_map/ppermute | solution.py:321
  275.4 6.1 %collective-permute-done.19 = bf16[2,1024,512]{2,1,0:T(8,128)(2,1)} collective-permute-done((bf16[2,1024,512]{2,1,0:T(8,128)(2,1)}, bf16[2,1024,512]{2,1,0:T(8,128)(2,1)}, u32[]{:S(2)}, u32[]{:S(2)}) %collective-permute-start.19) | collective-permute-done | bytes 2097184 | tf_op jit(solution)/shard_map/ppermute | solution.py:307
  281.9 5.3 %fusion = (bf16[2,1024,512]{2,1,0:T(8,128)(2,1)}, bf16[2,1024,512]{2,1,0:T(8,128)(2,1)}) fusion(bf16[2,1024,512]{2,1,0:T(8,128)(2,1)S(1)} %copy-done.14, bf16[2,1024,512]{2,1,0:T(8,128)(2,1)} %collective-permute-done.16, bf16[2,1024,512]{2,1,0:T(8,128)(2,1)} %collective-permute-done.19), kind=kLoop, calls=%fused_computation.2 | loop fusion | flops 7340032 | bytes 10485760 | tf_op jit(solution)/shard_map/convert_element_type | solution.py:300
  295.1 5.2 %collective-permute-start.20 = (bf16[2,1024,512]{2,1,0:T(8,128)(2,1)}, bf16[2,1024,512]{2,1,0:T(8,128)(2,1)}, u32[]{:S(2)}, u32[]{:S(2)}) collective-permute-start(bf16[2,1024,512]{2,1,0:T(8,128)(2,1)} %get-tuple-element.109), channel_id=1, source_target_pairs={{4,2},{5,3},{6,4},{7,5},{12,10},{13,11},{14,12},{15,13},{20,18},{2... | collective-permute-start | bytes 6291464 | tf_op jit(solution)/shard_map/ppermute | solution.py:307
  303.0 13.7 %collective-permute-done.25 = bf16[4,4,64,256]{3,2,1,0:T(8,128)(2,1)S(1)} collective-permute-done((bf16[4,4,64,256]{3,2,1,0:T(8,128)(2,1)S(1)}, bf16[4,4,64,256]{3,2,1,0:T(8,128)(2,1)S(1)}, u32[]{:S(2)}, u32[]{:S(2)}) %collective-permute-start.25) | collective-permute-done | bytes 524320 | tf_op jit(solution)/shard_map/ppermute | solution.py:322
  318.2 9.6 %all-to-all-start.1 = ((bf16[4,2,4,64,256]{4,3,2,1,0:T(8,128)(2,1)}), bf16[4,2,4,64,256]{4,3,2,1,0:T(8,128)(2,1)S(1)}, u32[]{:S(2)}, u32[]{:S(2)}) async-start(bf16[4,2,4,64,256]{4,3,2,1,0:T(8,128)(2,1)} %copy.62), calls=%async_computation.1 | async-start | bytes 2097152 | tf_op jit(solution)/shard_map/all_to_all | solution.py:422
  333.8 8.2 %collective-permute-done.34 = bf16[16,64,256]{2,1,0:T(8,128)(2,1)S(1)} collective-permute-done((bf16[16,64,256]{2,1,0:T(8,128)(2,1)S(1)}, bf16[16,64,256]{2,1,0:T(8,128)(2,1)S(1)}, u32[]{:S(2)}, u32[]{:S(2)}) %collective-permute-start.34) | collective-permute-done | bytes 524320 | tf_op jit(solution)/shard_map/ppermute | solution.py:330
  361.0 8.1 %all-to-all-done.1 = bf16[4,2,4,64,256]{4,3,2,1,0:T(8,128)(2,1)S(1)} async-done(((bf16[4,2,4,64,256]{4,3,2,1,0:T(8,128)(2,1)}), bf16[4,2,4,64,256]{4,3,2,1,0:T(8,128)(2,1)S(1)}, u32[]{:S(2)}, u32[]{:S(2)}) %all-to-all-start.1) | async-done | bytes 1048608 | tf_op jit(solution)/shard_map/all_to_all | solution.py:422
  374.9 7.0 %collective-permute-done.36 = bf16[4,4,64,256]{3,2,1,0:T(8,128)(2,1)S(1)} collective-permute-done((bf16[4,4,64,256]{3,2,1,0:T(8,128)(2,1)S(1)}, bf16[4,4,64,256]{3,2,1,0:T(8,128)(2,1)S(1)}, u32[]{:S(2)}, u32[]{:S(2)}) %collective-permute-start.36) | collective-permute-done | bytes 524320 | tf_op jit(solution)/shard_map/ppermute | solution.py:330
  390.8 17.4 %collective-permute-done.31 = bf16[2,16,64,256]{3,2,1,0:T(8,128)(2,1)} collective-permute-done((bf16[2,16,64,256]{3,2,1,0:T(8,128)(2,1)}, bf16[2,16,64,256]{3,2,1,0:T(8,128)(2,1)}, u32[]{:S(2)}, u32[]{:S(2)}) %collective-permute-start.31) | collective-permute-done | bytes 1048608 | tf_op jit(solution)/shard_map/ppermute | solution.py:331
  418.0 5.7 %collective-permute-done.27.q_ref = bf16[2,4,4,64,256]{4,3,2,1,0:T(8,128)(2,1)} collective-permute-done((bf16[2,4,4,64,256]{4,3,2,1,0:T(8,128)(2,1)S(1)}, bf16[2,4,4,64,256]{4,3,2,1,0:T(8,128)(2,1)}, u32[]{:S(2)}, u32[]{:S(2)}) %collective-permute-start.27) | collective-permute-done | bytes 1048608 | tf_op jit(solution)/shard_map/ppermute | solution.py:331
  423.7 5.1 %finish.4 = f32[4,256,1024]{2,1,0:T(8,128)} custom-call(s32[4]{0:T(128)} %copy-done.26, bf16[2,4,4,64,256]{4,3,2,1,0:T(8,128)(2,1)} %copy-done.10, bf16[2,4,4,64,256]{4,3,2,1,0:T(8,128)(2,1)} %collective-permute-done.27.q_ref), custom_call_target="tpu_custom_call" | custom-call | bytes 6291456 | tf_op jit(solution)/shard_map/finish/pallas_call | solution.py:272
  (180 shorter events, 164.4 us)
Async XLA Ops:
  34.9 48.5 %collective-permute-start.6 = (bf16[2,1024,512]{2,1,0:T(8,128)(2,1)S(1)}, bf16[2,1024,512]{2,1,0:T(8,128)(2,1)S(1)}, u32[]{:S(2)}, u32[]{:S(2)}) collective-permute-start(bf16[2,1024,512]{2,1,0:T(8,128)(2,1)S(1)} %pad_maximum_fusion.1.refs_0_.refs_3_), channel_id=1, source_target_pairs={{0,2},{1,3},{2,4},{3,5},{4,6},{5,7},{8,10},{9,11},{10,12},{11,13},... | collective-permute-start | bytes 6291464 | tf_op jit(solution)/shard_map/ppermute | solution.py:379
  39.2 48.1 %collective-permute-start.4 = (bf16[2,1024,512]{2,1,0:T(8,128)(2,1)S(1)}, bf16[2,1024,512]{2,1,0:T(8,128)(2,1)S(1)}, u32[]{:S(2)}, u32[]{:S(2)}) collective-permute-start(bf16[2,1024,512]{2,1,0:T(8,128)(2,1)S(1)} %pad_maximum_fusion.1.refs_0_.refs_3_), channel_id=1, source_target_pairs={{2,0},{3,1},{4,2},{5,3},{6,4},{7,5},{10,8},{11,9},{12,10},{13,11},... | collective-permute-start | bytes 6291464 | tf_op jit(solution)/shard_map/ppermute | solution.py:380
  83.4 47.7 %collective-permute-start.7 = (bf16[2,1024,512]{2,1,0:T(8,128)(2,1)S(1)}, bf16[2,1024,512]{2,1,0:T(8,128)(2,1)}, u32[]{:S(2)}, u32[]{:S(2)}) collective-permute-start(bf16[2,1024,512]{2,1,0:T(8,128)(2,1)S(1)} %collective-permute-done.6.refs_0_.refs_3_), channel_id=1, source_target_pairs={{2,4},{3,5},{4,6},{5,7},{10,12},{11,13},{12,14},{13,15},{18,20},{1... | collective-permute-start | bytes 6291464 | tf_op jit(solution)/shard_map/ppermute | solution.py:379
  87.3 47.3 %collective-permute-start.5 = (bf16[2,1024,512]{2,1,0:T(8,128)(2,1)S(1)}, bf16[2,1024,512]{2,1,0:T(8,128)(2,1)}, u32[]{:S(2)}, u32[]{:S(2)}) collective-permute-start(bf16[2,1024,512]{2,1,0:T(8,128)(2,1)S(1)} %collective-permute-done.4.refs_0_.refs_3_), channel_id=1, source_target_pairs={{2,0},{3,1},{4,2},{5,3},{10,8},{11,9},{12,10},{13,11},{18,16},{19,... | collective-permute-start | bytes 6291464 | tf_op jit(solution)/shard_map/ppermute | solution.py:380
  94.9 41.8 %collective-permute-start.2 = (bf16[4,4,64,256]{3,2,1,0:T(8,128)(2,1)S(1)}, bf16[4,4,64,256]{3,2,1,0:T(8,128)(2,1)S(1)}, u32[]{:S(2)}, u32[]{:S(2)}) collective-permute-start(bf16[4,4,64,256]{3,2,1,0:T(8,128)(2,1)S(1)} %get-tuple-element.128), channel_id=1, source_target_pairs={{0,8},{8,0},{16,24},{24,16},{1,9},{9,1},{17,25},{25,17},{2,10},{10... | collective-permute-start | bytes 1572872 | tf_op jit(solution)/shard_map/ppermute | solution.py:330
  105.9 52.7 %collective-permute-start.1 = (bf16[2,4,4,64,256]{4,3,2,1,0:T(8,128)(2,1)}, bf16[2,4,4,64,256]{4,3,2,1,0:T(8,128)(2,1)}, u32[]{:S(2)}, u32[]{:S(2)}) collective-permute-start(bf16[2,4,4,64,256]{4,3,2,1,0:T(8,128)(2,1)} %pad_maximum_fusion.7), channel_id=1, source_target_pairs={{0,8},{8,0},{16,24},{24,16},{1,9},{9,1},{17,25},{25,17},{2,10},{10... | collective-permute-start | bytes 3145736 | tf_op jit(solution)/shard_map/ppermute | solution.py:331
  131.0 52.2 %collective-permute-start.8 = (bf16[2,1024,512]{2,1,0:T(8,128)(2,1)}, bf16[2,1024,512]{2,1,0:T(8,128)(2,1)S(1)}, u32[]{:S(2)}, u32[]{:S(2)}) collective-permute-start(bf16[2,1024,512]{2,1,0:T(8,128)(2,1)} %collective-permute-done.7.refs_1_.refs_4_), channel_id=1, source_target_pairs={{4,6},{5,7},{12,14},{13,15},{20,22},{21,23},{28,30},{29,31}} | collective-permute-start | bytes 6291464 | tf_op jit(solution)/shard_map/ppermute | solution.py:379
  134.6 49.2 %collective-permute-start.9 = (bf16[2,1024,512]{2,1,0:T(8,128)(2,1)}, bf16[2,1024,512]{2,1,0:T(8,128)(2,1)}, u32[]{:S(2)}, u32[]{:S(2)}) collective-permute-start(bf16[2,1024,512]{2,1,0:T(8,128)(2,1)} %collective-permute-done.5.refs_0_.refs_3_), channel_id=1, source_target_pairs={{2,0},{3,1},{10,8},{11,9},{18,16},{19,17},{26,24},{27,25}} | collective-permute-start | bytes 6291464 | tf_op jit(solution)/shard_map/ppermute | solution.py:380
  231.3 50.1 %collective-permute-start.19 = (bf16[2,1024,512]{2,1,0:T(8,128)(2,1)}, bf16[2,1024,512]{2,1,0:T(8,128)(2,1)}, u32[]{:S(2)}, u32[]{:S(2)}) collective-permute-start(bf16[2,1024,512]{2,1,0:T(8,128)(2,1)} %get-tuple-element.73), channel_id=1, source_target_pairs={{6,4},{7,5},{14,12},{15,13},{22,20},{23,21},{30,28},{31,29}} | collective-permute-start | bytes 6291464 | tf_op jit(solution)/shard_map/ppermute | solution.py:307
  232.6 49.3 %collective-permute-start.16 = (bf16[2,1024,512]{2,1,0:T(8,128)(2,1)S(1)}, bf16[2,1024,512]{2,1,0:T(8,128)(2,1)}, u32[]{:S(2)}, u32[]{:S(2)}) collective-permute-start(bf16[2,1024,512]{2,1,0:T(8,128)(2,1)S(1)} %copy-done.11), channel_id=1, source_target_pairs={{0,2},{1,3},{8,10},{9,11},{16,18},{17,19},{24,26},{25,27}} | collective-permute-start | bytes 6291464 | tf_op jit(solution)/shard_map/ppermute | solution.py:306
  247.9 40.8 %collective-permute-start.24 = (bf16[2,4,4,64,256]{4,3,2,1,0:T(8,128)(2,1)}, bf16[2,4,4,64,256]{4,3,2,1,0:T(8,128)(2,1)S(1)}, u32[]{:S(2)}, u32[]{:S(2)}) collective-permute-start(bf16[2,4,4,64,256]{4,3,2,1,0:T(8,128)(2,1)} %get-tuple-element.77), channel_id=1, source_target_pairs={{0,16},{8,24},{16,0},{24,8},{1,17},{9,25},{17,1},{25,9},{2,18},{10... | collective-permute-start | bytes 3145736 | tf_op jit(solution)/shard_map/ppermute | solution.py:321
  260.9 34.2 %collective-permute-start.28 = (bf16[2,16,64,256]{3,2,1,0:T(8,128)(2,1)}, bf16[2,16,64,256]{3,2,1,0:T(8,128)(2,1)S(1)}, u32[]{:S(2)}, u32[]{:S(2)}) collective-permute-start(bf16[2,16,64,256]{3,2,1,0:T(8,128)(2,1)} %get-tuple-element.79), channel_id=1, source_target_pairs={{0,8},{8,0},{16,24},{24,16},{1,9},{9,1},{17,25},{25,17},{2,10},{10... | collective-permute-start | bytes 3145736 | tf_op jit(solution)/shard_map/ppermute | solution.py:321
  272.7 55.1 %collective-permute-start.33 = (bf16[16,64,256]{2,1,0:T(8,128)(2,1)}, bf16[16,64,256]{2,1,0:T(8,128)(2,1)}, u32[]{:S(2)}, u32[]{:S(2)}) collective-permute-start(bf16[16,64,256]{2,1,0:T(8,128)(2,1)} %fusion.9), channel_id=1, source_target_pairs={{0,8},{8,0},{16,24},{24,16},{1,9},{9,1},{17,25},{25,17},{2,10},{10... | collective-permute-start | bytes 1572872 | tf_op jit(solution)/shard_map/ppermute | solution.py:322
  287.3 57.7 %collective-permute-start.17 = (bf16[2,1024,512]{2,1,0:T(8,128)(2,1)}, bf16[2,1024,512]{2,1,0:T(8,128)(2,1)}, u32[]{:S(2)}, u32[]{:S(2)}) collective-permute-start(bf16[2,1024,512]{2,1,0:T(8,128)(2,1)} %get-tuple-element.108), channel_id=1, source_target_pairs={{0,2},{1,3},{2,4},{3,5},{8,10},{9,11},{10,12},{11,13},{16,18},{17,... | collective-permute-start | bytes 6291464 | tf_op jit(solution)/shard_map/ppermute | solution.py:306
  288.9 27.8 %collective-permute-start.25 = (bf16[4,4,64,256]{3,2,1,0:T(8,128)(2,1)S(1)}, bf16[4,4,64,256]{3,2,1,0:T(8,128)(2,1)S(1)}, u32[]{:S(2)}, u32[]{:S(2)}) collective-permute-start(bf16[4,4,64,256]{3,2,1,0:T(8,128)(2,1)S(1)} %fusion.7), channel_id=1, source_target_pairs={{0,8},{8,0},{16,24},{24,16},{1,9},{9,1},{17,25},{25,17},{2,10},{10... | collective-permute-start | bytes 1572872 | tf_op jit(solution)/shard_map/ppermute | solution.py:322
  295.1 57.5 %collective-permute-start.20 = (bf16[2,1024,512]{2,1,0:T(8,128)(2,1)}, bf16[2,1024,512]{2,1,0:T(8,128)(2,1)}, u32[]{:S(2)}, u32[]{:S(2)}) collective-permute-start(bf16[2,1024,512]{2,1,0:T(8,128)(2,1)} %get-tuple-element.109), channel_id=1, source_target_pairs={{4,2},{5,3},{6,4},{7,5},{12,10},{13,11},{14,12},{15,13},{20,18},{2... | collective-permute-start | bytes 6291464 | tf_op jit(solution)/shard_map/ppermute | solution.py:307
  301.3 29.8 %collective-permute-start.29 = (bf16[16,64,256]{2,1,0:T(8,128)(2,1)}, bf16[16,64,256]{2,1,0:T(8,128)(2,1)}, u32[]{:S(2)}, u32[]{:S(2)}) collective-permute-start(bf16[16,64,256]{2,1,0:T(8,128)(2,1)} %fusion.8), channel_id=1, source_target_pairs={{0,16},{8,24},{16,0},{24,8},{1,17},{9,25},{17,1},{25,9},{2,18},{10... | collective-permute-start | bytes 1572872 | tf_op jit(solution)/shard_map/ppermute | solution.py:322
  318.2 51.0 %all-to-all-start.1 = ((bf16[4,2,4,64,256]{4,3,2,1,0:T(8,128)(2,1)}), bf16[4,2,4,64,256]{4,3,2,1,0:T(8,128)(2,1)S(1)}, u32[]{:S(2)}, u32[]{:S(2)}) async-start(bf16[4,2,4,64,256]{4,3,2,1,0:T(8,128)(2,1)} %copy.62), calls=%async_computation.1 | async-start | bytes 2097152 | tf_op jit(solution)/shard_map/all_to_all | solution.py:422
  332.3 38.6 %collective-permute-start.30 = (bf16[16,64,256]{2,1,0:T(8,128)(2,1)S(1)}, bf16[16,64,256]{2,1,0:T(8,128)(2,1)}, u32[]{:S(2)}, u32[]{:S(2)}) collective-permute-start(bf16[16,64,256]{2,1,0:T(8,128)(2,1)S(1)} %fusion.3), channel_id=1, source_target_pairs={{0,16},{8,24},{16,0},{24,8},{1,17},{9,25},{17,1},{25,9},{2,18},{10... | collective-permute-start | bytes 1572872 | tf_op jit(solution)/shard_map/ppermute | solution.py:330
  343.5 41.5 %collective-permute-start.35 = (bf16[2,16,64,256]{3,2,1,0:T(8,128)(2,1)}, bf16[2,16,64,256]{3,2,1,0:T(8,128)(2,1)S(1)}, u32[]{:S(2)}, u32[]{:S(2)}) collective-permute-start(bf16[2,16,64,256]{3,2,1,0:T(8,128)(2,1)} %get-tuple-element.122), channel_id=1, source_target_pairs={{0,16},{8,24},{16,0},{24,8},{1,17},{9,25},{17,1},{25,9},{2,18},{10... | collective-permute-start | bytes 3145736 | tf_op jit(solution)/shard_map/ppermute | solution.py:331
  348.5 80.3 %collective-permute-start.18 = (bf16[2,1024,512]{2,1,0:T(8,128)(2,1)}, bf16[2,1024,512]{2,1,0:T(8,128)(2,1)}, u32[]{:S(2)}, u32[]{:S(2)}) collective-permute-start(bf16[2,1024,512]{2,1,0:T(8,128)(2,1)} %add_convert_fusion.2), channel_id=1, source_target_pairs={{0,2},{1,3},{2,4},{3,5},{4,6},{5,7},{8,10},{9,11},{10,12},{11,13},... | collective-permute-start | bytes 6291464 | tf_op jit(solution)/shard_map/ppermute | solution.py:306
  356.1 72.6 %collective-permute-start.21 = (bf16[2,1024,512]{2,1,0:T(8,128)(2,1)}, bf16[2,1024,512]{2,1,0:T(8,128)(2,1)}, u32[]{:S(2)}, u32[]{:S(2)}) collective-permute-start(bf16[2,1024,512]{2,1,0:T(8,128)(2,1)} %add_convert_fusion.1), channel_id=1, source_target_pairs={{2,0},{3,1},{4,2},{5,3},{6,4},{7,5},{10,8},{11,9},{12,10},{13,11},... | collective-permute-start | bytes 6291464 | tf_op jit(solution)/shard_map/ppermute | solution.py:307
  383.7 29.5 %collective-permute-start.37 = (bf16[2,4,4,64,256]{4,3,2,1,0:T(8,128)(2,1)S(1)}, bf16[2,4,4,64,256]{4,3,2,1,0:T(8,128)(2,1)}, u32[]{:S(2)}, u32[]{:S(2)}) collective-permute-start(bf16[2,4,4,64,256]{4,3,2,1,0:T(8,128)(2,1)S(1)} %pad_maximum_fusion.13.p_ref), channel_id=1, source_target_pairs={{0,16},{8,24},{16,0},{24,8},{1,17},{9,25},{17,1},{25,9},{2,18},{10... | collective-permute-start | bytes 3145736 | tf_op jit(solution)/shard_map/ppermute | solution.py:331
  385.0 38.7 %collective-permute-start.27 = (bf16[2,4,4,64,256]{4,3,2,1,0:T(8,128)(2,1)S(1)}, bf16[2,4,4,64,256]{4,3,2,1,0:T(8,128)(2,1)}, u32[]{:S(2)}, u32[]{:S(2)}) collective-permute-start(bf16[2,4,4,64,256]{4,3,2,1,0:T(8,128)(2,1)S(1)} %pad_maximum_fusion.10.p_ref), channel_id=1, source_target_pairs={{0,8},{8,0},{16,24},{24,16},{1,9},{9,1},{17,25},{25,17},{2,10},{10... | collective-permute-start | bytes 3145736 | tf_op jit(solution)/shard_map/ppermute | solution.py:331
  (45 other events, 768.1 us)

commit v4 on v3

v4 whole, which is shorter than its diff:
```python
import functools
import math

import jax
import jax.numpy as jnp
from jax import lax
from jax.experimental import pallas as pl
from jax.experimental.pallas import tpu as pltpu
from jax.sharding import PartitionSpec as P

F32 = jnp.float32
BF16 = jnp.bfloat16
MIDDLE_MIB = 60


def params(mib, dims=1):
    return pltpu.CompilerParams(
        dimension_semantics=("arbitrary",) * dims, vmem_limit_bytes=mib * 1024 * 1024
    )


def gelu_parts(value_in):
    cdf_part = 0.5 * (1.0 + lax.erf(value_in * 0.7071067811865476))
    slope_part = cdf_part + value_in * jnp.exp(-0.5 * value_in * value_in) * 0.3989422804014327
    return (value_in * cdf_part, slope_part)


def dot(a, b, ca, cb):
    return lax.dot_general(a, b, (((ca,), (cb,)), ((), ())), preferred_element_type=F32)


def cost(flops, elements, trans=0):
    return pl.CostEstimate(flops=flops, bytes_accessed=2 * elements, transcendentals=trans)


def assemble_kernel(meta, *refs):
    out_ref = refs[-1]
    _, _, wd, size, bw = out_ref.shape
    step = size // 4
    half = size // 2
    low = meta[0] == 0
    for e in range(4):
        share = lax.bitwise_xor(meta[1], e) * step
        first = refs[e][0, 0] if e < 3 else refs[3][0]
        second = refs[e][0, 1] if e < 3 else refs[4][0]
        left, right = first[:, :, : bw // 2], first[:, :, bw // 2 :]
        first = jnp.concatenate(
            [jnp.where(low, left, right), jnp.where(low, right, left)], axis=2
        )
        out_ref[0, 0, :, pl.ds(pl.multiple_of(share, step), step), :] = first
        row = lax.rem(share + meta[0] * half, size)
        out_ref[1, 0, :, pl.ds(pl.multiple_of(row, step), step), :] = second


def assemble(core, mine, own, by_x, by_y, diag):
    nl, _, wd, step, bw = own.shape
    spec = pl.BlockSpec((1, 2, wd, step, bw), lambda k, meta: (k, 0, 0, 0, 0))
    dspec = pl.BlockSpec((1, wd, step, bw), lambda k, meta: (k, 0, 0, 0))
    return pl.pallas_call(
        assemble_kernel,
        grid_spec=pltpu.PrefetchScalarGridSpec(
            num_scalar_prefetch=1,
            grid=(nl,),
            in_specs=[spec, spec, spec, dspec, dspec],
            out_specs=pl.BlockSpec((2, 1, wd, 4 * step, bw), lambda k, meta: (0, k, 0, 0, 0)),
        ),
        out_shape=jax.ShapeDtypeStruct((2, nl, wd, 4 * step, bw), BF16),
        compiler_params=params(12),
        cost_estimate=cost(0, 16 * nl * wd * step * bw),
        name="assemble",
    )(jnp.stack([core, mine]).astype(jnp.int32), own, by_x, by_y, *diag)


def total(refs, span):
    val = refs[0][span, :]
    for ref in refs[1:]:
        val = val + ref[span, :]
    return val


def weight_spec(side, w14s, pa):
    same = w14s[0] is w14s[1]
    shape = (1, 1, pa, *w14s[side].shape[3:])
    return pl.BlockSpec(shape, lambda s, meta: (side if same else 0, meta[0], s, 0, 0))


def expand_kernel(meta, *refs, side, pa, bw, hd, sub):
    x_refs, (w_ref, own_ref, send_ref) = refs[:-3], refs[-3:]
    m = hd * sub
    own, send = [], []
    for a in range(pa):
        x = total(x_refs, slice(a * bw, (a + 1) * bw))
        val = dot(w_ref[0, 0, a], x, side, 0)
        own.append(val[:m].reshape(hd, sub, val.shape[-1]))
        send.append(val[m:].reshape(hd, sub, val.shape[-1]))
    own_ref[...] = jnp.concatenate(own, axis=1).astype(BF16)
    send_ref[...] = jnp.concatenate(send, axis=1).astype(BF16)


def expand(side, meta, xs, w14s, hd, sub):
    _, nl, wd, m2, bw = w14s[1].shape
    rows = xs[0].shape[-1]
    pa = min(wd, 2)
    out = jax.ShapeDtypeStruct((hd, wd * sub, rows), BF16)
    out_spec = pl.BlockSpec((hd, pa * sub, rows), lambda s, meta: (0, s, 0))
    return pl.pallas_call(
        functools.partial(expand_kernel, side=side, pa=pa, bw=bw, hd=hd, sub=sub),
        grid_spec=pltpu.PrefetchScalarGridSpec(
            num_scalar_prefetch=1,
            grid=(wd // pa,),
            in_specs=[pl.BlockSpec((pa * bw, rows), lambda s, meta: (s, 0))] * len(xs)
            + [weight_spec(side, w14s, pa)],
            out_specs=[out_spec, out_spec],
        ),
        out_shape=[out, out],
        compiler_params=params(12),
        cost_estimate=cost(2 * wd * m2 * bw * rows, wd * (bw * rows + m2 * bw + m2 * rows)),
        name="expand",
    )(meta, *xs, w14s[side])


def put_shares(meta, first, gsc, val, keep_ref, send_ref, index, dp):
    step = val.shape[0] // dp
    gsc[...] = val.astype(gsc.dtype)
    half = dp // 2
    for p in range(dp):
        row = pl.multiple_of(meta[first + p] * step, step)
        ref = keep_ref if p < half else send_ref
        ref[(p % half, *index)] = gsc[pl.ds(row, step), :].astype(BF16)


def join(pieces):
    if pieces[0].shape[0] % 16:
        return jnp.concatenate([p.astype(F32) for p in pieces], axis=0).astype(BF16)
    return jnp.concatenate(pieces, axis=0)


def rows_of(meta, sides, b, nl):
    pieces = []
    for k in range(nl):
        for side in sides:
            val = side[k][b]
            if k in (1, nl - 1):
                val = jnp.where(meta[2] == k, side[nl][b], val)
            pieces.append(val)
    return join(pieces)


def split_cores(val, own_ref, send_ref, b, nl, part):
    for k in range(nl):
        own_ref[b, k * part : (k + 1) * part] = val[2 * k * part : (2 * k + 1) * part].astype(BF16)
        send_ref[b, k * part : (k + 1) * part] = val[(2 * k + 1) * part : (2 * k + 2) * part].astype(BF16)


def forward_kernel(meta, *refs, nl, part, hb):
    sides = (refs[: nl + 1], refs[nl + 1 : 2 * nl + 2])
    w2_ref, w3_ref, own_ref, send_ref, y_ref, act_ref, slope_ref = refs[2 * nl + 2 :]
    for b in range(hb):
        yb = rows_of(meta, sides, b, nl)
        y_ref[b] = yb
        val, slope = gelu_parts(dot(w2_ref[b], yb, 0, 0))
        act = val.astype(BF16)
        act_ref[b] = act
        slope_ref[b] = slope.astype(BF16)
        split_cores(dot(w3_ref[b], act, 1, 0), own_ref, send_ref, b, nl, part)


def backward_kernel(meta, *refs, nl, part, hb, dp, scale):
    sides = (refs[: nl + 1], refs[nl + 1 : 2 * nl + 2])
    refs = refs[2 * nl + 2 :]
    w2_ref, w3_ref, y_ref, act_ref, slope_ref, own_ref, send_ref = refs[:7]
    g2k_ref, g2s_ref, g3k_ref, g3s_ref, gsc = refs[7:]
    for b in range(hb):
        dzb = rows_of(meta, sides, b, nl)
        dact = dot(w3_ref[b], dzb, 0, 0)
        dpre = (dact * slope_ref[b].astype(F32)).astype(BF16)
        split_cores(dot(w2_ref[b], dpre, 1, 0), own_ref, send_ref, b, nl, part)
        put_shares(meta, 4, gsc.at[b, 0], dot(y_ref[b], dpre, 1, 1) * scale, g2k_ref, g2s_ref, (b,), dp)
        put_shares(
            meta, 4 + dp, gsc.at[b, 1], dot(dzb, act_ref[b], 1, 1) * scale, g3k_ref, g3s_ref, (b,), dp
        )


def middle(back, meta, owns, recvs, w2, w3, saved, dp, scale):
    hd, k, j = w2.shape
    nl = len(owns) - 1
    _, part, rows = owns[0].shape
    hb = 2
    half = dp // 2
    slot = pl.BlockSpec((hb, part, rows), lambda b, meta: (b, 0, 0))
    one = pl.BlockSpec((hb, nl * part, rows), lambda b, meta: (b, 0, 0))
    full = pl.BlockSpec((hb, k, rows), lambda b, meta: (b, 0, 0))
    wspec = pl.BlockSpec((hb, k, j), lambda b, meta: (b, 0, 0))
    gspec = pl.BlockSpec((half, hb, k // dp, j), lambda b, meta: (0, b, 0, 0))
    zout = jax.ShapeDtypeStruct((hd, nl * part, rows), BF16)
    yout = jax.ShapeDtypeStruct((hd, k, rows), BF16)
    gout = jax.ShapeDtypeStruct((half, hd, k // dp, j), BF16)
    gtype = BF16 if (k // dp) % 16 == 0 else F32
    in_specs = [slot] * (2 * nl + 2) + [wspec, wspec]
    if back:
        body = functools.partial(backward_kernel, nl=nl, part=part, hb=hb, dp=dp, scale=scale)
        in_specs += [full] * 3
        out_specs, out_shape = [one] * 2 + [gspec] * 4, [zout] * 2 + [gout] * 4
        scratch = [pltpu.VMEM((hb, 2, k, j), gtype)]
        work = cost(8 * hd * k * j * rows, 5 * hd * k * rows + 4 * hd * k * j)
    else:
        body = functools.partial(forward_kernel, nl=nl, part=part, hb=hb)
        out_specs, out_shape = [one] * 2 + [full] * 3, [zout] * 2 + [yout] * 3
        scratch = []
        work = cost(4 * hd * k * j * rows, 5 * hd * k * rows + 2 * hd * k * j, 2 * hd * j * rows)
    return pl.pallas_call(
        body,
        grid_spec=pltpu.PrefetchScalarGridSpec(
            num_scalar_prefetch=1,
            grid=(hd // hb,),
            in_specs=in_specs,
            out_specs=out_specs,
            scratch_shapes=scratch,
        ),
        out_shape=out_shape,
        compiler_params=params(MIDDLE_MIB),
        cost_estimate=work,
        name="backward" if back else "forward",
    )(meta, *owns, *recvs, w2, w3, *saved)


def block_rows(own_ref, recv_ref, pa, hd, sub):
    wide = [ref[...].astype(F32) for ref in (own_ref, recv_ref)]
    rows = wide[0].shape[-1]
    return [
        jnp.concatenate(
            [v[:, a * sub : (a + 1) * sub, :].reshape(hd * sub, rows) for v in wide], axis=0
        ).astype(BF16)
        for a in range(pa)
    ]


def output_kernel(meta, zo_ref, zr_ref, w4_ref, out_ref, *, pa, bw, hd, sub):
    for a, z in enumerate(block_rows(zo_ref, zr_ref, pa, hd, sub)):
        out_ref[0, a * bw : (a + 1) * bw, :] = dot(w4_ref[0, 0, a], z, 0, 0).astype(BF16)


def output_parts(meta, z_own, z_recv, w14s, sub):
    same = w14s[0] is w14s[1]
    w4 = w14s[1]
    _, nl, wd, m2, bw = w4.shape
    hd, _, rows = z_own.shape
    pa = min(wd, 2)
    steps = wd // pa
    zspec = pl.BlockSpec((hd, pa * sub, rows), lambda k, s, meta: (0, k * steps + s, 0))
    wspec = pl.BlockSpec(
        (1, 1, pa, m2, bw), lambda k, s, meta: (1 if same else 0, meta[k], s, 0, 0)
    )
    return pl.pallas_call(
        functools.partial(output_kernel, pa=pa, bw=bw, hd=hd, sub=sub),
        grid_spec=pltpu.PrefetchScalarGridSpec(
            num_scalar_prefetch=1,
            grid=(nl, steps),
            in_specs=[zspec, zspec, wspec],
            out_specs=pl.BlockSpec((1, pa * bw, rows), lambda k, s, meta: (meta[k], s, 0)),
        ),
        out_shape=jax.ShapeDtypeStruct((nl, wd * bw, rows), BF16),
        compiler_params=params(16, 2),
        cost_estimate=cost(2 * nl * wd * m2 * bw * rows, nl * wd * (bw * rows + m2 * rows + m2 * bw)),
        name="output",
    )(meta, z_own, z_recv, w4)


def contract_kernel(meta, *refs, nx, late, chain, pa, bw, hd, sub, dp, scale):
    zo_ref, zr_ref, dyo_ref, dyr_ref, w1_ref = refs[:5]
    x_refs, g_refs = refs[5 : 5 + nx], refs[5 + nx : 5 + 2 * nx]
    refs = refs[5 + 2 * nx + (4 if chain else 0) :]
    part_ref, g1k_ref, g1s_ref, g4k_ref, g4s_ref, gsc = refs
    zs = block_rows(zo_ref, zr_ref, pa, hd, sub)
    dys = block_rows(dyo_ref, dyr_ref, pa, hd, sub)

    def shard(refs, span):
        if late:
            return jnp.where(meta[3] > 0, refs[1][span, :], refs[0][span, :])
        return total(refs, span)

    for a in range(pa):
        span = slice(a * bw, (a + 1) * bw)
        z, dy = zs[a], dys[a]
        part_ref[span, :] = dot(w1_ref[0, 0, a], dy, 1, 0).astype(BF16)
        g1 = dot(dy, shard(x_refs, span), 1, 1) * scale
        g4 = dot(z, shard(g_refs, span), 1, 1) * scale
        put_shares(meta, 4, gsc.at[a, 0], g1, g1k_ref, g1s_ref, (0, a), dp)
        put_shares(meta, 4 + dp, gsc.at[a, 1], g4, g4k_ref, g4s_ref, (0, a), dp)


def contract(k, meta, zdy, w14s, xs, gs, late, grads, sub, dp, scale):
    _, nl, wd, m2, bw = w14s[1].shape
    hd, _, rows = zdy[0].shape
    pa = min(wd, 2)
    steps = wd // pa
    half = dp // 2
    zspec = pl.BlockSpec((hd, pa * sub, rows), lambda s, meta: (0, k * steps + s, 0))
    xspec = pl.BlockSpec((pa * bw, rows), lambda s, meta: (s, 0))
    gspec = pl.BlockSpec((half, 1, pa, m2 // dp, bw), lambda s, meta: (0, meta[0], s, 0, 0))
    gout = jax.ShapeDtypeStruct((half, nl, wd, m2 // dp, bw), BF16)
    gtype = BF16 if (m2 // dp) % 16 == 0 else F32
    args = [meta, *zdy, w14s[0], *xs, *gs]
    specs = [zspec] * 4 + [weight_spec(0, w14s, pa)] + [xspec] * (2 * len(xs))
    aliases = {}
    if grads is not None:
        aliases = {len(args) + i: 1 + i for i in range(4)}
        args += list(grads)
        specs += [pl.BlockSpec(memory_space=pl.ANY)] * 4
    return pl.pallas_call(
        functools.partial(
            contract_kernel,
            nx=len(xs),
            late=late,
            chain=grads is not None,
            pa=pa,
            bw=bw,
            hd=hd,
            sub=sub,
            dp=dp,
            scale=scale,
        ),
        grid_spec=pltpu.PrefetchScalarGridSpec(
            num_scalar_prefetch=1,
            grid=(steps,),
            in_specs=specs,
            out_specs=[xspec, gspec, gspec, gspec, gspec],
            scratch_shapes=[pltpu.VMEM((pa, 2, m2, bw), gtype)],
        ),
        out_shape=[jax.ShapeDtypeStruct(xs[0].shape, BF16), gout, gout, gout, gout],
        input_output_aliases=aliases,
        compiler_params=params(20),
        cost_estimate=cost(
            6 * wd * m2 * bw * rows, wd * (3 * bw * rows + 2 * m2 * rows + 3 * m2 * bw)
        ),
        name="contract",
    )(*args)


def finish_kernel(tab, *refs, dp, piece, flip):
    val_refs, o_ref, sc = refs[:dp], refs[dp], refs[dp + 1]
    count = o_ref.shape[0]
    for a in range(count):
        for e in range(dp):
            val = val_refs[e][0, a].astype(F32)
            step = val.shape[0]
            share = lax.bitwise_xor(tab[0], e) * (step // piece)
            for i in range(step // piece):
                row = pl.multiple_of(tab[1 + share + i], piece)
                if flip:
                    sc[pl.ds(row, piece), :] = val[i * piece : (i + 1) * piece]
                else:
                    o_ref[a, pl.ds(row, piece), :] = val[i * piece : (i + 1) * piece]
        if flip:
            o_ref[a] = sc[...].T


def finish(tab, shares, flip):
    dp = len(shares)
    outer, wd, step, bw = shares[0].shape
    size = dp * step
    pieces = tab.shape[0] - 1
    piece = size // pieces
    count = min(wd, 4)
    if flip and size % 128:
        base = tab[0]
        merged = jnp.stack(shares)[jnp.arange(dp) ^ base]
        merged = jnp.transpose(merged, (1, 2, 0, 3, 4)).reshape(outer, wd, pieces, piece, bw)
        merged = merged[:, :, jnp.argsort(tab[1:])].reshape(outer, wd, size, bw)
        return jnp.transpose(merged, (1, 3, 0, 2)).reshape(wd, bw, outer * size).astype(F32)
    spec = pl.BlockSpec((1, count, step, bw), lambda o, a, tab: (o, a, 0, 0))
    if flip:
        shape = (wd, bw, outer * size)
        ospec = pl.BlockSpec((count, bw, size), lambda o, a, tab: (a, 0, o))
    else:
        shape = (wd, outer * size, bw)
        ospec = pl.BlockSpec((count, size, bw), lambda o, a, tab: (a, o, 0))
    return pl.pallas_call(
        functools.partial(finish_kernel, dp=dp, piece=piece, flip=flip),
        grid_spec=pltpu.PrefetchScalarGridSpec(
            num_scalar_prefetch=1,
            grid=(outer, wd // count),
            in_specs=[spec] * dp,
            out_specs=ospec,
            scratch_shapes=[pltpu.VMEM((size, bw), F32)],
        ),
        out_shape=jax.ShapeDtypeStruct(shape, F32),
        compiler_params=params(12, 2),
        cost_estimate=cost(0, 3 * wd * outer * size * bw),
        name="finish",
    )(tab, *shares)


def close_kernel(a_ref, b_ref, c_ref, out_ref):
    val = a_ref[...].astype(F32) + b_ref[...].astype(F32) + c_ref[...].astype(F32)
    out_ref[...] = val.T.astype(BF16)


def close(a, b, c):
    width, rows = a.shape
    block = min(width, 256)
    return pl.pallas_call(
        close_kernel,
        grid=(width // block,),
        in_specs=[pl.BlockSpec((block, rows), lambda s: (s, 0))] * 3,
        out_specs=pl.BlockSpec((rows, block), lambda s: (0, s)),
        out_shape=jax.ShapeDtypeStruct((rows, width), BF16),
        compiler_params=params(12),
        cost_estimate=cost(2 * width * rows, 4 * width * rows),
        name="close",
    )(a, b, c)


def up_pairs(lo, hi):
    return [(2 * p + c, 2 * p + 2 + c) for p in range(lo, hi) for c in range(2)]


def down_pairs(lo, hi):
    return [(2 * p + 2 + c, 2 * p + c) for p in range(lo, hi) for c in range(2)]


def swap(val, n):
    return lax.ppermute(val, "tensor", [(i, i ^ 1) for i in range(n)])


def add(a, b):
    return (a.astype(F32) + b.astype(F32)).astype(BF16)


X_PAIRS = [(i, i ^ 1) for i in range(4)]
Y_PAIRS = [(i, i ^ 2) for i in range(4)]


def reduce_dp(grads, dp, orders):
    if dp != 4:
        return [lax.psum_scatter(jnp.concatenate(pair), "dp") for pair in grads]
    came = [lax.ppermute(g[1], "dp", p[0]) for g, p in zip(grads, orders)]
    second = [add(g[0][1], c[1]) for g, c in zip(grads, came)]
    second = lax.optimization_barrier(second)
    second = [lax.ppermute(v, "dp", p[1]) for v, p in zip(second, orders)]
    return [
        (g[0][0].astype(F32) + c[0].astype(F32) + v.astype(F32)).astype(BF16)
        for g, c, v in zip(grads, came, second)
    ]


def gather_dp(val, dp, x_last):
    if dp != 4:
        every = lax.all_gather(val, "dp")
        return [every[q] for q in range(dp)]
    by_x = lax.ppermute(val, "dp", X_PAIRS)
    by_y = lax.ppermute(val, "dp", Y_PAIRS)
    if x_last:
        diag = lax.ppermute(by_y, "dp", X_PAIRS)
    else:
        diag = lax.ppermute(by_x, "dp", Y_PAIRS)
    return [val, by_x, by_y, diag]


def body(tokens, cotangent, w_first, w_second, w_third, w_fourth):
    rows = tokens.shape[0]
    wd, bw, _ = w_first.shape
    hd = w_second.shape[0]
    n = lax.axis_size("tensor")
    dp = lax.axis_size("dp")
    nl = n // 2
    sub = bw // (wd * n)
    part = wd * sub
    m = hd * sub
    m2 = 2 * m
    step = m2 // dp
    scale = 1.0 / math.sqrt(rows * dp)
    me = lax.axis_index("tensor")
    mine = lax.axis_index("dp")
    pos, core = me // 2, me % 2
    lines = [[2 * p + c for p in range(nl)] for c in range(2)]
    x_first, y_first = (X_PAIRS, Y_PAIRS), (Y_PAIRS, X_PAIRS)

    dps = jnp.arange(dp, dtype=jnp.int32)
    if dp == 4:
        inv_x = (((dps & 1) << 1) | (dps >> 1)) ^ mine
        inv_y = dps ^ mine
        base = mine
    else:
        inv_x = inv_y = dps
        base = mine * 0
    low_end, high_end = pos == 0, pos == nl - 1
    late_slot = jnp.where(low_end, nl - 1, jnp.where(high_end, 1, -1))

    def meta_of(head, late):
        head = jnp.stack([jnp.asarray(v, jnp.int32) for v in (head, core, late_slot, late)])
        return jnp.concatenate([head, inv_x, inv_y])

    w1 = lax.dynamic_index_in_dim(
        w_first.reshape(wd, dp, bw // dp, nl * m2), mine, axis=1, keepdims=False
    )
    w4 = lax.dynamic_index_in_dim(
        w_fourth.reshape(wd, nl, dp, step, bw), mine, axis=2, keepdims=False
    )
    if m2 == bw:
        w1 = w1.reshape(wd, step, nl, bw)
        w14 = jnp.stack([jnp.transpose(w1, (2, 0, 1, 3)), jnp.transpose(w4, (1, 0, 2, 3))], axis=1)
        w14 = lax.all_to_all(
            w14, "tensor", split_axis=0, concat_axis=0, axis_index_groups=lines, tiled=True
        )
        sides = [w14[:, 0], w14[:, 1]]
    else:
        w1 = jnp.transpose(w1.reshape(wd, bw // dp, nl, m2), (2, 0, 1, 3))
        w4 = jnp.transpose(w4, (1, 0, 2, 3))
        sides = [
            lax.all_to_all(
                w, "tensor", split_axis=0, concat_axis=0, axis_index_groups=lines, tiled=True
            )
            for w in (w1, w4)
        ]
    x_own, g_own = tokens.T, cotangent.T
    x_own, sides = lax.optimization_barrier((x_own, sides))
    whole = dp == 4 and m2 == bw
    if whole:
        by_x = lax.ppermute(w14, "dp", X_PAIRS)
        by_y = lax.ppermute(w14, "dp", Y_PAIRS)
        gate = [by_x, by_y]
    else:
        gate = [lax.all_gather(w, "dp") for w in sides]

    def relative(w):
        w = w.reshape(hd, nl, 2, part, bw)
        w = jnp.where(core == 0, w, w[:, :, ::-1])
        w = lax.dynamic_slice_in_dim(jnp.concatenate([w, w], axis=1), pos, nl, axis=1)
        return w.reshape(hd, bw, bw)

    w2 = relative(w_second)
    w3 = relative(jnp.swapaxes(w_third, 1, 2))

    def hop(ups, downs, r):
        up = lax.ppermute(ups[-1], "tensor", up_pairs(r - 1, nl - 1))
        down = lax.ppermute(downs[-1], "tensor", down_pairs(0, nl - r))
        return up, down

    x_ups, x_downs = [x_own], [x_own]
    for r in range(1, nl):
        up, down = hop(x_ups, x_downs, r)
        if r == 1:
            up, down, gate, w2, w3 = lax.optimization_barrier((up, down, gate, w2, w3))
            if whole:
                by_x, by_y = gate
                gate = [
                    lax.ppermute(by_y[:, 0], "dp", X_PAIRS),
                    lax.ppermute(by_x[:, 1], "dp", Y_PAIRS),
                ]
        elif r == 2:
            up, down, gate, g_own = lax.optimization_barrier((up, down, gate, g_own))
        x_ups.append(up)
        x_downs.append(down)
    g_ups, g_downs = [g_own], [g_own]
    for r in range(1, nl):
        up, down = hop(g_ups, g_downs, r)
        up, down = lax.optimization_barrier((up, down))
        g_ups.append(up)
        g_downs.append(down)
    if whole:
        w14s = (assemble(core, mine, w14, by_x, by_y, gate),) * 2
    else:
        w1, w4 = gate
        w1 = jnp.transpose(w1, (1, 2, 0, 3, 4)).reshape(nl, wd, bw, 2, m)
        w4 = jnp.transpose(w4, (1, 2, 0, 3, 4)).reshape(nl, wd, 2, m, bw)
        w1 = jnp.where(core == 0, w1, w1[:, :, :, ::-1]).reshape(nl, wd, bw, m2)
        w4 = jnp.where(core == 0, w4, w4[:, :, ::-1]).reshape(nl, wd, m2, bw)
        w14s = (w1[None], w4[None])

    def slots_of(ups, downs):
        slots = [[ups[0]], [downs[1]]]
        slots += [[downs[k], ups[nl - k]] for k in range(2, nl - 1)]
        return slots + [[ups[1]], [ups[nl - 1], downs[nl - 1]]]

    metas = [meta_of((pos + k) % nl, 0) for k in range(nl)]
    metas[1] = meta_of((pos + 1) % nl, high_end)
    metas[nl - 1] = meta_of((pos + nl - 1) % nl, low_end)
    metas.append(meta_of(jnp.where(low_end, nl - 1, 0), 0))

    def first_factor(side, slots):
        owns, recvs = [], []
        for meta, xs in zip(metas, slots):
            mine_part, send = expand(side, meta, xs, w14s, hd, sub)
            owns.append(mine_part)
            recvs.append(swap(send, n))
        return owns, recvs

    x_slots, g_slots = slots_of(x_ups, x_downs), slots_of(g_ups, g_downs)
    owns, recvs = first_factor(0, x_slots)
    z_own, z_send, *saved = middle(False, metas[0], owns, recvs, w2, w3, [], dp, scale)
    z_recv = swap(z_send, n)
    places = ((pos + jnp.arange(nl)) % nl).astype(jnp.int32)
    outs = output_parts(places, z_own, z_recv, w14s, sub)
    layer_out = lax.psum_scatter(outs, "tensor", axis_index_groups=lines).T

    owns, recvs = first_factor(1, g_slots)
    dy_own, dy_send, *g23 = middle(True, metas[0], owns, recvs, w2, w3, saved, dp, scale)
    dy_recv = swap(dy_send, n)
    parts, grads = [None] * nl, None
    order = [k for pair in zip(range(nl - 1, nl // 2, -1), range(1, nl // 2)) for k in pair]
    for k in order + [nl // 2, 0]:
        late = k in (1, nl - 1)
        xs, gs = x_slots[k], g_slots[k]
        if late:
            xs = xs + [x_slots[nl][0 if k == 1 else 1]]
            gs = gs + [g_slots[nl][0 if k == 1 else 1]]
        parts[k], *grads = contract(
            k,
            metas[k],
            (z_own, z_recv, dy_own, dy_recv),
            w14s,
            xs,
            gs,
            late,
            grads,
            sub,
            dp,
            scale,
        )

    g1, g2, g3, g4 = reduce_dp(
        [grads[:2], g23[:2], g23[2:], grads[2:]], dp, (x_first, x_first, y_first, y_first)
    )
    g14 = jnp.stack([g1, g4], axis=1)
    g14 = lax.all_to_all(
        g14, "tensor", split_axis=0, concat_axis=0, axis_index_groups=lines, tiled=True
    )

    up, down = parts[nl - 1], parts[1]
    for r in range(1, nl):
        if r == nl - 1:
            up, down, g14 = lax.optimization_barrier((up, down, g14))
        up = lax.ppermute(up, "tensor", up_pairs(0, r))
        down = lax.ppermute(down, "tensor", down_pairs(nl - 1 - r, nl - 1))
        if r < nl - 1:
            up = add(up, parts[nl - 1 - r])
            down = add(down, parts[r + 1])
            up, down = lax.optimization_barrier((up, down))

    g2 = gather_dp(g2, dp, True)
    g3 = gather_dp(g3, dp, False)
    g1 = gather_dp(g14[:, 0], dp, True)
    g4 = gather_dp(g14[:, 1], dp, False)
    tokens_grad = close(parts[0], up, down)

    base = jnp.asarray(base, jnp.int32)[None]
    offset = jnp.arange(2 * nl, dtype=jnp.int32)
    wide_rows = (((offset // 2 + pos) % nl) * 2 + (offset + core) % 2) * part
    dual_rows = (jnp.arange(dp, dtype=jnp.int32) * step + core * m) % m2
    wide_tab = jnp.concatenate([base, wide_rows.astype(jnp.int32)])
    dual_tab = jnp.concatenate([base, dual_rows.astype(jnp.int32)])
    out_two = finish(wide_tab, [g[None] for g in g2], False)
    out_three = finish(wide_tab, [g[None] for g in g3], True)
    g1, g4, out_two, out_three = lax.optimization_barrier((g1, g4, out_two, out_three))
    return (
        layer_out,
        tokens_grad,
        finish(dual_tab, g1, True),
        out_two,
        out_three,
        finish(dual_tab, g4, False),
    )


def solution(mesh):
    return jax.shard_map(
        body,
        mesh=mesh,
        in_specs=(
            P("dp", "tensor"),
            P("dp", "tensor"),
            P("tensor", None, None),
            P("tensor", None, None),
            P("tensor", None, None),
            P("tensor", None, None),
        ),
        out_specs=(
            P("dp", "tensor"),
            P("dp", "tensor"),
            P("tensor", None, None),
            P("tensor", None, None),
            P("tensor", None, None),
            P("tensor", None, None),
        ),
        check_vma=False,
    )
```

time: 444 us -> 423 us (0.953)
  waiting for transfers between devices: 193 us -> 153 us
  local copies, waits for them, and re-layouts: 26.2 us -> 49 us
  other arithmetic: 38.1 us -> 18 us
  Pallas kernels: 82.5 us -> 97.4 us
    ppermute x32 -> x42, waiting for transfers between devices: 158 us -> 134 us  [the longest x3 42.8 us: body(): down = lax.ppermute(down, 'tensor', down_pairs(nl - 1 - r, nl - 1))]
    unnamed x63 -> x132, local copies, waits for them, and re-layouts: 14.5 us -> 35.1 us
    pallas_call x14 -> x23, Pallas kernels: 82.5 us -> 97.4 us  [the longest x2 30.6 us: middle(): pl.pallas_call(body, grid_spec=pltpu.PrefetchScalarGridSpec(num_scalar_pr...]
    convert_element_type x7, other arithmetic: 16.7 us -> 6.29 us  [add(): return (a.astype(F32) + b.astype(F32)).astype(BF16)]
    another operation x11 -> x2, other arithmetic: 11.1 us -> 0.82 us  [the longest x1 0.74 us: body(): jnp.stack([jnp.transpose(w1, (2, 0, 1, 3)), jnp.transpose(w4, (1, 0, 2, 3...]
    all_to_all x1, waiting for transfers between devices: 8.12 us -> 0.01 us  [body(): lax.all_to_all(g14, 'tensor', split_axis=0, concat_axis=0, axis_index_gro...]
    ppermute x32 -> x42, starting transfers between devices: 65.3 us -> 72.5 us  [the longest x6 20.4 us: hop(): down = lax.ppermute(downs[-1], 'tensor', down_pairs(0, nl - r))]
    ppermute x6 -> x12, waiting for transfers between devices: 9 us -> 1.99 us  [swap(): return lax.ppermute(val, 'tensor', [(i, i ^ 1) for i in range(n)])]
  transfers between devices with their start and end apart: 40 -> 57, of which waited for: 18 -> 22; matrix products, arithmetic and copies ran while one was open for 10% -> 8% of each run, Pallas kernels for 12% -> 23%
where the time goes in v4:
time: 423 us; the launch traced here: 419 us
  waiting for transfers between devices  153 us (36%)
  Pallas kernels  97.4 us (23%)
  starting transfers between devices  86.5 us (20%)
  local copies, waits for them, and re-layouts  49 us (12%)
  other arithmetic  18 us (4%)
  between operations  15.1 us (4%)
    ppermute x3, waiting for transfers between devices, body(): down = lax.ppermute(down, 'tensor', down_pairs(nl - 1 - r, nl - 1))  42.8 us
    unnamed x132, local copies, waits for them, and re-layouts  35.1 us
    pallas_call x2, Pallas kernels, middle(): pl.pallas_call(body, grid_spec=pltpu.PrefetchScalarGridSpec(num_scalar_pr...  30.6 us
    pallas_call x10, Pallas kernels, expand(): pl.pallas_call(functools.partial(expand_kernel, side=side, pa=pa, bw=bw,...  24.3 us
    ppermute x6, waiting for transfers between devices, hop(): up = lax.ppermute(ups[-1], 'tensor', up_pairs(r - 1, nl - 1))  23.4 us
    ppermute x4, waiting for transfers between devices, reduce_dp(): came = [lax.ppermute(g[1], 'dp', p[0]) for g, p in zip(grads, orders)]  21.5 us
    ppermute x6, starting transfers between devices, hop(): down = lax.ppermute(downs[-1], 'tensor', down_pairs(0, nl - r))  20.4 us
    pallas_call x4, Pallas kernels, finish(): pl.pallas_call(functools.partial(finish_kernel, dp=dp, piece=piece, flip=...  19.9 us
  transfers between devices with their start and end apart: 57, of which 22 were waited for; matrix products, arithmetic and copies ran while one was open for 8% of the time, Pallas kernels for 23%

profile of v4, /device:TPU:16, one launch (start us, length us, event | category | flops | bytes accessed | tf_op | source)
XLA Modules:
  0.0 419.1 jit_solution(17248437105543722405)
XLA Ops:
  12.6 5.2 %all-to-all-start = ((bf16[4,2,4,64,256]{4,3,2,1,0:T(8,128)(2,1)}), bf16[4,2,4,64,256]{4,3,2,1,0:T(8,128)(2,1)S(1)}, u32[]{:S(2)}, u32[]{:S(2)}) async-start(bf16[4,2,4,64,256]{4,3,2,1,0:T(8,128)(2,1)} %copy.46), calls=%async_computation | async-start | bytes 2097152 | tf_op jit(solution)/shard_map/all_to_all | solution.py:503
  24.3 17.1 %all-to-all-done.refs_0_ = bf16[4,2,4,64,256]{4,3,2,1,0:T(8,128)(2,1)S(1)} async-done(((bf16[4,2,4,64,256]{4,3,2,1,0:T(8,128)(2,1)}), bf16[4,2,4,64,256]{4,3,2,1,0:T(8,128)(2,1)S(1)}, u32[]{:S(2)}, u32[]{:S(2)}) %all-to-all-start) | async-done | bytes 1048608 | tf_op jit(solution)/shard_map/all_to_all | solution.py:503
  56.6 6.1 %collective-permute-done.1.refs_0_.refs_5_ = bf16[1024,512]{1,0:T(8,128)(2,1)S(1)} collective-permute-done((bf16[1024,512]{1,0:T(8,128)(2,1)S(1)}, bf16[1024,512]{1,0:T(8,128)(2,1)S(1)}, u32[]{:S(2)}, u32[]{:S(2)}) %collective-permute-start.1) | collective-permute-done | bytes 1048608 | tf_op jit(solution)/shard_map/ppermute | solution.py:537
  82.9 6.0 %collective-permute-done.6.refs_3_ = bf16[4,4,64,256]{3,2,1,0:T(8,128)(2,1)S(1)} collective-permute-done((bf16[4,4,64,256]{3,2,1,0:T(8,128)(2,1)}, bf16[4,4,64,256]{3,2,1,0:T(8,128)(2,1)S(1)}, u32[]{:S(2)}, u32[]{:S(2)}) %collective-permute-start.6) | collective-permute-done | bytes 524320 | tf_op jit(solution)/shard_map/ppermute | solution.py:548
  96.9 5.9 %collective-permute-start.17 = (bf16[1024,512]{1,0:T(8,128)(2,1)}, bf16[1024,512]{1,0:T(8,128)(2,1)}, u32[]{:S(2)}, u32[]{:S(2)}) collective-permute-start(bf16[1024,512]{1,0:T(8,128)(2,1)} %bitcast.20.refs_0_.refs_6_), channel_id=1, source_target_pairs={{2,0},{3,1},{4,2},{5,3},{6,4},{7,5},{10,8},{11,9},{12,10},{13,11},... | collective-permute-start | bytes 3145736 | tf_op jit(solution)/shard_map/ppermute | solution.py:537
  124.1 13.0 %collective-permute-done.16.refs_0_.refs_7_ = bf16[1024,512]{1,0:T(8,128)(2,1)} collective-permute-done((bf16[1024,512]{1,0:T(8,128)(2,1)}, bf16[1024,512]{1,0:T(8,128)(2,1)}, u32[]{:S(2)}, u32[]{:S(2)}) %collective-permute-start.16) | collective-permute-done | bytes 1048608 | tf_op jit(solution)/shard_map/ppermute | solution.py:536
  137.1 5.7 %collective-permute-start.19 = (bf16[1024,512]{1,0:T(8,128)(2,1)}, bf16[1024,512]{1,0:T(8,128)(2,1)}, u32[]{:S(2)}, u32[]{:S(2)}) collective-permute-start(bf16[1024,512]{1,0:T(8,128)(2,1)} %collective-permute-done.17.refs_0_.refs_7_), channel_id=1, source_target_pairs={{2,0},{3,1},{4,2},{5,3},{10,8},{11,9},{12,10},{13,11},{18,16},{19,... | collective-permute-start | bytes 3145736 | tf_op jit(solution)/shard_map/ppermute | solution.py:537
  146.0 14.8 %forward.1 = (bf16[16,128,512]{2,1,0:T(8,128)(2,1)}, bf16[16,128,512]{2,1,0:T(8,128)(2,1)}, bf16[16,256,512]{2,1,0:T(8,128)(2,1)}, bf16[16,256,512]{2,1,0:T(8,128)(2,1)}, bf16[16,256,512]{2,1,0:T(8,128)(2,1)}) custom-call(s32[12]{0:T(128)} %copy-done.47, bf16[16,32,512]{2,1,0:T(8,128)(2,1)} %copy-done.44, bf16[16,32,512]{2,1,0:T(8,128)(2,1)} %copy-done.43, ...), custom_call_target="tpu_custom_call" | custom-call | flops 2147483648 | bytes 25165824 | tf_op jit(solution)/shard_map/forward/pallas_call | solution.py:211
  160.9 4.0 collective-permute-done.19.refs_0_.refs_7_
  164.8 5.1 %collective-permute-done.18.refs_1_.refs_8_ = bf16[1024,512]{1,0:T(8,128)(2,1)} collective-permute-done((bf16[1024,512]{1,0:T(8,128)(2,1)}, bf16[1024,512]{1,0:T(8,128)(2,1)}, u32[]{:S(2)}, u32[]{:S(2)}) %collective-permute-start.18) | collective-permute-done | bytes 1048608 | tf_op jit(solution)/shard_map/ppermute | solution.py:536
  205.5 15.8 %backward.1 = (bf16[16,128,512]{2,1,0:T(8,128)(2,1)}, bf16[16,128,512]{2,1,0:T(8,128)(2,1)}, bf16[2,16,64,256]{3,2,1,0:T(8,128)(2,1)}, bf16[2,16,64,256]{3,2,1,0...) custom-call(s32[12]{0:T(128)} %copy-done.47, bf16[16,32,512]{2,1,0:T(8,128)(2,1)} %copy-done.35, ...), custom_call_target="tpu_custom_call" | custom-call | flops 4294967296 | bytes 29360128 | tf_op jit(solution)/shard_map/backward/pallas_call | solution.py:211
  251.2 20.5 %collective-permute-done.32 = bf16[2,4,4,64,256]{4,3,2,1,0:T(8,128)(2,1)S(1)} collective-permute-done((bf16[2,4,4,64,256]{4,3,2,1,0:T(8,128)(2,1)S(1)}, bf16[2,4,4,64,256]{4,3,2,1,0:T(8,128)(2,1)S(1)}, u32[]{:S(2)}, u32[]{:S(2)}) %collective-permute-start.32) | collective-permute-done | bytes 1048608 | tf_op jit(solution)/shard_map/ppermute | solution.py:437
  275.7 23.2 %collective-permute-done.29 = bf16[1024,512]{1,0:T(8,128)(2,1)S(1)} collective-permute-done((bf16[1024,512]{1,0:T(8,128)(2,1)S(1)}, bf16[1024,512]{1,0:T(8,128)(2,1)S(1)}, u32[]{:S(2)}, u32[]{:S(2)}) %collective-permute-start.29) | collective-permute-done | bytes 1048608 | tf_op jit(solution)/shard_map/ppermute | solution.py:635
  304.2 6.6 %all-to-all-start.1 = ((bf16[4,2,4,64,256]{4,3,2,1,0:T(8,128)(2,1)}), bf16[4,2,4,64,256]{4,3,2,1,0:T(8,128)(2,1)}, u32[]{:S(2)}, u32[]{:S(2)}) async-start(bf16[4,2,4,64,256]{4,3,2,1,0:T(8,128)(2,1)} %copy.53), calls=%async_computation.2 | async-start | bytes 2097152 | tf_op jit(solution)/shard_map/all_to_all | solution.py:626
  319.8 9.6 %collective-permute-done.30 = bf16[1024,512]{1,0:T(8,128)(2,1)} collective-permute-done((bf16[1024,512]{1,0:T(8,128)(2,1)}, bf16[1024,512]{1,0:T(8,128)(2,1)}, u32[]{:S(2)}, u32[]{:S(2)}) %collective-permute-start.30) | collective-permute-done | bytes 1048608 | tf_op jit(solution)/shard_map/ppermute | solution.py:634
  335.5 19.6 %collective-permute-done.31 = bf16[1024,512]{1,0:T(8,128)(2,1)S(1)} collective-permute-done((bf16[1024,512]{1,0:T(8,128)(2,1)}, bf16[1024,512]{1,0:T(8,128)(2,1)S(1)}, u32[]{:S(2)}, u32[]{:S(2)}) %collective-permute-start.31) | collective-permute-done | bytes 1048608 | tf_op jit(solution)/shard_map/ppermute | solution.py:635
  363.8 4.3 %collective-permute-start.39 = (bf16[1024,512]{1,0:T(8,128)(2,1)}, bf16[1024,512]{1,0:T(8,128)(2,1)}, u32[]{:S(2)}, u32[]{:S(2)}) collective-permute-start(bf16[1024,512]{1,0:T(8,128)(2,1)} %add_convert_fusion), channel_id=1, source_target_pairs={{2,0},{3,1},{4,2},{5,3},{6,4},{7,5},{10,8},{11,9},{12,10},{13,11},... | collective-permute-start | bytes 3145736 | tf_op jit(solution)/shard_map/ppermute | solution.py:635
  368.0 5.4 %collective-permute-done.44.refs_2_ = bf16[4,4,64,256]{3,2,1,0:T(8,128)(2,1)S(1)} collective-permute-done((bf16[4,4,64,256]{3,2,1,0:T(8,128)(2,1)S(1)}, bf16[4,4,64,256]{3,2,1,0:T(8,128)(2,1)S(1)}, u32[]{:S(2)}, u32[]{:S(2)}) %collective-permute-start.44) | collective-permute-done | bytes 524320 | tf_op jit(solution)/shard_map/ppermute | solution.py:452
  375.7 9.1 %collective-permute-done.41.refs_2_ = bf16[4,4,64,256]{3,2,1,0:T(8,128)(2,1)} collective-permute-done((bf16[4,4,64,256]{3,2,1,0:T(8,128)(2,1)}, bf16[4,4,64,256]{3,2,1,0:T(8,128)(2,1)}, u32[]{:S(2)}, u32[]{:S(2)}) %collective-permute-start.41) | collective-permute-done | bytes 524320 | tf_op jit(solution)/shard_map/ppermute | solution.py:452
  385.4 5.2 %finish.5 = f32[16,256,256]{2,1,0:T(8,128)} custom-call(s32[9]{0:T(128)S(1)} %pad_add_fusion.2.tab, bf16[1,16,64,256]{3,2,1,0:T(8,128)(2,1)S(1)} %bitcast.93, bf16[1,16,64,256]{3,2,1,0:T(8,128)(2,1)} %bitcast.46.refs_1_, bf16[1,16,64,256]{3,2,1,0:T(8,128)(2,1)} %bitcast.47.refs_2_, bf16[1,16,64,256]{3,2,1,0:T(8,128)(2,1)S(1)} %bitcast.95), custom_call_target="tpu_custom_call" | custom-call | bytes 6291456 | tf_op jit(solution)/shard_map/finish/pallas_call | solution.py:378
  390.6 4.6 %finish.4 = f32[16,256,256]{2,1,0:T(8,128)} custom-call(s32[9]{0:T(128)S(1)} %pad_add_fusion.2.tab, bf16[1,16,64,256]{3,2,1,0:T(8,128)(2,1)S(1)} %bitcast.92, bf16[1,16,64,256]{3,2,1,0:T(8,128)(2,1)} %bitcast.41.refs_1_, bf16[1,16,64,256]{3,2,1,0:T(8,128)(2,1)} %bitcast.42.refs_2_, bf16[1,16,64,256]{3,2,1,0:T(8,128)(2,1)S(1)} %bitcast.94), custom_call_target="tpu_custom_call" | custom-call | bytes 6291456 | tf_op jit(solution)/shard_map/finish/pallas_call | solution.py:378
  395.9 5.5 %finish.6 = f32[4,256,1024]{2,1,0:T(8,128)} custom-call(s32[5]{0:T(128)S(1)} %pad_add_fusion.1.tab, bf16[4,4,64,256]{3,2,1,0:T(8,128)(2,1)} %get-tuple-element.174.refs_0_, bf16[4,4,64,256]{3,2,1,0:T(8,128)(2,1)} %collective-permute-done.40.refs_1_, bf16[4,4,64,256]{3,2,1,0:T(8,128)(2,1)} %collective-permute-done.41.refs_2_, ...), custom_call_target="tpu_custom_call" | custom-call | bytes 6291456 | tf_op jit(solution)/shard_map/finish/pallas_call | solution.py:378
  401.4 4.6 %finish.7 = f32[4,1024,256]{2,1,0:T(8,128)} custom-call(s32[5]{0:T(128)S(1)} %pad_add_fusion.1.tab, bf16[4,4,64,256]{3,2,1,0:T(8,128)(2,1)S(1)} %copy-done.22, bf16[4,4,64,256]{3,2,1,0:T(8,128)(2,1)} %collective-permute-done.43.refs_1_, bf16[4,4,64,256]{3,2,1,0:T(8,128)(2,1)S(1)} %copy-done.37, bf16[4,4,64,256]{3,2,1,0:T(8,128)(2,1)} %collective-permute-done.45.refs_3_), custom_call_target="tpu_custom_call" | custom-call | bytes 6291456 | tf_op jit(solution)/shard_map/finish/pallas_call | solution.py:378
  406.0 4.0 close.1
  (284 shorter events, 183.2 us)
Async XLA Ops:
  12.6 28.7 %all-to-all-start = ((bf16[4,2,4,64,256]{4,3,2,1,0:T(8,128)(2,1)}), bf16[4,2,4,64,256]{4,3,2,1,0:T(8,128)(2,1)S(1)}, u32[]{:S(2)}, u32[]{:S(2)}) async-start(bf16[4,2,4,64,256]{4,3,2,1,0:T(8,128)(2,1)} %copy.46), calls=%async_computation | async-start | bytes 2097152 | tf_op jit(solution)/shard_map/all_to_all | solution.py:503
  17.8 392.2 %reduce-scatter.2.cloned.1.call-start = ((), (), s32[]{:S(2)}) async-start(), calls=%async_computation.3 | async-start | bytes 5242880 | tf_op jit(solution)/shard_map/reduce_scatter | solution.py:595
  18.4 44.3 %collective-permute-start.1 = (bf16[1024,512]{1,0:T(8,128)(2,1)S(1)}, bf16[1024,512]{1,0:T(8,128)(2,1)S(1)}, u32[]{:S(2)}, u32[]{:S(2)}) collective-permute-start(bf16[1024,512]{1,0:T(8,128)(2,1)S(1)} %bitcast.88), channel_id=1, source_target_pairs={{2,0},{3,1},{4,2},{5,3},{6,4},{7,5},{10,8},{11,9},{12,10},{13,11},... | collective-permute-start | bytes 3145736 | tf_op jit(solution)/shard_map/ppermute | solution.py:537
  20.9 42.9 %collective-permute-start = (bf16[1024,512]{1,0:T(8,128)(2,1)S(1)}, bf16[1024,512]{1,0:T(8,128)(2,1)}, u32[]{:S(2)}, u32[]{:S(2)}) collective-permute-start(bf16[1024,512]{1,0:T(8,128)(2,1)S(1)} %bitcast.89), channel_id=1, source_target_pairs={{0,2},{1,3},{2,4},{3,5},{4,6},{5,7},{8,10},{9,11},{10,12},{11,13},... | collective-permute-start | bytes 3145736 | tf_op jit(solution)/shard_map/ppermute | solution.py:536
  102.8 34.3 %collective-permute-start.16 = (bf16[1024,512]{1,0:T(8,128)(2,1)}, bf16[1024,512]{1,0:T(8,128)(2,1)}, u32[]{:S(2)}, u32[]{:S(2)}) collective-permute-start(bf16[1024,512]{1,0:T(8,128)(2,1)} %bitcast.20.refs_0_.refs_6_), channel_id=1, source_target_pairs={{0,2},{1,3},{2,4},{3,5},{4,6},{5,7},{8,10},{9,11},{10,12},{11,13},... | collective-permute-start | bytes 3145736 | tf_op jit(solution)/shard_map/ppermute | solution.py:536
  137.1 27.7 %collective-permute-start.19 = (bf16[1024,512]{1,0:T(8,128)(2,1)}, bf16[1024,512]{1,0:T(8,128)(2,1)}, u32[]{:S(2)}, u32[]{:S(2)}) collective-permute-start(bf16[1024,512]{1,0:T(8,128)(2,1)} %collective-permute-done.17.refs_0_.refs_7_), channel_id=1, source_target_pairs={{2,0},{3,1},{4,2},{5,3},{10,8},{11,9},{12,10},{13,11},{18,16},{19,... | collective-permute-start | bytes 3145736 | tf_op jit(solution)/shard_map/ppermute | solution.py:537
  142.9 27.0 %collective-permute-start.18 = (bf16[1024,512]{1,0:T(8,128)(2,1)}, bf16[1024,512]{1,0:T(8,128)(2,1)}, u32[]{:S(2)}, u32[]{:S(2)}) collective-permute-start(bf16[1024,512]{1,0:T(8,128)(2,1)} %collective-permute-done.16.refs_0_.refs_7_), channel_id=1, source_target_pairs={{2,4},{3,5},{4,6},{5,7},{10,12},{11,13},{12,14},{13,15},{18,20},{1... | collective-permute-start | bytes 3145736 | tf_op jit(solution)/shard_map/ppermute | solution.py:536
  160.8 36.9 %collective-permute-start.15 = (bf16[16,128,512]{2,1,0:T(8,128)(2,1)}, bf16[16,128,512]{2,1,0:T(8,128)(2,1)S(1)}, u32[]{:S(2)}, u32[]{:S(2)}) collective-permute-start(bf16[16,128,512]{2,1,0:T(8,128)(2,1)} %get-tuple-element.116), channel_id=1, source_target_pairs={{0,1},{1,0},{2,3},{3,2},{4,5},{5,4},{6,7},{7,6},{8,9},{9,8},{10,11... | collective-permute-start | bytes 6291464 | tf_op jit(solution)/shard_map/ppermute | solution.py:423
  221.4 28.6 %collective-permute-start.33 = (bf16[2,16,64,256]{3,2,1,0:T(8,128)(2,1)}, bf16[2,16,64,256]{3,2,1,0:T(8,128)(2,1)S(1)}, u32[]{:S(2)}, u32[]{:S(2)}) collective-permute-start(bf16[2,16,64,256]{3,2,1,0:T(8,128)(2,1)} %get-tuple-element.162), channel_id=1, source_target_pairs={{0,8},{8,0},{16,24},{24,16},{1,9},{9,1},{17,25},{25,17},{2,10},{10... | collective-permute-start | bytes 3145736 | tf_op jit(solution)/shard_map/ppermute | solution.py:437
  223.0 28.0 %collective-permute-start.34 = (bf16[2,16,64,256]{3,2,1,0:T(8,128)(2,1)}, bf16[2,16,64,256]{3,2,1,0:T(8,128)(2,1)S(1)}, u32[]{:S(2)}, u32[]{:S(2)}) collective-permute-start(bf16[2,16,64,256]{3,2,1,0:T(8,128)(2,1)} %get-tuple-element.164), channel_id=1, source_target_pairs={{0,16},{8,24},{16,0},{24,8},{1,17},{9,25},{17,1},{25,9},{2,18},{10... | collective-permute-start | bytes 3145736 | tf_op jit(solution)/shard_map/ppermute | solution.py:437
  248.7 50.1 %collective-permute-start.29 = (bf16[1024,512]{1,0:T(8,128)(2,1)S(1)}, bf16[1024,512]{1,0:T(8,128)(2,1)S(1)}, u32[]{:S(2)}, u32[]{:S(2)}) collective-permute-start(bf16[1024,512]{1,0:T(8,128)(2,1)S(1)} %get-tuple-element.154), channel_id=1, source_target_pairs={{6,4},{7,5},{14,12},{15,13},{22,20},{23,21},{30,28},{31,29}} | collective-permute-start | bytes 3145736 | tf_op jit(solution)/shard_map/ppermute | solution.py:635
  250.1 49.2 %collective-permute-start.28 = (bf16[1024,512]{1,0:T(8,128)(2,1)S(1)}, bf16[1024,512]{1,0:T(8,128)(2,1)S(1)}, u32[]{:S(2)}, u32[]{:S(2)}) collective-permute-start(bf16[1024,512]{1,0:T(8,128)(2,1)S(1)} %get-tuple-element.152), channel_id=1, source_target_pairs={{0,2},{1,3},{8,10},{9,11},{16,18},{17,19},{24,26},{25,27}} | collective-permute-start | bytes 3145736 | tf_op jit(solution)/shard_map/ppermute | solution.py:634
  273.1 29.3 %collective-permute-start.36 = (bf16[4,4,64,256]{3,2,1,0:T(8,128)(2,1)S(1)}, bf16[4,4,64,256]{3,2,1,0:T(8,128)(2,1)S(1)}, u32[]{:S(2)}, u32[]{:S(2)}) collective-permute-start(bf16[4,4,64,256]{3,2,1,0:T(8,128)(2,1)S(1)} %fusion.8), channel_id=1, source_target_pairs={{0,16},{8,24},{16,0},{24,8},{1,17},{9,25},{17,1},{25,9},{2,18},{10... | collective-permute-start | bytes 1572872 | tf_op jit(solution)/shard_map/ppermute | solution.py:440
  273.9 28.7 %collective-permute-start.37 = (bf16[4,4,64,256]{3,2,1,0:T(8,128)(2,1)S(1)}, bf16[4,4,64,256]{3,2,1,0:T(8,128)(2,1)S(1)}, u32[]{:S(2)}, u32[]{:S(2)}) collective-permute-start(bf16[4,4,64,256]{3,2,1,0:T(8,128)(2,1)S(1)} %fusion.11), channel_id=1, source_target_pairs={{0,8},{8,0},{16,24},{24,16},{1,9},{9,1},{17,25},{25,17},{2,10},{10... | collective-permute-start | bytes 1572872 | tf_op jit(solution)/shard_map/ppermute | solution.py:440
  274.4 39.0 %collective-permute-start.46 = (bf16[16,64,256]{2,1,0:T(8,128)(2,1)S(1)}, bf16[16,64,256]{2,1,0:T(8,128)(2,1)}, u32[]{:S(2)}, u32[]{:S(2)}) collective-permute-start(bf16[16,64,256]{2,1,0:T(8,128)(2,1)S(1)} %fusion.9), channel_id=1, source_target_pairs={{0,16},{8,24},{16,0},{24,8},{1,17},{9,25},{17,1},{25,9},{2,18},{10... | collective-permute-start | bytes 1572872 | tf_op jit(solution)/shard_map/ppermute | solution.py:440
  301.1 28.3 %collective-permute-start.30 = (bf16[1024,512]{1,0:T(8,128)(2,1)}, bf16[1024,512]{1,0:T(8,128)(2,1)}, u32[]{:S(2)}, u32[]{:S(2)}) collective-permute-start(bf16[1024,512]{1,0:T(8,128)(2,1)} %get-tuple-element.155), channel_id=1, source_target_pairs={{0,2},{1,3},{2,4},{3,5},{8,10},{9,11},{10,12},{11,13},{16,18},{17,... | collective-permute-start | bytes 3145736 | tf_op jit(solution)/shard_map/ppermute | solution.py:634
  304.2 52.3 %all-to-all-start.1 = ((bf16[4,2,4,64,256]{4,3,2,1,0:T(8,128)(2,1)}), bf16[4,2,4,64,256]{4,3,2,1,0:T(8,128)(2,1)}, u32[]{:S(2)}, u32[]{:S(2)}) async-start(bf16[4,2,4,64,256]{4,3,2,1,0:T(8,128)(2,1)} %copy.53), calls=%async_computation.2 | async-start | bytes 2097152 | tf_op jit(solution)/shard_map/all_to_all | solution.py:626
  310.9 44.3 %collective-permute-start.31 = (bf16[1024,512]{1,0:T(8,128)(2,1)}, bf16[1024,512]{1,0:T(8,128)(2,1)S(1)}, u32[]{:S(2)}, u32[]{:S(2)}) collective-permute-start(bf16[1024,512]{1,0:T(8,128)(2,1)} %get-tuple-element.156), channel_id=1, source_target_pairs={{4,2},{5,3},{6,4},{7,5},{12,10},{13,11},{14,12},{15,13},{20,18},{2... | collective-permute-start | bytes 3145736 | tf_op jit(solution)/shard_map/ppermute | solution.py:635
  319.2 40.4 %collective-permute-start.47 = (bf16[16,64,256]{2,1,0:T(8,128)(2,1)S(1)}, bf16[16,64,256]{2,1,0:T(8,128)(2,1)}, u32[]{:S(2)}, u32[]{:S(2)}) collective-permute-start(bf16[16,64,256]{2,1,0:T(8,128)(2,1)S(1)} %fusion.5), channel_id=1, source_target_pairs={{0,8},{8,0},{16,24},{24,16},{1,9},{9,1},{17,25},{25,17},{2,10},{10... | collective-permute-start | bytes 1572872 | tf_op jit(solution)/shard_map/ppermute | solution.py:451
  329.4 30.6 %collective-permute-start.52 = (bf16[16,64,256]{2,1,0:T(8,128)(2,1)S(1)}, bf16[16,64,256]{2,1,0:T(8,128)(2,1)}, u32[]{:S(2)}, u32[]{:S(2)}) collective-permute-start(bf16[16,64,256]{2,1,0:T(8,128)(2,1)S(1)} %fusion.4), channel_id=1, source_target_pairs={{0,16},{8,24},{16,0},{24,8},{1,17},{9,25},{17,1},{25,9},{2,18},{10... | collective-permute-start | bytes 1572872 | tf_op jit(solution)/shard_map/ppermute | solution.py:452
  333.2 27.8 %collective-permute-start.49 = (bf16[16,64,256]{2,1,0:T(8,128)(2,1)}, bf16[16,64,256]{2,1,0:T(8,128)(2,1)S(1)}, u32[]{:S(2)}, u32[]{:S(2)}) collective-permute-start(bf16[16,64,256]{2,1,0:T(8,128)(2,1)} %collective-permute-done.48), channel_id=1, source_target_pairs={{0,8},{8,0},{16,24},{24,16},{1,9},{9,1},{17,25},{25,17},{2,10},{10... | collective-permute-start | bytes 1572872 | tf_op jit(solution)/shard_map/ppermute | solution.py:454
  334.7 29.0 %collective-permute-start.53 = (bf16[16,64,256]{2,1,0:T(8,128)(2,1)}, bf16[16,64,256]{2,1,0:T(8,128)(2,1)S(1)}, u32[]{:S(2)}, u32[]{:S(2)}) collective-permute-start(bf16[16,64,256]{2,1,0:T(8,128)(2,1)} %collective-permute-done.51), channel_id=1, source_target_pairs={{0,16},{8,24},{16,0},{24,8},{1,17},{9,25},{17,1},{25,9},{2,18},{10... | collective-permute-start | bytes 1572872 | tf_op jit(solution)/shard_map/ppermute | solution.py:456
  361.8 44.2 %collective-permute-start.38 = (bf16[1024,512]{1,0:T(8,128)(2,1)}, bf16[1024,512]{1,0:T(8,128)(2,1)}, u32[]{:S(2)}, u32[]{:S(2)}) collective-permute-start(bf16[1024,512]{1,0:T(8,128)(2,1)} %add_convert_fusion.1), channel_id=1, source_target_pairs={{0,2},{1,3},{2,4},{3,5},{4,6},{5,7},{8,10},{9,11},{10,12},{11,13},... | collective-permute-start | bytes 3145736 | tf_op jit(solution)/shard_map/ppermute | solution.py:634
  363.8 42.3 %collective-permute-start.39 = (bf16[1024,512]{1,0:T(8,128)(2,1)}, bf16[1024,512]{1,0:T(8,128)(2,1)}, u32[]{:S(2)}, u32[]{:S(2)}) collective-permute-start(bf16[1024,512]{1,0:T(8,128)(2,1)} %add_convert_fusion), channel_id=1, source_target_pairs={{2,0},{3,1},{4,2},{5,3},{6,4},{7,5},{10,8},{11,9},{12,10},{13,11},... | collective-permute-start | bytes 3145736 | tf_op jit(solution)/shard_map/ppermute | solution.py:635
  (96 other events, 1069.7 us)
Sparse Core Ops, SparseCore 0:
  205.6 100.4 reduce-scatter.1

commit v5 on v4

--- a/solution.py
+++ b/solution.py
@@ -185,7 +185,7 @@
     hd, k, j = w2.shape
     nl = len(owns) - 1
     _, part, rows = owns[0].shape
-    hb = 2
+    hb = 4
     half = dp // 2
     slot = pl.BlockSpec((hb, part, rows), lambda b, meta: (b, 0, 0))
     one = pl.BlockSpec((hb, nl * part, rows), lambda b, meta: (b, 0, 0))
@@ -361,7 +361,7 @@
     size = dp * step
     pieces = tab.shape[0] - 1
     piece = size // pieces
-    count = min(wd, 4)
+    count = min(wd, 8)
     if flip and size % 128:
         base = tab[0]
         merged = jnp.stack(shares)[jnp.arange(dp) ^ base]

time: 423 us -> 422 us (level)
  transfers between devices with their start and end apart: 57 -> 57, of which waited for: 22 -> 23; matrix products, arithmetic and copies ran while one was open for 8% -> 8% of each run, Pallas kernels for 23% -> 22%
where the time goes in v5:
time: 422 us; the launch traced here: 418 us
  waiting for transfers between devices  155 us (37%)
  Pallas kernels  93.4 us (22%)
  starting transfers between devices  87.4 us (21%)
  local copies, waits for them, and re-layouts  49 us (12%)
  other arithmetic  18 us (4%)
  between operations  15.1 us (4%)
    ppermute x3, waiting for transfers between devices, body(): down = lax.ppermute(down, 'tensor', down_pairs(nl - 1 - r, nl - 1))  42.7 us
    unnamed x132, local copies, waits for them, and re-layouts  35.1 us
    pallas_call x2, Pallas kernels, middle(): pl.pallas_call(body, grid_spec=pltpu.PrefetchScalarGridSpec(num_scalar_pr...  28.4 us
    pallas_call x10, Pallas kernels, expand(): pl.pallas_call(functools.partial(expand_kernel, side=side, pa=pa, bw=bw,...  24.3 us
    ppermute x6, waiting for transfers between devices, hop(): up = lax.ppermute(ups[-1], 'tensor', up_pairs(r - 1, nl - 1))  23.4 us
    ppermute x4, waiting for transfers between devices, reduce_dp(): came = [lax.ppermute(g[1], 'dp', p[0]) for g, p in zip(grads, orders)]  21.8 us
    ppermute x6, starting transfers between devices, hop(): down = lax.ppermute(downs[-1], 'tensor', down_pairs(0, nl - r))  20.4 us
    pallas_call x4, Pallas kernels, finish(): pl.pallas_call(functools.partial(finish_kernel, dp=dp, piece=piece, flip=...  18.1 us
  transfers between devices with their start and end apart: 57, of which 23 were waited for; matrix products, arithmetic and copies ran while one was open for 8% of the time, Pallas kernels for 22%

profile of v5, /device:TPU:16, one launch (start us, length us, event | category | flops | bytes accessed | tf_op | source)
XLA Modules:
  0.0 417.7 jit_solution(9884129341450241695)
XLA Ops:
  12.6 5.2 %all-to-all-start = ((bf16[4,2,4,64,256]{4,3,2,1,0:T(8,128)(2,1)}), bf16[4,2,4,64,256]{4,3,2,1,0:T(8,128)(2,1)S(1)}, u32[]{:S(2)}, u32[]{:S(2)}) async-start(bf16[4,2,4,64,256]{4,3,2,1,0:T(8,128)(2,1)} %copy.46), calls=%async_computation | async-start | bytes 2097152 | tf_op jit(solution)/shard_map/all_to_all | solution.py:503
  24.3 17.1 %all-to-all-done.refs_0_ = bf16[4,2,4,64,256]{4,3,2,1,0:T(8,128)(2,1)S(1)} async-done(((bf16[4,2,4,64,256]{4,3,2,1,0:T(8,128)(2,1)}), bf16[4,2,4,64,256]{4,3,2,1,0:T(8,128)(2,1)S(1)}, u32[]{:S(2)}, u32[]{:S(2)}) %all-to-all-start) | async-done | bytes 1048608 | tf_op jit(solution)/shard_map/all_to_all | solution.py:503
  56.6 6.1 %collective-permute-done.1.refs_0_.refs_5_ = bf16[1024,512]{1,0:T(8,128)(2,1)S(1)} collective-permute-done((bf16[1024,512]{1,0:T(8,128)(2,1)S(1)}, bf16[1024,512]{1,0:T(8,128)(2,1)S(1)}, u32[]{:S(2)}, u32[]{:S(2)}) %collective-permute-start.1) | collective-permute-done | bytes 1048608 | tf_op jit(solution)/shard_map/ppermute | solution.py:537
  82.9 6.0 %collective-permute-done.6.refs_3_ = bf16[4,4,64,256]{3,2,1,0:T(8,128)(2,1)S(1)} collective-permute-done((bf16[4,4,64,256]{3,2,1,0:T(8,128)(2,1)}, bf16[4,4,64,256]{3,2,1,0:T(8,128)(2,1)S(1)}, u32[]{:S(2)}, u32[]{:S(2)}) %collective-permute-start.6) | collective-permute-done | bytes 524320 | tf_op jit(solution)/shard_map/ppermute | solution.py:548
  96.9 5.9 %collective-permute-start.17 = (bf16[1024,512]{1,0:T(8,128)(2,1)}, bf16[1024,512]{1,0:T(8,128)(2,1)}, u32[]{:S(2)}, u32[]{:S(2)}) collective-permute-start(bf16[1024,512]{1,0:T(8,128)(2,1)} %bitcast.20.refs_0_.refs_6_), channel_id=1, source_target_pairs={{2,0},{3,1},{4,2},{5,3},{6,4},{7,5},{10,8},{11,9},{12,10},{13,11},... | collective-permute-start | bytes 3145736 | tf_op jit(solution)/shard_map/ppermute | solution.py:537
  124.1 13.0 %collective-permute-done.16.refs_0_.refs_7_ = bf16[1024,512]{1,0:T(8,128)(2,1)} collective-permute-done((bf16[1024,512]{1,0:T(8,128)(2,1)}, bf16[1024,512]{1,0:T(8,128)(2,1)}, u32[]{:S(2)}, u32[]{:S(2)}) %collective-permute-start.16) | collective-permute-done | bytes 1048608 | tf_op jit(solution)/shard_map/ppermute | solution.py:536
  137.1 5.7 %collective-permute-start.19 = (bf16[1024,512]{1,0:T(8,128)(2,1)}, bf16[1024,512]{1,0:T(8,128)(2,1)}, u32[]{:S(2)}, u32[]{:S(2)}) collective-permute-start(bf16[1024,512]{1,0:T(8,128)(2,1)} %collective-permute-done.17.refs_0_.refs_7_), channel_id=1, source_target_pairs={{2,0},{3,1},{4,2},{5,3},{10,8},{11,9},{12,10},{13,11},{18,16},{19,... | collective-permute-start | bytes 3145736 | tf_op jit(solution)/shard_map/ppermute | solution.py:537
  146.0 14.0 %forward.1 = (bf16[16,128,512]{2,1,0:T(8,128)(2,1)}, bf16[16,128,512]{2,1,0:T(8,128)(2,1)}, bf16[16,256,512]{2,1,0:T(8,128)(2,1)}, bf16[16,256,512]{2,1,0:T(8,128)(2,1)}, bf16[16,256,512]{2,1,0:T(8,128)(2,1)}) custom-call(s32[12]{0:T(128)} %copy-done.47, bf16[16,32,512]{2,1,0:T(8,128)(2,1)} %copy-done.44, bf16[16,32,512]{2,1,0:T(8,128)(2,1)} %copy-done.43, ...), custom_call_target="tpu_custom_call" | custom-call | flops 2147483648 | bytes 25165824 | tf_op jit(solution)/shard_map/forward/pallas_call | solution.py:211
  160.0 4.8 %collective-permute-done.19.refs_0_.refs_7_ = bf16[1024,512]{1,0:T(8,128)(2,1)} collective-permute-done((bf16[1024,512]{1,0:T(8,128)(2,1)}, bf16[1024,512]{1,0:T(8,128)(2,1)}, u32[]{:S(2)}, u32[]{:S(2)}) %collective-permute-start.19) | collective-permute-done | bytes 1048608 | tf_op jit(solution)/shard_map/ppermute | solution.py:537
  164.8 5.1 %collective-permute-done.18.refs_1_.refs_8_ = bf16[1024,512]{1,0:T(8,128)(2,1)} collective-permute-done((bf16[1024,512]{1,0:T(8,128)(2,1)}, bf16[1024,512]{1,0:T(8,128)(2,1)}, u32[]{:S(2)}, u32[]{:S(2)}) %collective-permute-start.18) | collective-permute-done | bytes 1048608 | tf_op jit(solution)/shard_map/ppermute | solution.py:536
  190.9 4.0 collective-permute-done.20.refs_0_.refs_8_
  205.5 14.5 %backward.1 = (bf16[16,128,512]{2,1,0:T(8,128)(2,1)}, bf16[16,128,512]{2,1,0:T(8,128)(2,1)}, bf16[2,16,64,256]{3,2,1,0:T(8,128)(2,1)}, bf16[2,16,64,256]{3,2,1,0...) custom-call(s32[12]{0:T(128)} %copy-done.47, bf16[16,32,512]{2,1,0:T(8,128)(2,1)} %copy-done.35, ...), custom_call_target="tpu_custom_call" | custom-call | flops 4294967296 | bytes 29360128 | tf_op jit(solution)/shard_map/backward/pallas_call | solution.py:211
  249.5 20.7 %collective-permute-done.32 = bf16[2,4,4,64,256]{4,3,2,1,0:T(8,128)(2,1)S(1)} collective-permute-done((bf16[2,4,4,64,256]{4,3,2,1,0:T(8,128)(2,1)S(1)}, bf16[2,4,4,64,256]{4,3,2,1,0:T(8,128)(2,1)S(1)}, u32[]{:S(2)}, u32[]{:S(2)}) %collective-permute-start.32) | collective-permute-done | bytes 1048608 | tf_op jit(solution)/shard_map/ppermute | solution.py:437
  274.3 22.9 %collective-permute-done.29 = bf16[1024,512]{1,0:T(8,128)(2,1)S(1)} collective-permute-done((bf16[1024,512]{1,0:T(8,128)(2,1)S(1)}, bf16[1024,512]{1,0:T(8,128)(2,1)S(1)}, u32[]{:S(2)}, u32[]{:S(2)}) %collective-permute-start.29) | collective-permute-done | bytes 1048608 | tf_op jit(solution)/shard_map/ppermute | solution.py:635
  302.7 7.2 %all-to-all-start.1 = ((bf16[4,2,4,64,256]{4,3,2,1,0:T(8,128)(2,1)}), bf16[4,2,4,64,256]{4,3,2,1,0:T(8,128)(2,1)}, u32[]{:S(2)}, u32[]{:S(2)}) async-start(bf16[4,2,4,64,256]{4,3,2,1,0:T(8,128)(2,1)} %copy.53), calls=%async_computation.2 | async-start | bytes 2097152 | tf_op jit(solution)/shard_map/all_to_all | solution.py:626
  318.8 9.0 %collective-permute-done.30 = bf16[1024,512]{1,0:T(8,128)(2,1)} collective-permute-done((bf16[1024,512]{1,0:T(8,128)(2,1)}, bf16[1024,512]{1,0:T(8,128)(2,1)}, u32[]{:S(2)}, u32[]{:S(2)}) %collective-permute-start.30) | collective-permute-done | bytes 1048608 | tf_op jit(solution)/shard_map/ppermute | solution.py:634
  334.0 19.8 %collective-permute-done.31 = bf16[1024,512]{1,0:T(8,128)(2,1)S(1)} collective-permute-done((bf16[1024,512]{1,0:T(8,128)(2,1)}, bf16[1024,512]{1,0:T(8,128)(2,1)S(1)}, u32[]{:S(2)}, u32[]{:S(2)}) %collective-permute-start.31) | collective-permute-done | bytes 1048608 | tf_op jit(solution)/shard_map/ppermute | solution.py:635
  362.5 4.3 %collective-permute-start.39 = (bf16[1024,512]{1,0:T(8,128)(2,1)}, bf16[1024,512]{1,0:T(8,128)(2,1)}, u32[]{:S(2)}, u32[]{:S(2)}) collective-permute-start(bf16[1024,512]{1,0:T(8,128)(2,1)} %add_convert_fusion), channel_id=1, source_target_pairs={{2,0},{3,1},{4,2},{5,3},{6,4},{7,5},{10,8},{11,9},{12,10},{13,11},... | collective-permute-start | bytes 3145736 | tf_op jit(solution)/shard_map/ppermute | solution.py:635
  366.8 5.2 %collective-permute-done.44.refs_2_ = bf16[4,4,64,256]{3,2,1,0:T(8,128)(2,1)S(1)} collective-permute-done((bf16[4,4,64,256]{3,2,1,0:T(8,128)(2,1)S(1)}, bf16[4,4,64,256]{3,2,1,0:T(8,128)(2,1)S(1)}, u32[]{:S(2)}, u32[]{:S(2)}) %collective-permute-start.44) | collective-permute-done | bytes 524320 | tf_op jit(solution)/shard_map/ppermute | solution.py:452
  374.8 8.6 %collective-permute-done.41.refs_2_ = bf16[4,4,64,256]{3,2,1,0:T(8,128)(2,1)} collective-permute-done((bf16[4,4,64,256]{3,2,1,0:T(8,128)(2,1)}, bf16[4,4,64,256]{3,2,1,0:T(8,128)(2,1)}, u32[]{:S(2)}, u32[]{:S(2)}) %collective-permute-start.41) | collective-permute-done | bytes 524320 | tf_op jit(solution)/shard_map/ppermute | solution.py:452
  384.2 4.3 %finish.5 = f32[16,256,256]{2,1,0:T(8,128)} custom-call(s32[9]{0:T(128)S(1)} %pad_add_fusion.2.tab, bf16[1,16,64,256]{3,2,1,0:T(8,128)(2,1)S(1)} %bitcast.93, bf16[1,16,64,256]{3,2,1,0:T(8,128)(2,1)} %bitcast.46.refs_1_, bf16[1,16,64,256]{3,2,1,0:T(8,128)(2,1)} %bitcast.47.refs_2_, bf16[1,16,64,256]{3,2,1,0:T(8,128)(2,1)S(1)} %bitcast.95), custom_call_target="tpu_custom_call" | custom-call | bytes 6291456 | tf_op jit(solution)/shard_map/finish/pallas_call | solution.py:378
  394.5 5.5 %finish.6 = f32[4,256,1024]{2,1,0:T(8,128)} custom-call(s32[5]{0:T(128)S(1)} %pad_add_fusion.1.tab, bf16[4,4,64,256]{3,2,1,0:T(8,128)(2,1)} %get-tuple-element.174.refs_0_, bf16[4,4,64,256]{3,2,1,0:T(8,128)(2,1)} %collective-permute-done.40.refs_1_, bf16[4,4,64,256]{3,2,1,0:T(8,128)(2,1)} %collective-permute-done.41.refs_2_, ...), custom_call_target="tpu_custom_call" | custom-call | bytes 6291456 | tf_op jit(solution)/shard_map/finish/pallas_call | solution.py:378
  400.0 4.6 %finish.7 = f32[4,1024,256]{2,1,0:T(8,128)} custom-call(s32[5]{0:T(128)S(1)} %pad_add_fusion.1.tab, bf16[4,4,64,256]{3,2,1,0:T(8,128)(2,1)S(1)} %copy-done.22, bf16[4,4,64,256]{3,2,1,0:T(8,128)(2,1)} %collective-permute-done.43.refs_1_, bf16[4,4,64,256]{3,2,1,0:T(8,128)(2,1)S(1)} %copy-done.37, bf16[4,4,64,256]{3,2,1,0:T(8,128)(2,1)} %collective-permute-done.45.refs_3_), custom_call_target="tpu_custom_call" | custom-call | bytes 6291456 | tf_op jit(solution)/shard_map/finish/pallas_call | solution.py:378
  404.6 4.0 close.1
  (284 shorter events, 185.2 us)
Async XLA Ops:
  12.6 28.7 %all-to-all-start = ((bf16[4,2,4,64,256]{4,3,2,1,0:T(8,128)(2,1)}), bf16[4,2,4,64,256]{4,3,2,1,0:T(8,128)(2,1)S(1)}, u32[]{:S(2)}, u32[]{:S(2)}) async-start(bf16[4,2,4,64,256]{4,3,2,1,0:T(8,128)(2,1)} %copy.46), calls=%async_computation | async-start | bytes 2097152 | tf_op jit(solution)/shard_map/all_to_all | solution.py:503
  17.8 390.8 %reduce-scatter.2.cloned.1.call-start = ((), (), s32[]{:S(2)}) async-start(), calls=%async_computation.3 | async-start | bytes 5242880 | tf_op jit(solution)/shard_map/reduce_scatter | solution.py:595
  18.4 44.3 %collective-permute-start.1 = (bf16[1024,512]{1,0:T(8,128)(2,1)S(1)}, bf16[1024,512]{1,0:T(8,128)(2,1)S(1)}, u32[]{:S(2)}, u32[]{:S(2)}) collective-permute-start(bf16[1024,512]{1,0:T(8,128)(2,1)S(1)} %bitcast.88), channel_id=1, source_target_pairs={{2,0},{3,1},{4,2},{5,3},{6,4},{7,5},{10,8},{11,9},{12,10},{13,11},... | collective-permute-start | bytes 3145736 | tf_op jit(solution)/shard_map/ppermute | solution.py:537
  20.9 42.9 %collective-permute-start = (bf16[1024,512]{1,0:T(8,128)(2,1)S(1)}, bf16[1024,512]{1,0:T(8,128)(2,1)}, u32[]{:S(2)}, u32[]{:S(2)}) collective-permute-start(bf16[1024,512]{1,0:T(8,128)(2,1)S(1)} %bitcast.89), channel_id=1, source_target_pairs={{0,2},{1,3},{2,4},{3,5},{4,6},{5,7},{8,10},{9,11},{10,12},{11,13},... | collective-permute-start | bytes 3145736 | tf_op jit(solution)/shard_map/ppermute | solution.py:536
  102.8 34.3 %collective-permute-start.16 = (bf16[1024,512]{1,0:T(8,128)(2,1)}, bf16[1024,512]{1,0:T(8,128)(2,1)}, u32[]{:S(2)}, u32[]{:S(2)}) collective-permute-start(bf16[1024,512]{1,0:T(8,128)(2,1)} %bitcast.20.refs_0_.refs_6_), channel_id=1, source_target_pairs={{0,2},{1,3},{2,4},{3,5},{4,6},{5,7},{8,10},{9,11},{10,12},{11,13},... | collective-permute-start | bytes 3145736 | tf_op jit(solution)/shard_map/ppermute | solution.py:536
  137.1 27.7 %collective-permute-start.19 = (bf16[1024,512]{1,0:T(8,128)(2,1)}, bf16[1024,512]{1,0:T(8,128)(2,1)}, u32[]{:S(2)}, u32[]{:S(2)}) collective-permute-start(bf16[1024,512]{1,0:T(8,128)(2,1)} %collective-permute-done.17.refs_0_.refs_7_), channel_id=1, source_target_pairs={{2,0},{3,1},{4,2},{5,3},{10,8},{11,9},{12,10},{13,11},{18,16},{19,... | collective-permute-start | bytes 3145736 | tf_op jit(solution)/shard_map/ppermute | solution.py:537
  142.9 27.0 %collective-permute-start.18 = (bf16[1024,512]{1,0:T(8,128)(2,1)}, bf16[1024,512]{1,0:T(8,128)(2,1)}, u32[]{:S(2)}, u32[]{:S(2)}) collective-permute-start(bf16[1024,512]{1,0:T(8,128)(2,1)} %collective-permute-done.16.refs_0_.refs_7_), channel_id=1, source_target_pairs={{2,4},{3,5},{4,6},{5,7},{10,12},{11,13},{12,14},{13,15},{18,20},{1... | collective-permute-start | bytes 3145736 | tf_op jit(solution)/shard_map/ppermute | solution.py:536
  160.0 37.8 %collective-permute-start.15 = (bf16[16,128,512]{2,1,0:T(8,128)(2,1)}, bf16[16,128,512]{2,1,0:T(8,128)(2,1)S(1)}, u32[]{:S(2)}, u32[]{:S(2)}) collective-permute-start(bf16[16,128,512]{2,1,0:T(8,128)(2,1)} %get-tuple-element.116), channel_id=1, source_target_pairs={{0,1},{1,0},{2,3},{3,2},{4,5},{5,4},{6,7},{7,6},{8,9},{9,8},{10,11... | collective-permute-start | bytes 6291464 | tf_op jit(solution)/shard_map/ppermute | solution.py:423
  220.1 28.3 %collective-permute-start.33 = (bf16[2,16,64,256]{3,2,1,0:T(8,128)(2,1)}, bf16[2,16,64,256]{3,2,1,0:T(8,128)(2,1)S(1)}, u32[]{:S(2)}, u32[]{:S(2)}) collective-permute-start(bf16[2,16,64,256]{3,2,1,0:T(8,128)(2,1)} %get-tuple-element.162), channel_id=1, source_target_pairs={{0,8},{8,0},{16,24},{24,16},{1,9},{9,1},{17,25},{25,17},{2,10},{10... | collective-permute-start | bytes 3145736 | tf_op jit(solution)/shard_map/ppermute | solution.py:437
  221.7 27.7 %collective-permute-start.34 = (bf16[2,16,64,256]{3,2,1,0:T(8,128)(2,1)}, bf16[2,16,64,256]{3,2,1,0:T(8,128)(2,1)S(1)}, u32[]{:S(2)}, u32[]{:S(2)}) collective-permute-start(bf16[2,16,64,256]{3,2,1,0:T(8,128)(2,1)} %get-tuple-element.164), channel_id=1, source_target_pairs={{0,16},{8,24},{16,0},{24,8},{1,17},{9,25},{17,1},{25,9},{2,18},{10... | collective-permute-start | bytes 3145736 | tf_op jit(solution)/shard_map/ppermute | solution.py:437
  247.1 50.1 %collective-permute-start.29 = (bf16[1024,512]{1,0:T(8,128)(2,1)S(1)}, bf16[1024,512]{1,0:T(8,128)(2,1)S(1)}, u32[]{:S(2)}, u32[]{:S(2)}) collective-permute-start(bf16[1024,512]{1,0:T(8,128)(2,1)S(1)} %get-tuple-element.154), channel_id=1, source_target_pairs={{6,4},{7,5},{14,12},{15,13},{22,20},{23,21},{30,28},{31,29}} | collective-permute-start | bytes 3145736 | tf_op jit(solution)/shard_map/ppermute | solution.py:635
  248.4 49.3 %collective-permute-start.28 = (bf16[1024,512]{1,0:T(8,128)(2,1)S(1)}, bf16[1024,512]{1,0:T(8,128)(2,1)S(1)}, u32[]{:S(2)}, u32[]{:S(2)}) collective-permute-start(bf16[1024,512]{1,0:T(8,128)(2,1)S(1)} %get-tuple-element.152), channel_id=1, source_target_pairs={{0,2},{1,3},{8,10},{9,11},{16,18},{17,19},{24,26},{25,27}} | collective-permute-start | bytes 3145736 | tf_op jit(solution)/shard_map/ppermute | solution.py:634
  271.7 29.2 %collective-permute-start.36 = (bf16[4,4,64,256]{3,2,1,0:T(8,128)(2,1)S(1)}, bf16[4,4,64,256]{3,2,1,0:T(8,128)(2,1)S(1)}, u32[]{:S(2)}, u32[]{:S(2)}) collective-permute-start(bf16[4,4,64,256]{3,2,1,0:T(8,128)(2,1)S(1)} %fusion.8), channel_id=1, source_target_pairs={{0,16},{8,24},{16,0},{24,8},{1,17},{9,25},{17,1},{25,9},{2,18},{10... | collective-permute-start | bytes 1572872 | tf_op jit(solution)/shard_map/ppermute | solution.py:440
  272.2 28.9 %collective-permute-start.37 = (bf16[4,4,64,256]{3,2,1,0:T(8,128)(2,1)S(1)}, bf16[4,4,64,256]{3,2,1,0:T(8,128)(2,1)S(1)}, u32[]{:S(2)}, u32[]{:S(2)}) collective-permute-start(bf16[4,4,64,256]{3,2,1,0:T(8,128)(2,1)S(1)} %fusion.11), channel_id=1, source_target_pairs={{0,8},{8,0},{16,24},{24,16},{1,9},{9,1},{17,25},{25,17},{2,10},{10... | collective-permute-start | bytes 1572872 | tf_op jit(solution)/shard_map/ppermute | solution.py:440
  272.7 39.7 %collective-permute-start.46 = (bf16[16,64,256]{2,1,0:T(8,128)(2,1)S(1)}, bf16[16,64,256]{2,1,0:T(8,128)(2,1)}, u32[]{:S(2)}, u32[]{:S(2)}) collective-permute-start(bf16[16,64,256]{2,1,0:T(8,128)(2,1)S(1)} %fusion.9), channel_id=1, source_target_pairs={{0,16},{8,24},{16,0},{24,8},{1,17},{9,25},{17,1},{25,9},{2,18},{10... | collective-permute-start | bytes 1572872 | tf_op jit(solution)/shard_map/ppermute | solution.py:440
  299.6 28.3 %collective-permute-start.30 = (bf16[1024,512]{1,0:T(8,128)(2,1)}, bf16[1024,512]{1,0:T(8,128)(2,1)}, u32[]{:S(2)}, u32[]{:S(2)}) collective-permute-start(bf16[1024,512]{1,0:T(8,128)(2,1)} %get-tuple-element.155), channel_id=1, source_target_pairs={{0,2},{1,3},{2,4},{3,5},{8,10},{9,11},{10,12},{11,13},{16,18},{17,... | collective-permute-start | bytes 3145736 | tf_op jit(solution)/shard_map/ppermute | solution.py:634
  302.7 52.4 %all-to-all-start.1 = ((bf16[4,2,4,64,256]{4,3,2,1,0:T(8,128)(2,1)}), bf16[4,2,4,64,256]{4,3,2,1,0:T(8,128)(2,1)}, u32[]{:S(2)}, u32[]{:S(2)}) async-start(bf16[4,2,4,64,256]{4,3,2,1,0:T(8,128)(2,1)} %copy.53), calls=%async_computation.2 | async-start | bytes 2097152 | tf_op jit(solution)/shard_map/all_to_all | solution.py:626
  309.9 43.9 %collective-permute-start.31 = (bf16[1024,512]{1,0:T(8,128)(2,1)}, bf16[1024,512]{1,0:T(8,128)(2,1)S(1)}, u32[]{:S(2)}, u32[]{:S(2)}) collective-permute-start(bf16[1024,512]{1,0:T(8,128)(2,1)} %get-tuple-element.156), channel_id=1, source_target_pairs={{4,2},{5,3},{6,4},{7,5},{12,10},{13,11},{14,12},{15,13},{20,18},{2... | collective-permute-start | bytes 3145736 | tf_op jit(solution)/shard_map/ppermute | solution.py:635
  317.8 40.7 %collective-permute-start.47 = (bf16[16,64,256]{2,1,0:T(8,128)(2,1)S(1)}, bf16[16,64,256]{2,1,0:T(8,128)(2,1)}, u32[]{:S(2)}, u32[]{:S(2)}) collective-permute-start(bf16[16,64,256]{2,1,0:T(8,128)(2,1)S(1)} %fusion.5), channel_id=1, source_target_pairs={{0,8},{8,0},{16,24},{24,16},{1,9},{9,1},{17,25},{25,17},{2,10},{10... | collective-permute-start | bytes 1572872 | tf_op jit(solution)/shard_map/ppermute | solution.py:451
  327.8 31.3 %collective-permute-start.52 = (bf16[16,64,256]{2,1,0:T(8,128)(2,1)S(1)}, bf16[16,64,256]{2,1,0:T(8,128)(2,1)}, u32[]{:S(2)}, u32[]{:S(2)}) collective-permute-start(bf16[16,64,256]{2,1,0:T(8,128)(2,1)S(1)} %fusion.4), channel_id=1, source_target_pairs={{0,16},{8,24},{16,0},{24,8},{1,17},{9,25},{17,1},{25,9},{2,18},{10... | collective-permute-start | bytes 1572872 | tf_op jit(solution)/shard_map/ppermute | solution.py:452
  331.8 28.0 %collective-permute-start.49 = (bf16[16,64,256]{2,1,0:T(8,128)(2,1)}, bf16[16,64,256]{2,1,0:T(8,128)(2,1)S(1)}, u32[]{:S(2)}, u32[]{:S(2)}) collective-permute-start(bf16[16,64,256]{2,1,0:T(8,128)(2,1)} %collective-permute-done.48), channel_id=1, source_target_pairs={{0,8},{8,0},{16,24},{24,16},{1,9},{9,1},{17,25},{25,17},{2,10},{10... | collective-permute-start | bytes 1572872 | tf_op jit(solution)/shard_map/ppermute | solution.py:454
  333.5 29.1 %collective-permute-start.53 = (bf16[16,64,256]{2,1,0:T(8,128)(2,1)}, bf16[16,64,256]{2,1,0:T(8,128)(2,1)S(1)}, u32[]{:S(2)}, u32[]{:S(2)}) collective-permute-start(bf16[16,64,256]{2,1,0:T(8,128)(2,1)} %collective-permute-done.51), channel_id=1, source_target_pairs={{0,16},{8,24},{16,0},{24,8},{1,17},{9,25},{17,1},{25,9},{2,18},{10... | collective-permute-start | bytes 1572872 | tf_op jit(solution)/shard_map/ppermute | solution.py:456
  360.6 44.0 %collective-permute-start.38 = (bf16[1024,512]{1,0:T(8,128)(2,1)}, bf16[1024,512]{1,0:T(8,128)(2,1)}, u32[]{:S(2)}, u32[]{:S(2)}) collective-permute-start(bf16[1024,512]{1,0:T(8,128)(2,1)} %add_convert_fusion.1), channel_id=1, source_target_pairs={{0,2},{1,3},{2,4},{3,5},{4,6},{5,7},{8,10},{9,11},{10,12},{11,13},... | collective-permute-start | bytes 3145736 | tf_op jit(solution)/shard_map/ppermute | solution.py:634
  362.5 42.1 %collective-permute-start.39 = (bf16[1024,512]{1,0:T(8,128)(2,1)}, bf16[1024,512]{1,0:T(8,128)(2,1)}, u32[]{:S(2)}, u32[]{:S(2)}) collective-permute-start(bf16[1024,512]{1,0:T(8,128)(2,1)} %add_convert_fusion), channel_id=1, source_target_pairs={{2,0},{3,1},{4,2},{5,3},{6,4},{7,5},{10,8},{11,9},{12,10},{13,11},... | collective-permute-start | bytes 3145736 | tf_op jit(solution)/shard_map/ppermute | solution.py:635
  (96 other events, 1066.5 us)
Sparse Core Ops, SparseCore 0:
  205.6 100.4 reduce-scatter.1

commit v6 on v5

--- a/solution.py
+++ b/solution.py
@@ -10,7 +10,7 @@
 
 F32 = jnp.float32
 BF16 = jnp.bfloat16
-MIDDLE_MIB = 60
+MIDDLE_MIB = 40
 
 
 def params(mib, dims=1):

time: 422 us -> 421 us (level)
  local copies, waits for them, and re-layouts: 49 us -> 39.1 us
  waiting for transfers between devices: 155 us -> 164 us
  Pallas kernels: 93.4 us -> 86 us
  starting transfers between devices: 87.4 us -> 94.1 us
    unnamed x132 -> x118, local copies, waits for them, and re-layouts: 35.1 us -> 25.4 us
    ppermute x6, waiting for transfers between devices: 23.4 us -> 29.9 us  [hop(): up = lax.ppermute(ups[-1], 'tensor', up_pairs(r - 1, nl - 1))]
    pallas_call x2, Pallas kernels: 28.4 us -> 22.3 us  [middle(): pl.pallas_call(body, grid_spec=pltpu.PrefetchScalarGridSpec(num_scalar_pr...]
    ppermute x6, waiting for transfers between devices: 12.8 us -> 18.8 us  [hop(): down = lax.ppermute(downs[-1], 'tensor', down_pairs(0, nl - r))]
    all_to_all x1, starting transfers between devices: 7.19 us -> 12.9 us  [body(): lax.all_to_all(g14, 'tensor', split_axis=0, concat_axis=0, axis_index_gro...]
    ppermute x4, waiting for transfers between devices: 21.8 us -> 27 us  [reduce_dp(): came = [lax.ppermute(g[1], 'dp', p[0]) for g, p in zip(grads, orders)]]
    ppermute x3, waiting for transfers between devices: 42.7 us -> 38.2 us  [body(): down = lax.ppermute(down, 'tensor', down_pairs(nl - 1 - r, nl - 1))]
  transfers between devices with their start and end apart: 57 -> 57, of which waited for: 23 -> 26; matrix products, arithmetic and copies ran while one was open for 8% -> 8% of each run, Pallas kernels for 22% -> 21%
where the time goes in v6:
time: 421 us; the launch traced here: 417 us
  waiting for transfers between devices  164 us (39%)
  starting transfers between devices  94.1 us (22%)
  Pallas kernels  86 us (20%)
  local copies, waits for them, and re-layouts  39.1 us (9%)
  other arithmetic  18 us (4%)
  between operations  15 us (4%)
    ppermute x3, waiting for transfers between devices, body(): down = lax.ppermute(down, 'tensor', down_pairs(nl - 1 - r, nl - 1))  38.2 us
    ppermute x6, waiting for transfers between devices, hop(): up = lax.ppermute(ups[-1], 'tensor', up_pairs(r - 1, nl - 1))  29.9 us
    ppermute x4, waiting for transfers between devices, reduce_dp(): came = [lax.ppermute(g[1], 'dp', p[0]) for g, p in zip(grads, orders)]  27 us
    unnamed x118, local copies, waits for them, and re-layouts  25.4 us
    pallas_call x10, Pallas kernels, expand(): pl.pallas_call(functools.partial(expand_kernel, side=side, pa=pa, bw=bw,...  23.4 us
    pallas_call x2, Pallas kernels, middle(): pl.pallas_call(body, grid_spec=pltpu.PrefetchScalarGridSpec(num_scalar_pr...  22.3 us
    ppermute x6, starting transfers between devices, hop(): down = lax.ppermute(downs[-1], 'tensor', down_pairs(0, nl - r))  19.6 us
    ppermute x6, waiting for transfers between devices, hop(): down = lax.ppermute(downs[-1], 'tensor', down_pairs(0, nl - r))  18.8 us
  transfers between devices with their start and end apart: 57, of which 26 were waited for; matrix products, arithmetic and copies ran while one was open for 8% of the time, Pallas kernels for 21%

profile of v6, /device:TPU:16, one launch (start us, length us, event | category | flops | bytes accessed | tf_op | source)
XLA Modules:
  0.0 416.7 jit_solution(7524537627899327570)
XLA Ops:
  12.6 5.2 %all-to-all-start = ((bf16[4,2,4,64,256]{4,3,2,1,0:T(8,128)(2,1)}), bf16[4,2,4,64,256]{4,3,2,1,0:T(8,128)(2,1)S(1)}, u32[]{:S(2)}, u32[]{:S(2)}) async-start(bf16[4,2,4,64,256]{4,3,2,1,0:T(8,128)(2,1)} %copy.46), calls=%async_computation | async-start | bytes 2097152 | tf_op jit(solution)/shard_map/all_to_all | solution.py:503
  24.3 17.1 %all-to-all-done.refs_0_ = bf16[4,2,4,64,256]{4,3,2,1,0:T(8,128)(2,1)S(1)} async-done(((bf16[4,2,4,64,256]{4,3,2,1,0:T(8,128)(2,1)}), bf16[4,2,4,64,256]{4,3,2,1,0:T(8,128)(2,1)S(1)}, u32[]{:S(2)}, u32[]{:S(2)}) %all-to-all-start) | async-done | bytes 1048608 | tf_op jit(solution)/shard_map/all_to_all | solution.py:503
  56.6 6.1 %collective-permute-done.1.refs_0_.refs_5_ = bf16[1024,512]{1,0:T(8,128)(2,1)S(1)} collective-permute-done((bf16[1024,512]{1,0:T(8,128)(2,1)S(1)}, bf16[1024,512]{1,0:T(8,128)(2,1)S(1)}, u32[]{:S(2)}, u32[]{:S(2)}) %collective-permute-start.1) | collective-permute-done | bytes 1048608 | tf_op jit(solution)/shard_map/ppermute | solution.py:537
  82.9 6.0 %collective-permute-done.6.refs_3_ = bf16[4,4,64,256]{3,2,1,0:T(8,128)(2,1)S(1)} collective-permute-done((bf16[4,4,64,256]{3,2,1,0:T(8,128)(2,1)}, bf16[4,4,64,256]{3,2,1,0:T(8,128)(2,1)S(1)}, u32[]{:S(2)}, u32[]{:S(2)}) %collective-permute-start.6) | collective-permute-done | bytes 524320 | tf_op jit(solution)/shard_map/ppermute | solution.py:548
  96.9 5.9 %collective-permute-start.17 = (bf16[1024,512]{1,0:T(8,128)(2,1)}, bf16[1024,512]{1,0:T(8,128)(2,1)}, u32[]{:S(2)}, u32[]{:S(2)}) collective-permute-start(bf16[1024,512]{1,0:T(8,128)(2,1)} %bitcast.20.refs_0_.refs_6_), channel_id=1, source_target_pairs={{2,0},{3,1},{4,2},{5,3},{6,4},{7,5},{10,8},{11,9},{12,10},{13,11},... | collective-permute-start | bytes 3145736 | tf_op jit(solution)/shard_map/ppermute | solution.py:537
  122.9 14.2 %collective-permute-done.16.refs_0_.refs_7_ = bf16[1024,512]{1,0:T(8,128)(2,1)} collective-permute-done((bf16[1024,512]{1,0:T(8,128)(2,1)}, bf16[1024,512]{1,0:T(8,128)(2,1)}, u32[]{:S(2)}, u32[]{:S(2)}) %collective-permute-start.16) | collective-permute-done | bytes 1048608 | tf_op jit(solution)/shard_map/ppermute | solution.py:536
  137.2 4.9 %collective-permute-start.19 = (bf16[1024,512]{1,0:T(8,128)(2,1)}, bf16[1024,512]{1,0:T(8,128)(2,1)S(1)}, u32[]{:S(2)}, u32[]{:S(2)}) collective-permute-start(bf16[1024,512]{1,0:T(8,128)(2,1)} %collective-permute-done.17.refs_0_.refs_7_), channel_id=1, source_target_pairs={{2,0},{3,1},{4,2},{5,3},{10,8},{11,9},{12,10},{13,11},{18,16},{19,... | collective-permute-start | bytes 3145736 | tf_op jit(solution)/shard_map/ppermute | solution.py:537
  144.0 10.0 %forward.1 = (bf16[16,128,512]{2,1,0:T(8,128)(2,1)S(1)}, bf16[16,128,512]{2,1,0:T(8,128)(2,1)S(1)}, bf16[16,256,512]{2,1,0:T(8,128)(2,1)}, bf16[16,256,512]{2,1,0:T(8,128)(2,1)}, bf16[16,256,512]{2,1,0:T(8,128)(2,1)}) custom-call(s32[12]{0:T(128)S(1)} %concatenate.27.meta, bf16[16,32,512]{2,1,0:T(8,128)(2,1)S(1)} %get-tuple-element.101.refs_0_, ...), custom_call_target="tpu_custom_call" | custom-call | flops 2147483648 | bytes 25165824 | tf_op jit(solution)/shard_map/forward/pallas_call | solution.py:211
  154.0 10.9 %collective-permute-done.19.refs_0_.refs_7_ = bf16[1024,512]{1,0:T(8,128)(2,1)S(1)} collective-permute-done((bf16[1024,512]{1,0:T(8,128)(2,1)}, bf16[1024,512]{1,0:T(8,128)(2,1)S(1)}, u32[]{:S(2)}, u32[]{:S(2)}) %collective-permute-start.19) | collective-permute-done | bytes 1048608 | tf_op jit(solution)/shard_map/ppermute | solution.py:537
  164.9 4.1 collective-permute-done.18.refs_1_.refs_8_
  185.1 8.5 %collective-permute-done.20.refs_0_.refs_8_ = bf16[1024,512]{1,0:T(8,128)(2,1)S(1)} collective-permute-done((bf16[1024,512]{1,0:T(8,128)(2,1)S(1)}, bf16[1024,512]{1,0:T(8,128)(2,1)S(1)}, u32[]{:S(2)}, u32[]{:S(2)}) %collective-permute-start.20) | collective-permute-done | bytes 1048608 | tf_op jit(solution)/shard_map/ppermute | solution.py:536
  209.2 12.4 %backward.1 = (bf16[16,128,512]{2,1,0:T(8,128)(2,1)S(1)}, bf16[16,128,512]{2,1,0:T(8,128)(2,1)S(1)}, bf16[2,16,64,256]{3,2,1,0:T(8,128)(2,1)S(1)}, bf16[2,16,64,...) custom-call(s32[12]{0:T(128)S(1)} %concatenate.27.meta, ...), custom_call_target="tpu_custom_call" | custom-call | flops 4294967296 | bytes 29360128 | tf_op jit(solution)/shard_map/backward/pallas_call | solution.py:211
  242.7 5.0 %collective-permute-done.33 = bf16[2,16,64,256]{3,2,1,0:T(8,128)(2,1)S(1)} collective-permute-done((bf16[2,16,64,256]{3,2,1,0:T(8,128)(2,1)S(1)}, bf16[2,16,64,256]{3,2,1,0:T(8,128)(2,1)S(1)}, u32[]{:S(2)}, u32[]{:S(2)}) %collective-permute-start.33) | collective-permute-done | bytes 1048608 | tf_op jit(solution)/shard_map/ppermute | solution.py:437
  249.4 20.3 %collective-permute-done.32 = bf16[2,4,4,64,256]{4,3,2,1,0:T(8,128)(2,1)S(1)} collective-permute-done((bf16[2,4,4,64,256]{4,3,2,1,0:T(8,128)(2,1)S(1)}, bf16[2,4,4,64,256]{4,3,2,1,0:T(8,128)(2,1)S(1)}, u32[]{:S(2)}, u32[]{:S(2)}) %collective-permute-start.32) | collective-permute-done | bytes 1048608 | tf_op jit(solution)/shard_map/ppermute | solution.py:437
  273.7 17.9 %collective-permute-done.29 = bf16[1024,512]{1,0:T(8,128)(2,1)S(1)} collective-permute-done((bf16[1024,512]{1,0:T(8,128)(2,1)S(1)}, bf16[1024,512]{1,0:T(8,128)(2,1)S(1)}, u32[]{:S(2)}, u32[]{:S(2)}) %collective-permute-start.29) | collective-permute-done | bytes 1048608 | tf_op jit(solution)/shard_map/ppermute | solution.py:635
  297.0 12.9 %all-to-all-start.1 = ((bf16[4,2,4,64,256]{4,3,2,1,0:T(8,128)(2,1)}), bf16[4,2,4,64,256]{4,3,2,1,0:T(8,128)(2,1)}, u32[]{:S(2)}, u32[]{:S(2)}) async-start(bf16[4,2,4,64,256]{4,3,2,1,0:T(8,128)(2,1)} %copy.53), calls=%async_computation.2 | async-start | bytes 2097152 | tf_op jit(solution)/shard_map/all_to_all | solution.py:626
  318.2 7.5 %collective-permute-done.30 = bf16[1024,512]{1,0:T(8,128)(2,1)} collective-permute-done((bf16[1024,512]{1,0:T(8,128)(2,1)}, bf16[1024,512]{1,0:T(8,128)(2,1)}, u32[]{:S(2)}, u32[]{:S(2)}) %collective-permute-start.30) | collective-permute-done | bytes 1048608 | tf_op jit(solution)/shard_map/ppermute | solution.py:634
  332.5 20.3 %collective-permute-done.31 = bf16[1024,512]{1,0:T(8,128)(2,1)S(1)} collective-permute-done((bf16[1024,512]{1,0:T(8,128)(2,1)}, bf16[1024,512]{1,0:T(8,128)(2,1)S(1)}, u32[]{:S(2)}, u32[]{:S(2)}) %collective-permute-start.31) | collective-permute-done | bytes 1048608 | tf_op jit(solution)/shard_map/ppermute | solution.py:635
  362.5 4.3 %collective-permute-start.39 = (bf16[1024,512]{1,0:T(8,128)(2,1)}, bf16[1024,512]{1,0:T(8,128)(2,1)}, u32[]{:S(2)}, u32[]{:S(2)}) collective-permute-start(bf16[1024,512]{1,0:T(8,128)(2,1)} %add_convert_fusion), channel_id=1, source_target_pairs={{2,0},{3,1},{4,2},{5,3},{6,4},{7,5},{10,8},{11,9},{12,10},{13,11},... | collective-permute-start | bytes 3145736 | tf_op jit(solution)/shard_map/ppermute | solution.py:635
  366.8 4.3 %collective-permute-done.44.refs_2_ = bf16[4,4,64,256]{3,2,1,0:T(8,128)(2,1)S(1)} collective-permute-done((bf16[4,4,64,256]{3,2,1,0:T(8,128)(2,1)S(1)}, bf16[4,4,64,256]{3,2,1,0:T(8,128)(2,1)S(1)}, u32[]{:S(2)}, u32[]{:S(2)}) %collective-permute-start.44) | collective-permute-done | bytes 524320 | tf_op jit(solution)/shard_map/ppermute | solution.py:452
  374.1 8.3 %collective-permute-done.41.refs_2_ = bf16[4,4,64,256]{3,2,1,0:T(8,128)(2,1)} collective-permute-done((bf16[4,4,64,256]{3,2,1,0:T(8,128)(2,1)}, bf16[4,4,64,256]{3,2,1,0:T(8,128)(2,1)}, u32[]{:S(2)}, u32[]{:S(2)}) %collective-permute-start.41) | collective-permute-done | bytes 524320 | tf_op jit(solution)/shard_map/ppermute | solution.py:452
  384.1 4.3 %finish.5 = f32[16,256,256]{2,1,0:T(8,128)} custom-call(s32[9]{0:T(128)S(1)} %pad_add_fusion.2.tab, bf16[1,16,64,256]{3,2,1,0:T(8,128)(2,1)S(1)} %bitcast.97, bf16[1,16,64,256]{3,2,1,0:T(8,128)(2,1)} %bitcast.46.refs_1_, bf16[1,16,64,256]{3,2,1,0:T(8,128)(2,1)} %bitcast.47.refs_2_, bf16[1,16,64,256]{3,2,1,0:T(8,128)(2,1)S(1)} %bitcast.99), custom_call_target="tpu_custom_call" | custom-call | bytes 6291456 | tf_op jit(solution)/shard_map/finish/pallas_call | solution.py:378
  393.5 5.5 %finish.6 = f32[4,256,1024]{2,1,0:T(8,128)} custom-call(s32[5]{0:T(128)S(1)} %pad_add_fusion.1.tab, bf16[4,4,64,256]{3,2,1,0:T(8,128)(2,1)} %get-tuple-element.174.refs_0_, bf16[4,4,64,256]{3,2,1,0:T(8,128)(2,1)} %collective-permute-done.40.refs_1_, bf16[4,4,64,256]{3,2,1,0:T(8,128)(2,1)} %collective-permute-done.41.refs_2_, ...), custom_call_target="tpu_custom_call" | custom-call | bytes 6291456 | tf_op jit(solution)/shard_map/finish/pallas_call | solution.py:378
  399.0 4.6 %finish.7 = f32[4,1024,256]{2,1,0:T(8,128)} custom-call(s32[5]{0:T(128)S(1)} %pad_add_fusion.1.tab, bf16[4,4,64,256]{3,2,1,0:T(8,128)(2,1)S(1)} %copy-done.23, bf16[4,4,64,256]{3,2,1,0:T(8,128)(2,1)} %collective-permute-done.43.refs_1_, bf16[4,4,64,256]{3,2,1,0:T(8,128)(2,1)S(1)} %copy-done.42, bf16[4,4,64,256]{3,2,1,0:T(8,128)(2,1)} %collective-permute-done.45.refs_3_), custom_call_target="tpu_custom_call" | custom-call | bytes 6291456 | tf_op jit(solution)/shard_map/finish/pallas_call | solution.py:378
  (270 shorter events, 181.4 us)
Async XLA Ops:
  12.6 28.7 %all-to-all-start = ((bf16[4,2,4,64,256]{4,3,2,1,0:T(8,128)(2,1)}), bf16[4,2,4,64,256]{4,3,2,1,0:T(8,128)(2,1)S(1)}, u32[]{:S(2)}, u32[]{:S(2)}) async-start(bf16[4,2,4,64,256]{4,3,2,1,0:T(8,128)(2,1)} %copy.46), calls=%async_computation | async-start | bytes 2097152 | tf_op jit(solution)/shard_map/all_to_all | solution.py:503
  17.8 389.8 %reduce-scatter.2.cloned.1.call-start = ((), (), s32[]{:S(2)}) async-start(), calls=%async_computation.3 | async-start | bytes 5242880 | tf_op jit(solution)/shard_map/reduce_scatter | solution.py:595
  18.4 44.3 %collective-permute-start.1 = (bf16[1024,512]{1,0:T(8,128)(2,1)S(1)}, bf16[1024,512]{1,0:T(8,128)(2,1)S(1)}, u32[]{:S(2)}, u32[]{:S(2)}) collective-permute-start(bf16[1024,512]{1,0:T(8,128)(2,1)S(1)} %bitcast.92), channel_id=1, source_target_pairs={{2,0},{3,1},{4,2},{5,3},{6,4},{7,5},{10,8},{11,9},{12,10},{13,11},... | collective-permute-start | bytes 3145736 | tf_op jit(solution)/shard_map/ppermute | solution.py:537
  20.9 42.9 %collective-permute-start = (bf16[1024,512]{1,0:T(8,128)(2,1)S(1)}, bf16[1024,512]{1,0:T(8,128)(2,1)}, u32[]{:S(2)}, u32[]{:S(2)}) collective-permute-start(bf16[1024,512]{1,0:T(8,128)(2,1)S(1)} %bitcast.93), channel_id=1, source_target_pairs={{0,2},{1,3},{2,4},{3,5},{4,6},{5,7},{8,10},{9,11},{10,12},{11,13},... | collective-permute-start | bytes 3145736 | tf_op jit(solution)/shard_map/ppermute | solution.py:536
  102.9 34.3 %collective-permute-start.16 = (bf16[1024,512]{1,0:T(8,128)(2,1)}, bf16[1024,512]{1,0:T(8,128)(2,1)}, u32[]{:S(2)}, u32[]{:S(2)}) collective-permute-start(bf16[1024,512]{1,0:T(8,128)(2,1)} %bitcast.20.refs_0_.refs_6_), channel_id=1, source_target_pairs={{0,2},{1,3},{2,4},{3,5},{4,6},{5,7},{8,10},{9,11},{10,12},{11,13},... | collective-permute-start | bytes 3145736 | tf_op jit(solution)/shard_map/ppermute | solution.py:536
  137.2 27.7 %collective-permute-start.19 = (bf16[1024,512]{1,0:T(8,128)(2,1)}, bf16[1024,512]{1,0:T(8,128)(2,1)S(1)}, u32[]{:S(2)}, u32[]{:S(2)}) collective-permute-start(bf16[1024,512]{1,0:T(8,128)(2,1)} %collective-permute-done.17.refs_0_.refs_7_), channel_id=1, source_target_pairs={{2,0},{3,1},{4,2},{5,3},{10,8},{11,9},{12,10},{13,11},{18,16},{19,... | collective-permute-start | bytes 3145736 | tf_op jit(solution)/shard_map/ppermute | solution.py:537
  142.0 27.0 %collective-permute-start.18 = (bf16[1024,512]{1,0:T(8,128)(2,1)}, bf16[1024,512]{1,0:T(8,128)(2,1)S(1)}, u32[]{:S(2)}, u32[]{:S(2)}) collective-permute-start(bf16[1024,512]{1,0:T(8,128)(2,1)} %collective-permute-done.16.refs_0_.refs_7_), channel_id=1, source_target_pairs={{2,4},{3,5},{4,6},{5,7},{10,12},{11,13},{12,14},{13,15},{18,20},{1... | collective-permute-start | bytes 3145736 | tf_op jit(solution)/shard_map/ppermute | solution.py:536
  154.0 42.4 %collective-permute-start.15 = (bf16[16,128,512]{2,1,0:T(8,128)(2,1)S(1)}, bf16[16,128,512]{2,1,0:T(8,128)(2,1)S(1)}, u32[]{:S(2)}, u32[]{:S(2)}) collective-permute-start(bf16[16,128,512]{2,1,0:T(8,128)(2,1)S(1)} %get-tuple-element.116), channel_id=1, source_target_pairs={{0,1},{1,0},{2,3},{3,2},{4,5},{5,4},{6,7},{7,6},{8,9},{9,8},{10,11... | collective-permute-start | bytes 6291464 | tf_op jit(solution)/shard_map/ppermute | solution.py:423
  175.8 28.1 %collective-permute-start.22 = (bf16[16,32,512]{2,1,0:T(8,128)(2,1)}, bf16[16,32,512]{2,1,0:T(8,128)(2,1)}, u32[]{:S(2)}, u32[]{:S(2)}) collective-permute-start(bf16[16,32,512]{2,1,0:T(8,128)(2,1)} %get-tuple-element.129), channel_id=1, source_target_pairs={{0,1},{1,0},{2,3},{3,2},{4,5},{5,4},{6,7},{7,6},{8,9},{9,8},{10,11... | collective-permute-start | bytes 1572872 | tf_op jit(solution)/shard_map/ppermute | solution.py:423
  221.6 26.0 %collective-permute-start.33 = (bf16[2,16,64,256]{3,2,1,0:T(8,128)(2,1)S(1)}, bf16[2,16,64,256]{3,2,1,0:T(8,128)(2,1)S(1)}, u32[]{:S(2)}, u32[]{:S(2)}) collective-permute-start(bf16[2,16,64,256]{3,2,1,0:T(8,128)(2,1)S(1)} %get-tuple-element.162), channel_id=1, source_target_pairs={{0,8},{8,0},{16,24},{24,16},{1,9},{9,1},{17,25},{25,17},{2,10},{10... | collective-permute-start | bytes 3145736 | tf_op jit(solution)/shard_map/ppermute | solution.py:437
  239.3 30.3 %collective-permute-start.32 = (bf16[2,4,4,64,256]{4,3,2,1,0:T(8,128)(2,1)S(1)}, bf16[2,4,4,64,256]{4,3,2,1,0:T(8,128)(2,1)S(1)}, u32[]{:S(2)}, u32[]{:S(2)}) collective-permute-start(bf16[2,4,4,64,256]{4,3,2,1,0:T(8,128)(2,1)S(1)} %get-tuple-element.160), channel_id=1, source_target_pairs={{0,8},{8,0},{16,24},{24,16},{1,9},{9,1},{17,25},{25,17},{2,10},{10... | collective-permute-start | bytes 3145736 | tf_op jit(solution)/shard_map/ppermute | solution.py:437
  240.9 30.0 %collective-permute-start.35 = (bf16[2,4,4,64,256]{4,3,2,1,0:T(8,128)(2,1)S(1)}, bf16[2,4,4,64,256]{4,3,2,1,0:T(8,128)(2,1)S(1)}, u32[]{:S(2)}, u32[]{:S(2)}) collective-permute-start(bf16[2,4,4,64,256]{4,3,2,1,0:T(8,128)(2,1)S(1)} %get-tuple-element.166), channel_id=1, source_target_pairs={{0,16},{8,24},{16,0},{24,8},{1,17},{9,25},{17,1},{25,9},{2,18},{10... | collective-permute-start | bytes 3145736 | tf_op jit(solution)/shard_map/ppermute | solution.py:437
  241.4 50.1 %collective-permute-start.29 = (bf16[1024,512]{1,0:T(8,128)(2,1)S(1)}, bf16[1024,512]{1,0:T(8,128)(2,1)S(1)}, u32[]{:S(2)}, u32[]{:S(2)}) collective-permute-start(bf16[1024,512]{1,0:T(8,128)(2,1)S(1)} %get-tuple-element.154), channel_id=1, source_target_pairs={{6,4},{7,5},{14,12},{15,13},{22,20},{23,21},{30,28},{31,29}} | collective-permute-start | bytes 3145736 | tf_op jit(solution)/shard_map/ppermute | solution.py:635
  247.7 44.4 %collective-permute-start.28 = (bf16[1024,512]{1,0:T(8,128)(2,1)S(1)}, bf16[1024,512]{1,0:T(8,128)(2,1)S(1)}, u32[]{:S(2)}, u32[]{:S(2)}) collective-permute-start(bf16[1024,512]{1,0:T(8,128)(2,1)S(1)} %get-tuple-element.152), channel_id=1, source_target_pairs={{0,2},{1,3},{8,10},{9,11},{16,18},{17,19},{24,26},{25,27}} | collective-permute-start | bytes 3145736 | tf_op jit(solution)/shard_map/ppermute | solution.py:634
  272.1 40.3 %collective-permute-start.46 = (bf16[16,64,256]{2,1,0:T(8,128)(2,1)S(1)}, bf16[16,64,256]{2,1,0:T(8,128)(2,1)}, u32[]{:S(2)}, u32[]{:S(2)}) collective-permute-start(bf16[16,64,256]{2,1,0:T(8,128)(2,1)S(1)} %fusion.9), channel_id=1, source_target_pairs={{0,16},{8,24},{16,0},{24,8},{1,17},{9,25},{17,1},{25,9},{2,18},{10... | collective-permute-start | bytes 1572872 | tf_op jit(solution)/shard_map/ppermute | solution.py:440
  294.0 31.8 %collective-permute-start.30 = (bf16[1024,512]{1,0:T(8,128)(2,1)}, bf16[1024,512]{1,0:T(8,128)(2,1)}, u32[]{:S(2)}, u32[]{:S(2)}) collective-permute-start(bf16[1024,512]{1,0:T(8,128)(2,1)} %get-tuple-element.155), channel_id=1, source_target_pairs={{0,2},{1,3},{2,4},{3,5},{8,10},{9,11},{10,12},{11,13},{16,18},{17,... | collective-permute-start | bytes 3145736 | tf_op jit(solution)/shard_map/ppermute | solution.py:634
  297.0 57.1 %all-to-all-start.1 = ((bf16[4,2,4,64,256]{4,3,2,1,0:T(8,128)(2,1)}), bf16[4,2,4,64,256]{4,3,2,1,0:T(8,128)(2,1)}, u32[]{:S(2)}, u32[]{:S(2)}) async-start(bf16[4,2,4,64,256]{4,3,2,1,0:T(8,128)(2,1)} %copy.53), calls=%async_computation.2 | async-start | bytes 2097152 | tf_op jit(solution)/shard_map/all_to_all | solution.py:626
  309.8 43.0 %collective-permute-start.31 = (bf16[1024,512]{1,0:T(8,128)(2,1)}, bf16[1024,512]{1,0:T(8,128)(2,1)S(1)}, u32[]{:S(2)}, u32[]{:S(2)}) collective-permute-start(bf16[1024,512]{1,0:T(8,128)(2,1)} %get-tuple-element.156), channel_id=1, source_target_pairs={{4,2},{5,3},{6,4},{7,5},{12,10},{13,11},{14,12},{15,13},{20,18},{2... | collective-permute-start | bytes 3145736 | tf_op jit(solution)/shard_map/ppermute | solution.py:635
  317.7 39.3 %collective-permute-start.47 = (bf16[16,64,256]{2,1,0:T(8,128)(2,1)S(1)}, bf16[16,64,256]{2,1,0:T(8,128)(2,1)}, u32[]{:S(2)}, u32[]{:S(2)}) collective-permute-start(bf16[16,64,256]{2,1,0:T(8,128)(2,1)S(1)} %fusion.5), channel_id=1, source_target_pairs={{0,8},{8,0},{16,24},{24,16},{1,9},{9,1},{17,25},{25,17},{2,10},{10... | collective-permute-start | bytes 1572872 | tf_op jit(solution)/shard_map/ppermute | solution.py:451
  325.7 32.7 %collective-permute-start.52 = (bf16[16,64,256]{2,1,0:T(8,128)(2,1)S(1)}, bf16[16,64,256]{2,1,0:T(8,128)(2,1)}, u32[]{:S(2)}, u32[]{:S(2)}) collective-permute-start(bf16[16,64,256]{2,1,0:T(8,128)(2,1)S(1)} %fusion.4), channel_id=1, source_target_pairs={{0,16},{8,24},{16,0},{24,8},{1,17},{9,25},{17,1},{25,9},{2,18},{10... | collective-permute-start | bytes 1572872 | tf_op jit(solution)/shard_map/ppermute | solution.py:452
  329.4 30.3 %collective-permute-start.49 = (bf16[16,64,256]{2,1,0:T(8,128)(2,1)}, bf16[16,64,256]{2,1,0:T(8,128)(2,1)S(1)}, u32[]{:S(2)}, u32[]{:S(2)}) collective-permute-start(bf16[16,64,256]{2,1,0:T(8,128)(2,1)} %collective-permute-done.48), channel_id=1, source_target_pairs={{0,8},{8,0},{16,24},{24,16},{1,9},{9,1},{17,25},{25,17},{2,10},{10... | collective-permute-start | bytes 1572872 | tf_op jit(solution)/shard_map/ppermute | solution.py:454
  331.2 31.3 %collective-permute-start.53 = (bf16[16,64,256]{2,1,0:T(8,128)(2,1)}, bf16[16,64,256]{2,1,0:T(8,128)(2,1)S(1)}, u32[]{:S(2)}, u32[]{:S(2)}) collective-permute-start(bf16[16,64,256]{2,1,0:T(8,128)(2,1)} %collective-permute-done.51), channel_id=1, source_target_pairs={{0,16},{8,24},{16,0},{24,8},{1,17},{9,25},{17,1},{25,9},{2,18},{10... | collective-permute-start | bytes 1572872 | tf_op jit(solution)/shard_map/ppermute | solution.py:456
  360.6 43.0 %collective-permute-start.38 = (bf16[1024,512]{1,0:T(8,128)(2,1)}, bf16[1024,512]{1,0:T(8,128)(2,1)}, u32[]{:S(2)}, u32[]{:S(2)}) collective-permute-start(bf16[1024,512]{1,0:T(8,128)(2,1)} %add_convert_fusion.1), channel_id=1, source_target_pairs={{0,2},{1,3},{2,4},{3,5},{4,6},{5,7},{8,10},{9,11},{10,12},{11,13},... | collective-permute-start | bytes 3145736 | tf_op jit(solution)/shard_map/ppermute | solution.py:634
  362.5 41.1 %collective-permute-start.39 = (bf16[1024,512]{1,0:T(8,128)(2,1)}, bf16[1024,512]{1,0:T(8,128)(2,1)}, u32[]{:S(2)}, u32[]{:S(2)}) collective-permute-start(bf16[1024,512]{1,0:T(8,128)(2,1)} %add_convert_fusion), channel_id=1, source_target_pairs={{2,0},{3,1},{4,2},{5,3},{6,4},{7,5},{10,8},{11,9},{12,10},{13,11},... | collective-permute-start | bytes 3145736 | tf_op jit(solution)/shard_map/ppermute | solution.py:635
  (89 other events, 1265.2 us)
Sparse Core Ops, SparseCore 0:
  204.0 100.5 reduce-scatter.1
